TPU v7x, 32 devices: a whole 2x2x4 slice. The times are simulated.
32 devices in a mesh: dp: 8 (over y, x, core), tensor: 4 (over z).
Axes of the slice: x: 2, y: 2, z: 4, core: 2. Of those that a mesh axis runs over, the one named last changes fastest.
Arguments:
- inputs: bfloat16 [16, 1024, 1024], P('dp', 'tensor'), may hold values from -6 to 6
- lengths: int32 [16], P('dp'), may hold values from 256 to 1024, as said below
- w_query: bfloat16 [1024, 1024], P('dp', 'tensor'), may hold values from -0.1875 to 0.1875
- w_key: bfloat16 [1024, 1024], P('dp', 'tensor'), may hold values from -0.1875 to 0.1875
- w_value: bfloat16 [1024, 1024], P('dp', 'tensor'), may hold values from -0.1875 to 0.1875
- b_query: bfloat16 [1024], P('tensor'), may hold values from -3 to 3
- b_value: bfloat16 [1024], P('tensor'), may hold values from -0.29882812 to 0.29882812
- w_out: bfloat16 [1024, 1024], P('tensor', 'dp'), may hold values from -1.5 to 1.5
- b_out: bfloat16 [1024], replicated, may hold values from -3 to 3
- gain_one: bfloat16 [1024], replicated, may hold values from 0.099609375 to 1.8984375
- shift_one: bfloat16 [1024], replicated, may hold values from -3 to 3
- w_in: bfloat16 [1024, 4096], P('dp', 'tensor'), may hold values from -0.1875 to 0.1875
- b_in: bfloat16 [4096], P('tensor'), may hold values from -3 to 3
- w_back: bfloat16 [4096, 1024], P('tensor', 'dp'), may hold values from -0.09375 to 0.09375
- b_back: bfloat16 [1024], replicated, may hold values from -3 to 3
- gain_two: bfloat16 [1024], replicated, may hold values from 0.099609375 to 1.8984375
- shift_two: bfloat16 [1024], replicated, may hold values from -3 to 3
- cotangent: bfloat16 [16, 1024, 1024], P('dp', 'tensor'), may hold values from -6 to 6
Outputs:
- layer_out: bfloat16 [16, 1024, 1024], P('dp', 'tensor')
- grad_inputs: float32 [16, 1024, 1024], P('dp', 'tensor')
- grad_w_query: float32 [1024, 1024], P('dp', 'tensor')
- grad_w_key: float32 [1024, 1024], P('dp', 'tensor')
- grad_w_value: float32 [1024, 1024], P('dp', 'tensor')
- grad_b_query: float32 [1024], P('tensor')
- grad_b_value: float32 [1024], P('tensor')
- grad_w_out: float32 [1024, 1024], P('tensor', 'dp')
- grad_b_out: float32 [1024], replicated
- grad_gain_one: float32 [1024], replicated
- grad_shift_one: float32 [1024], replicated
- grad_w_in: float32 [1024, 4096], P('dp', 'tensor')
- grad_b_in: float32 [4096], P('tensor')
- grad_w_back: float32 [4096, 1024], P('tensor', 'dp')
- grad_b_back: float32 [1024], replicated
- grad_gain_two: float32 [1024], replicated
- grad_shift_two: float32 [1024], replicated
Inputs may be any that keep to these rules, and one draw needn't show every extreme that they name: The first lengths[s] slots of sequence s are real tokens; one sequence has 1024 and another 1024 // 4.
All inputs are finite; a program needn't handle non-finite values.
Results may differ from a plain program's by a relative error of at most 0.015.
The roundings to bfloat16 on the way count: a program that leaves them out, or rounds other values in their place, can miss the bound.
Values may be sent and summed in bfloat16 or wider, within the bound.
A program may use at most 192 MiB of HBM per device.

v0:
```python
from functools import partial

import jax
import jax.numpy as jnp
from jax import lax
from jax.sharding import PartitionSpec as P

HD = 64


EPSILON = 1e-05
NEGATIVE = -1e30


def norm_rows(values, norm_gain, norm_shift):
    average = jnp.mean(values, axis=-1, keepdims=True)
    centered = values - average
    variance = jnp.mean(centered * centered, axis=-1, keepdims=True)
    return centered * lax.rsqrt(variance + EPSILON) * norm_gain + norm_shift


def gelu_exact(values):
    return jax.nn.gelu(values, approximate=False)


def contract_rows(left_side, right_side):
    return lax.dot_general(
        left_side, right_side, (((0,), (0,)), ((), ())), preferred_element_type=jnp.float32
    )


def contract_cols(left_side, right_side):
    return lax.dot_general(
        left_side, right_side, (((1,), (1,)), ((), ())), preferred_element_type=jnp.float32
    )


def attend_forward(query_rows, key_rows, value_rows, key_valid):
    scores = jnp.einsum("qhd,khd->hqk", query_rows, key_rows, preferred_element_type=jnp.float32)
    scores = jnp.where(key_valid[None, None, :], scores, NEGATIVE)
    largest = jnp.max(scores, axis=-1, keepdims=True)
    weights = jnp.exp(scores - largest)
    row_total = jnp.sum(weights, axis=-1, keepdims=True)
    chances = (weights / row_total).astype(jnp.bfloat16)
    context = jnp.einsum("hqk,khd->qhd", chances, value_rows, preferred_element_type=jnp.float32)
    return (context, largest[:, :, 0] + jnp.log(row_total[:, :, 0]))


def attend_backward(log_total, grad_context, query_rows, key_rows, value_rows, key_valid):
    scores = jnp.einsum("qhd,khd->hqk", query_rows, key_rows, preferred_element_type=jnp.float32)
    scores = jnp.where(key_valid[None, None, :], scores, NEGATIVE)
    chances = jnp.exp(scores - log_total[:, :, None])
    grad_values = jnp.einsum(
        "hqk,qhd->khd",
        chances.astype(jnp.bfloat16),
        grad_context,
        preferred_element_type=jnp.float32,
    )
    grad_chances = jnp.einsum(
        "qhd,khd->hqk", grad_context, value_rows, preferred_element_type=jnp.float32
    )
    inner = jnp.sum(grad_chances * chances, axis=-1, keepdims=True)
    grad_scores = (chances * (grad_chances - inner)).astype(jnp.bfloat16)
    grad_queries = jnp.einsum(
        "hqk,khd->qhd", grad_scores, key_rows, preferred_element_type=jnp.float32
    )
    grad_keys = jnp.einsum(
        "hqk,qhd->khd", grad_scores, query_rows, preferred_element_type=jnp.float32
    )
    return (grad_queries, grad_keys, grad_values)


def fetch_weights(w_query, w_key, w_value, w_in, w_out, w_back):
    gathered_rows = (
        lax.all_gather(w_query, "dp", axis=0, tiled=True),
        lax.all_gather(w_key, "dp", axis=0, tiled=True),
        lax.all_gather(w_value, "dp", axis=0, tiled=True),
        lax.all_gather(w_in, "dp", axis=0, tiled=True),
    )
    gathered_columns = (
        lax.all_gather(w_out, "dp", axis=1, tiled=True),
        lax.all_gather(w_back, "dp", axis=1, tiled=True),
    )
    joined = jnp.concatenate([gathered_rows[0], gathered_rows[1], gathered_rows[2]], axis=1)
    return (joined, gathered_rows[3], gathered_columns[0], gathered_columns[1])


def on_device(
    inputs,
    lengths,
    w_query,
    w_key,
    w_value,
    b_query,
    b_value,
    w_out,
    b_out,
    gain_one,
    shift_one,
    w_in,
    b_in,
    w_back,
    b_back,
    gain_two,
    shift_two,
    cotangent,
):
    f32 = jnp.float32
    bf16 = jnp.bfloat16
    tensor_size = lax.axis_size("tensor")
    rows_here = inputs.shape[1]
    slots = rows_here * tensor_size
    local_width = w_query.shape[1]
    local_hidden = w_in.shape[1]
    local_heads = local_width // HD
    query_scale = HD ** (-0.5)
    block_rows = min(512, slots)
    row_place = lax.axis_index("tensor") * rows_here + jnp.arange(rows_here)
    query_bias = b_query.astype(f32)
    value_bias = b_value.astype(f32)
    out_bias = b_out.astype(f32)
    in_bias = b_in.astype(f32)
    back_bias = b_back.astype(f32)
    gain_first = gain_one.astype(f32)
    shift_first = shift_one.astype(f32)
    gain_second = gain_two.astype(f32)
    shift_second = shift_two.astype(f32)

    def one_batch(totals_now, batch_item):
        own_rows, length, grad_own = batch_item
        joined, matrix_in, matrix_out, matrix_back = fetch_weights(
            w_query, w_key, w_value, w_in, w_out, w_back
        )
        row_valid = row_place < length
        key_valid = jnp.arange(slots) < length
        full_in = lax.all_gather(own_rows, "tensor", axis=0, tiled=True)
        projected = jnp.dot(full_in, joined, preferred_element_type=f32)
        query_all = ((projected[:, :local_width] + query_bias) * query_scale).astype(bf16)
        key_all = projected[:, local_width : 2 * local_width].astype(bf16)
        value_all = (projected[:, 2 * local_width :] + value_bias).astype(bf16)
        query_heads = query_all.reshape(slots, local_heads, HD)
        key_heads = key_all.reshape(slots, local_heads, HD)
        value_heads = value_all.reshape(slots, local_heads, HD)
        context_blocks = []
        log_blocks = []
        for row_start in range(0, slots, block_rows):
            query_block = query_heads[row_start : row_start + block_rows]
            produced = attend_forward(query_block, key_heads, value_heads, key_valid)
            context_blocks.append(produced[0])
            log_blocks.append(produced[1])
        context_low = (
            jnp.concatenate(context_blocks, axis=0).reshape(slots, local_width).astype(bf16)
        )
        log_total = jnp.concatenate(log_blocks, axis=1)
        attended = lax.psum_scatter(
            jnp.dot(context_low, matrix_out, preferred_element_type=f32),
            "tensor",
            scatter_dimension=0,
            tiled=True,
        )
        first_sum = own_rows.astype(f32) + attended + out_bias
        first_norm, first_back = jax.vjp(norm_rows, first_sum, gain_first, shift_first)
        first_low = first_norm.astype(bf16)
        full_first = lax.all_gather(first_low, "tensor", axis=0, tiled=True)
        pre_act = jnp.dot(full_first, matrix_in, preferred_element_type=f32) + in_bias
        activated, gelu_back = jax.vjp(gelu_exact, pre_act)
        hidden_low = activated.astype(bf16)
        mixed_rows = lax.psum_scatter(
            jnp.dot(hidden_low, matrix_back, preferred_element_type=f32),
            "tensor",
            scatter_dimension=0,
            tiled=True,
        )
        second_sum = first_norm + mixed_rows + back_bias
        second, second_back = jax.vjp(norm_rows, second_sum, gain_second, shift_second)
        layer_rows = jnp.where(row_valid[:, None], second, 0.0).astype(bf16)
        joined, matrix_in, matrix_out, matrix_back = fetch_weights(
            w_query, w_key, w_value, w_in, w_out, w_back
        )
        grad_second = jnp.where(row_valid[:, None], grad_own.astype(f32), 0.0)
        grad_mixed, grad_gain_b, grad_shift_b = second_back(grad_second)
        full_grad_mixed = lax.all_gather(grad_mixed.astype(bf16), "tensor", axis=0, tiled=True)
        grad_activated = contract_cols(full_grad_mixed, matrix_back)
        grad_back_w = contract_rows(hidden_low, full_grad_mixed)
        (grad_pre,) = gelu_back(grad_activated)
        grad_pre_low = grad_pre.astype(bf16)
        grad_in_bias = jnp.sum(grad_pre_low.astype(f32), axis=0)
        grad_in_w = contract_rows(full_first, grad_pre_low)
        grad_first_mix = lax.psum_scatter(
            contract_cols(grad_pre_low, matrix_in), "tensor", scatter_dimension=0, tiled=True
        )
        grad_first = grad_mixed + grad_first_mix
        grad_att, grad_gain_a, grad_shift_a = first_back(grad_first)
        full_grad_att = lax.all_gather(grad_att.astype(bf16), "tensor", axis=0, tiled=True)
        grad_context = contract_cols(full_grad_att, matrix_out).astype(bf16)
        grad_out_w = contract_rows(context_low, full_grad_att)
        grad_context_heads = grad_context.reshape(slots, local_heads, HD)
        query_grad_blocks = []
        key_grad_sum = jnp.zeros((slots, local_heads, HD), f32)
        value_grad_sum = jnp.zeros((slots, local_heads, HD), f32)
        for row_start in range(0, slots, block_rows):
            query_block = query_heads[row_start : row_start + block_rows]
            block_fn = partial(
                attend_backward,
                log_total[:, row_start : row_start + block_rows],
                grad_context_heads[row_start : row_start + block_rows],
            )
            produced = block_fn(query_block, key_heads, value_heads, key_valid)
            query_grad_blocks.append(produced[0])
            key_grad_sum = key_grad_sum + produced[1]
            value_grad_sum = value_grad_sum + produced[2]
        grad_query_low = (
            jnp.concatenate(query_grad_blocks, axis=0).reshape(slots, local_width).astype(bf16)
        )
        grad_key_low = key_grad_sum.reshape(slots, local_width).astype(bf16)
        grad_value_low = value_grad_sum.reshape(slots, local_width).astype(bf16)
        grad_projected = jnp.concatenate(
            [grad_query_low * query_scale, grad_key_low, grad_value_low], axis=1
        )
        grad_joined_w = contract_rows(full_in, grad_projected)
        grad_query_bias = jnp.sum(grad_projected[:, :local_width].astype(f32), axis=0)
        grad_value_bias = jnp.sum(grad_value_low.astype(f32), axis=0)
        grad_input_mix = lax.psum_scatter(
            contract_cols(grad_projected, joined).astype(jnp.bfloat16),
            "tensor",
            scatter_dimension=0,
            tiled=True,
        ).astype(jnp.float32)
        grad_rows = grad_att + grad_input_mix
        increments = (
            grad_joined_w,
            grad_out_w,
            grad_in_w,
            grad_back_w,
            grad_query_bias,
            grad_value_bias,
            grad_in_bias,
            jnp.sum(grad_att, axis=0),
            grad_gain_a,
            grad_shift_a,
            jnp.sum(grad_mixed, axis=0),
            grad_gain_b,
            grad_shift_b,
        )
        totals_next = jax.tree.map(jnp.add, totals_now, increments)
        return (totals_next, (layer_rows, grad_rows))

    model_width = w_out.shape[1] * lax.axis_size("dp")
    starting = (
        jnp.zeros((model_width, 3 * local_width), f32),
        jnp.zeros((local_width, model_width), f32),
        jnp.zeros((model_width, local_hidden), f32),
        jnp.zeros((local_hidden, model_width), f32),
        jnp.zeros((local_width,), f32),
        jnp.zeros((local_width,), f32),
        jnp.zeros((local_hidden,), f32),
        jnp.zeros((model_width,), f32),
        jnp.zeros((model_width,), f32),
        jnp.zeros((model_width,), f32),
        jnp.zeros((model_width,), f32),
        jnp.zeros((model_width,), f32),
        jnp.zeros((model_width,), f32),
    )
    totals, stacked = lax.scan(one_batch, starting, (inputs, lengths, cotangent))
    layer_out, grad_inputs = stacked
    grad_joined_w = totals[0]
    reduced_rows = (
        lax.psum_scatter(grad_joined_w[:, :local_width], "dp", scatter_dimension=0, tiled=True),
        lax.psum_scatter(
            grad_joined_w[:, local_width : 2 * local_width], "dp", scatter_dimension=0, tiled=True
        ),
        lax.psum_scatter(
            grad_joined_w[:, 2 * local_width :], "dp", scatter_dimension=0, tiled=True
        ),
        lax.psum_scatter(totals[2], "dp", scatter_dimension=0, tiled=True),
    )
    reduced_columns = (
        lax.psum_scatter(totals[1], "dp", scatter_dimension=1, tiled=True),
        lax.psum_scatter(totals[3], "dp", scatter_dimension=1, tiled=True),
    )
    bias_sums = lax.psum((totals[4], totals[5], totals[6]), "dp")
    norm_sums = lax.psum(
        (totals[7], totals[8], totals[9], totals[10], totals[11], totals[12]), ("dp", "tensor")
    )
    return (
        layer_out,
        grad_inputs,
        reduced_rows[0],
        reduced_rows[1],
        reduced_rows[2],
        bias_sums[0],
        bias_sums[1],
        reduced_columns[0],
        norm_sums[0],
        norm_sums[1],
        norm_sums[2],
        reduced_rows[3],
        bias_sums[2],
        reduced_columns[1],
        norm_sums[3],
        norm_sums[4],
        norm_sums[5],
    )


def solution(mesh):
    return jax.shard_map(
        on_device,
        mesh=mesh,
        in_specs=(
            P("dp", "tensor", None),
            P("dp"),
            P("dp", "tensor"),
            P("dp", "tensor"),
            P("dp", "tensor"),
            P("tensor"),
            P("tensor"),
            P("tensor", "dp"),
            P(),
            P(),
            P(),
            P("dp", "tensor"),
            P("tensor"),
            P("tensor", "dp"),
            P(),
            P(),
            P(),
            P("dp", "tensor", None),
        ),
        out_specs=(
            P("dp", "tensor", None),
            P("dp", "tensor", None),
            P("dp", "tensor"),
            P("dp", "tensor"),
            P("dp", "tensor"),
            P("tensor"),
            P("tensor"),
            P("tensor", "dp"),
            P(),
            P(),
            P(),
            P("dp", "tensor"),
            P("tensor"),
            P("tensor", "dp"),
            P(),
            P(),
            P(),
        ),
        check_vma=False,
    )
```

profile of v0, /device:TPU:0, one launch (start us, length us, event | category | flops | bytes accessed | tf_op | source)
XLA Modules:
  0.0 1471.8 jit_solution(11094318295025059923)
XLA Ops:
  14.3 1180.0 %while.39 = (s32[]{:T(128)}, f32[1024,768]{1,0:T(8,128)}, f32[256,1024]{1,0:T(8,128)}, f32[1024,1024]{1,0:T(8,128)}, f32[1024,1024]{1,0:T(8,128)}, /*index=5*/f3...) while((s32[]{:T(128)}, f32[1024,768]{1,0:T(8,128)}, ...), condition=%wide.region_28.29_spmd.clone, body=%wide.region_0.28_spmd.clone.sunk | while | flops 22766163968 | bytes 654625408 | solution.py:264
  18.1 11.7 all_gather.57
  29.8 9.5 all_gather.56
  39.4 9.2 all_gather.55
  48.6 9.5 all_gather.54
  58.2 7.7 all-gather.11.cloned.1.call-done
  85.5 75.0 %reduce-scatter.23.cloned.1.call-done = f32[256,1024]{1,0:T(8,128)} async-done(((f32[1024,1024]{1,0:T(8,128)}), f32[256,1024]{1,0:T(8,128)}) %reduce-scatter.23.cloned.1.call-update) | async-done | bytes 1048592 | tf_op jit(solution)/shard_map/while/body/eval_jaxpr/reduce_scatter | solution.py:155
  164.5 45.0 %all-gather.13.cloned.1.call-done = bf16[1024,1024]{1,0:T(8,128)(2,1)} async-done(((bf16[256,1024]{1,0:T(8,128)(2,1)}), bf16[1024,1024]{1,0:T(8,128)(2,1)}) %all-gather.13.cloned.1.call-update) | async-done | bytes 2097168 | tf_op jit(solution)/shard_map/while/body/eval_jaxpr/all_gather | solution.py:164
  209.5 14.9 %multiply_convert_fusion.5 = (bf16[1024,1024]{1,0:T(8,128)(2,1)}, f32[1024,1024]{1,0:T(8,128)}, f32[1024,1024]{1,0:T(8,128)}) fusion(f32[1024]{0:T(1024)S(1)} %get-tuple-element.881, bf16[1024,1024]{1,0:T(8,128)(2,1)} %all-gather.13.cloned.1.call-done, bf16[1024,1024]{1,0:T(8,128)(2,1)} %all-gather.15.cloned.1.call-done), kind=kOutput, calls=%fused_computation.26.clone.1 | convolution fusion | flops 2216689664 | bytes 14684160 | tf_op jit(solution)/shard_map/while/body/eval_jaxpr/dot_general | solution.py:165
  224.4 13.8 all-gather.17.cloned.1.call-done
  238.2 6.6 fusion.240
  245.6 76.2 %reduce-scatter.25.cloned.1.call-done = f32[256,1024]{1,0:T(8,128)} async-done(((f32[1024,1024]{1,0:T(8,128)}), f32[256,1024]{1,0:T(8,128)}) %reduce-scatter.25.cloned.1.call-update) | async-done | bytes 1048592 | tf_op jit(solution)/shard_map/while/body/eval_jaxpr/reduce_scatter | solution.py:168
  330.0 46.5 %all-gather.19.cloned.1.call-done = bf16[1024,1024]{1,0:T(8,128)(2,1)} async-done(((bf16[256,1024]{1,0:T(8,128)(2,1)}), bf16[1024,1024]{1,0:T(8,128)(2,1)}) %all-gather.19.cloned.1.call-update) | async-done | bytes 2097168 | tf_op jit(solution)/shard_map/while/body/eval_jaxpr/all_gather | solution.py:182
  376.4 8.5 convert_reduce_fusion.6
  390.7 75.6 %reduce-scatter.27.cloned.1.call-done = f32[256,1024]{1,0:T(8,128)} async-done(((f32[1024,1024]{1,0:T(8,128)}), f32[256,1024]{1,0:T(8,128)}) %reduce-scatter.27.cloned.1.call-update) | async-done | bytes 1048592 | tf_op jit(solution)/shard_map/while/body/eval_jaxpr/reduce_scatter | solution.py:189
  471.0 45.9 %all-gather.21.cloned.1.call-done = bf16[1024,1024]{1,0:T(8,128)(2,1)} async-done(((bf16[256,1024]{1,0:T(8,128)(2,1)}), bf16[1024,1024]{1,0:T(8,128)(2,1)}) %all-gather.21.cloned.1.call-update) | async-done | bytes 2097168 | tf_op jit(solution)/shard_map/while/body/eval_jaxpr/all_gather | solution.py:194
  525.4 6.1 fusion.248
  531.6 9.1 multiply_reduce_fusion.13
  540.7 8.1 multiply_convert_fusion.6
  560.8 7.0 select_add_fusion.23
  578.3 24.3 %reduce-scatter.29.cloned.1.call-done = bf16[256,1024]{1,0:T(8,128)(2,1)} async-done(((bf16[1024,1024]{1,0:T(8,128)(2,1)}), bf16[256,1024]{1,0:T(8,128)(2,1)}) %reduce-scatter.29.cloned.1.call-update) | async-done | bytes 524304 | tf_op jit(solution)/shard_map/while/body/eval_jaxpr/reduce_scatter | solution.py:223
  609.1 10.2 all_gather.57
  619.3 9.5 all_gather.56
  628.9 9.2 all_gather.55
  638.1 9.5 all_gather.54
  672.7 75.0 %reduce-scatter.23.cloned.1.call-done = f32[256,1024]{1,0:T(8,128)} async-done(((f32[1024,1024]{1,0:T(8,128)}), f32[256,1024]{1,0:T(8,128)}) %reduce-scatter.23.cloned.1.call-update) | async-done | bytes 1048592 | tf_op jit(solution)/shard_map/while/body/eval_jaxpr/reduce_scatter | solution.py:155
  751.3 45.4 %all-gather.13.cloned.1.call-done = bf16[1024,1024]{1,0:T(8,128)(2,1)} async-done(((bf16[256,1024]{1,0:T(8,128)(2,1)}), bf16[1024,1024]{1,0:T(8,128)(2,1)}) %all-gather.13.cloned.1.call-update) | async-done | bytes 2097168 | tf_op jit(solution)/shard_map/while/body/eval_jaxpr/all_gather | solution.py:164
  796.7 14.9 %multiply_convert_fusion.5 = (bf16[1024,1024]{1,0:T(8,128)(2,1)}, f32[1024,1024]{1,0:T(8,128)}, f32[1024,1024]{1,0:T(8,128)}) fusion(f32[1024]{0:T(1024)S(1)} %get-tuple-element.881, bf16[1024,1024]{1,0:T(8,128)(2,1)} %all-gather.13.cloned.1.call-done, bf16[1024,1024]{1,0:T(8,128)(2,1)} %all-gather.15.cloned.1.call-done), kind=kOutput, calls=%fused_computation.26.clone.1 | convolution fusion | flops 2216689664 | bytes 14684160 | tf_op jit(solution)/shard_map/while/body/eval_jaxpr/dot_general | solution.py:165
  811.6 13.8 all-gather.17.cloned.1.call-done
  825.4 6.6 fusion.240
  832.8 76.2 %reduce-scatter.25.cloned.1.call-done = f32[256,1024]{1,0:T(8,128)} async-done(((f32[1024,1024]{1,0:T(8,128)}), f32[256,1024]{1,0:T(8,128)}) %reduce-scatter.25.cloned.1.call-update) | async-done | bytes 1048592 | tf_op jit(solution)/shard_map/while/body/eval_jaxpr/reduce_scatter | solution.py:168
  917.2 46.5 %all-gather.19.cloned.1.call-done = bf16[1024,1024]{1,0:T(8,128)(2,1)} async-done(((bf16[256,1024]{1,0:T(8,128)(2,1)}), bf16[1024,1024]{1,0:T(8,128)(2,1)}) %all-gather.19.cloned.1.call-update) | async-done | bytes 2097168 | tf_op jit(solution)/shard_map/while/body/eval_jaxpr/all_gather | solution.py:182
  963.6 8.5 convert_reduce_fusion.6
  977.9 75.6 %reduce-scatter.27.cloned.1.call-done = f32[256,1024]{1,0:T(8,128)} async-done(((f32[1024,1024]{1,0:T(8,128)}), f32[256,1024]{1,0:T(8,128)}) %reduce-scatter.27.cloned.1.call-update) | async-done | bytes 1048592 | tf_op jit(solution)/shard_map/while/body/eval_jaxpr/reduce_scatter | solution.py:189
  1058.3 45.9 %all-gather.21.cloned.1.call-done = bf16[1024,1024]{1,0:T(8,128)(2,1)} async-done(((bf16[256,1024]{1,0:T(8,128)(2,1)}), bf16[1024,1024]{1,0:T(8,128)(2,1)}) %all-gather.21.cloned.1.call-update) | async-done | bytes 2097168 | tf_op jit(solution)/shard_map/while/body/eval_jaxpr/all_gather | solution.py:194
  1112.6 6.1 fusion.248
  1118.8 9.1 multiply_reduce_fusion.13
  1127.9 8.1 multiply_convert_fusion.6
  1148.2 8.2 select_add_fusion.23
  1156.5 6.8 select_add_fusion.22
  1172.2 17.8 %reduce-scatter.29.cloned.1.call-done = bf16[256,1024]{1,0:T(8,128)(2,1)} async-done(((bf16[1024,1024]{1,0:T(8,128)(2,1)}), bf16[256,1024]{1,0:T(8,128)(2,1)}) %reduce-scatter.29.cloned.1.call-update) | async-done | bytes 524304 | tf_op jit(solution)/shard_map/while/body/eval_jaxpr/reduce_scatter | solution.py:223
  1201.3 14.1 all-reduce.1
  1215.4 39.5 %all-reduce = (f32[1024]{0:T(1024)}, f32[1024]{0:T(1024)}, f32[1024]{0:T(1024)}, f32[1024]{0:T(1024)}, f32[1024]{0:T(1024)}, /*index=5*/f32[1024]{0:T(1024)}) all-reduce(f32[1024]{0:T(1024)S(1)} %copy-done.28, f32[1024]{0:T(1024)S(1)} %copy-done.25, f32[1024]{0:T(1024)S(1)} %copy-done.22, ...), channel_id=1, replica_groups=mesh['dp'=8,'tensor'=4] {'dp','tensor'}, use_global_device_ids=true, to_apply=%region_35.36 | all-reduce | flops 6144 | bytes 49152 | tf_op jit(solution)/shard_map/psum | solution.py:282
  1254.9 19.2 %reduce-scatter.15.cloned.1.call-done = f32[128,256]{1,0:T(8,128)} async-done(((f32[1024,256]{1,0:T(8,128)}), f32[128,256]{1,0:T(8,128)}) %reduce-scatter.15.cloned.1.call-update) | async-done | bytes 131088 | tf_op jit(solution)/shard_map/reduce_scatter | solution.py:272
  1274.1 39.8 %reduce-scatter.11.cloned.1.call-done = f32[128,256]{1,0:T(8,128)} async-done(((f32[1024,256]{1,0:T(8,128)}), f32[128,256]{1,0:T(8,128)}) %reduce-scatter.11.cloned.1.call-update) | async-done | bytes 131088 | tf_op jit(solution)/shard_map/reduce_scatter | solution.py:268
  1313.9 39.7 %reduce-scatter.13.cloned.1.call-done = f32[128,256]{1,0:T(8,128)} async-done(((f32[1024,256]{1,0:T(8,128)}), f32[128,256]{1,0:T(8,128)}) %reduce-scatter.13.cloned.1.call-update) | async-done | bytes 131088 | tf_op jit(solution)/shard_map/reduce_scatter | solution.py:269
  1353.6 55.3 %reduce-scatter.19.cloned.1.call-done = f32[128,1024]{1,0:T(8,128)} async-done(((f32[1024,1024]{1,0:T(8,128)}), f32[128,1024]{1,0:T(8,128)}) %reduce-scatter.19.cloned.1.call-update) | async-done | bytes 524304 | tf_op jit(solution)/shard_map/reduce_scatter | solution.py:275
  1408.9 55.5 %reduce-scatter.21.cloned.1.call-done = f32[1024,128]{1,0:T(8,128)} async-done(((f32[1024,1024]{1,0:T(8,128)}), f32[1024,128]{1,0:T(8,128)}) %reduce-scatter.21.cloned.1.call-update) | async-done | bytes 524304 | tf_op jit(solution)/shard_map/reduce_scatter | solution.py:279
  (384 shorter events, 175.9 us)
Async XLA Ops:
  14.3 51.6 %all-gather.11.cloned.1.call-start = ((), (), s32[]{:S(2)}) async-start(), calls=%async_computation.16 | async-start | bytes 2621440 | tf_op jit(solution)/shard_map/while/body/eval_jaxpr/all_gather | solution.py:136
  16.2 144.3 %reduce-scatter.23.cloned.1.call-start = ((), (), s32[]{:S(2)}) async-start(), calls=%async_computation.17 | async-start | bytes 5242880 | tf_op jit(solution)/shard_map/while/body/eval_jaxpr/reduce_scatter | solution.py:155
  29.8 52.3 %copy-start.12 = (bf16[256,1024]{1,0:T(8,128)(2,1)}, bf16[256,1024]{1,0:T(8,128)(2,1)S(1)}, u32[]{:S(2)}) copy-start(bf16[256,1024]{1,0:T(8,128)(2,1)S(1)} %all_gather.57) | copy-start | bytes 1572868 | tf_op jit(solution)/shard_map/while
  58.2 11.2 copy-start.18
  69.7 10.0 copy-start.4
  84.8 75.7 %copy-start.13 = (bf16[2,256,1024]{2,1,0:T(8,128)(2,1)S(1)}, bf16[2,256,1024]{2,1,0:T(8,128)(2,1)}, u32[]{:S(2)}) copy-start(bf16[2,256,1024]{2,1,0:T(8,128)(2,1)} %get-tuple-element.867) | copy-start | bytes 3145732 | tf_op jit(solution)/shard_map/while
  84.9 79.6 %all-gather.15.cloned.1.call-start = ((), (), s32[]{:S(2)}) async-start(), calls=%async_computation.19 | async-start | bytes 2359296 | tf_op jit(solution)/shard_map/while/body/eval_jaxpr/all_gather | solution.py:78
  85.4 124.0 %all-gather.13.cloned.1.call-start = ((), (), s32[]{:S(2)}) async-start(), calls=%async_computation.18 | async-start | bytes 2621440 | tf_op jit(solution)/shard_map/while/body/eval_jaxpr/all_gather | solution.py:164
  163.3 74.9 %all-gather.17.cloned.1.call-start = ((), (), s32[]{:S(2)}) async-start(), calls=%async_computation.20 | async-start | bytes 2359296 | tf_op jit(solution)/shard_map/while/body/eval_jaxpr/all_gather | solution.py:82
  163.9 157.9 %reduce-scatter.25.cloned.1.call-start = ((), (), s32[]{:S(2)}) async-start(), calls=%async_computation.21 | async-start | bytes 5242880 | tf_op jit(solution)/shard_map/while/body/eval_jaxpr/reduce_scatter | solution.py:168
  244.9 131.5 %all-gather.19.cloned.1.call-start = ((), (), s32[]{:S(2)}) async-start(), calls=%async_computation.22 | async-start | bytes 2621440 | tf_op jit(solution)/shard_map/while/body/eval_jaxpr/all_gather | solution.py:182
  329.9 136.4 %reduce-scatter.27.cloned.1.call-start = ((), (), s32[]{:S(2)}) async-start(), calls=%async_computation.23 | async-start | bytes 5242880 | tf_op jit(solution)/shard_map/while/body/eval_jaxpr/reduce_scatter | solution.py:189
  376.4 9.9 copy-start.37
  390.7 126.3 %all-gather.21.cloned.1.call-start = ((), (), s32[]{:S(2)}) async-start(), calls=%async_computation.24 | async-start | bytes 2621440 | tf_op jit(solution)/shard_map/while/body/eval_jaxpr/all_gather | solution.py:194
  470.8 131.8 %reduce-scatter.29.cloned.1.call-start = ((), (), s32[]{:S(2)}) async-start(), calls=%async_computation.25 | async-start | bytes 2621440 | tf_op jit(solution)/shard_map/while/body/eval_jaxpr/reduce_scatter | solution.py:223
  517.0 14.6 slice-start.2
  519.6 12.0 slice-start
  519.6 11.9 slice-start.3
  574.8 27.8 %copy-start.3 = (f32[256,1024]{1,0:T(8,128)S(1)}, f32[256,1024]{1,0:T(8,128)}, u32[]{:S(2)}) copy-start(f32[256,1024]{1,0:T(8,128)} %copy-done.2) | copy-start | bytes 3145732 | tf_op jit(solution)/shard_map/while
  605.2 47.9 %all-gather.11.cloned.1.call-start = ((), (), s32[]{:S(2)}) async-start(), calls=%async_computation.16 | async-start | bytes 2621440 | tf_op jit(solution)/shard_map/while/body/eval_jaxpr/all_gather | solution.py:136
  607.2 140.5 %reduce-scatter.23.cloned.1.call-start = ((), (), s32[]{:S(2)}) async-start(), calls=%async_computation.17 | async-start | bytes 5242880 | tf_op jit(solution)/shard_map/while/body/eval_jaxpr/reduce_scatter | solution.py:155
  619.3 50.0 %copy-start.12 = (bf16[256,1024]{1,0:T(8,128)(2,1)}, bf16[256,1024]{1,0:T(8,128)(2,1)S(1)}, u32[]{:S(2)}) copy-start(bf16[256,1024]{1,0:T(8,128)(2,1)S(1)} %all_gather.57) | copy-start | bytes 1572868 | tf_op jit(solution)/shard_map/while
  656.9 10.0 copy-start.4
  672.0 75.7 %copy-start.13 = (bf16[2,256,1024]{2,1,0:T(8,128)(2,1)S(1)}, bf16[2,256,1024]{2,1,0:T(8,128)(2,1)}, u32[]{:S(2)}) copy-start(bf16[2,256,1024]{2,1,0:T(8,128)(2,1)} %get-tuple-element.867) | copy-start | bytes 3145732 | tf_op jit(solution)/shard_map/while
  672.1 79.3 %all-gather.15.cloned.1.call-start = ((), (), s32[]{:S(2)}) async-start(), calls=%async_computation.19 | async-start | bytes 2359296 | tf_op jit(solution)/shard_map/while/body/eval_jaxpr/all_gather | solution.py:78
  672.7 124.0 %all-gather.13.cloned.1.call-start = ((), (), s32[]{:S(2)}) async-start(), calls=%async_computation.18 | async-start | bytes 2621440 | tf_op jit(solution)/shard_map/while/body/eval_jaxpr/all_gather | solution.py:164
  750.5 74.9 %all-gather.17.cloned.1.call-start = ((), (), s32[]{:S(2)}) async-start(), calls=%async_computation.20 | async-start | bytes 2359296 | tf_op jit(solution)/shard_map/while/body/eval_jaxpr/all_gather | solution.py:82
  751.1 157.9 %reduce-scatter.25.cloned.1.call-start = ((), (), s32[]{:S(2)}) async-start(), calls=%async_computation.21 | async-start | bytes 5242880 | tf_op jit(solution)/shard_map/while/body/eval_jaxpr/reduce_scatter | solution.py:168
  832.1 131.5 %all-gather.19.cloned.1.call-start = ((), (), s32[]{:S(2)}) async-start(), calls=%async_computation.22 | async-start | bytes 2621440 | tf_op jit(solution)/shard_map/while/body/eval_jaxpr/all_gather | solution.py:182
  917.1 136.4 %reduce-scatter.27.cloned.1.call-start = ((), (), s32[]{:S(2)}) async-start(), calls=%async_computation.23 | async-start | bytes 5242880 | tf_op jit(solution)/shard_map/while/body/eval_jaxpr/reduce_scatter | solution.py:189
  963.6 9.9 copy-start.37
  977.9 126.3 %all-gather.21.cloned.1.call-start = ((), (), s32[]{:S(2)}) async-start(), calls=%async_computation.24 | async-start | bytes 2621440 | tf_op jit(solution)/shard_map/while/body/eval_jaxpr/all_gather | solution.py:194
  1058.0 132.0 %reduce-scatter.29.cloned.1.call-start = ((), (), s32[]{:S(2)}) async-start(), calls=%async_computation.25 | async-start | bytes 2621440 | tf_op jit(solution)/shard_map/while/body/eval_jaxpr/reduce_scatter | solution.py:223
  1104.2 14.6 slice-start.2
  1106.8 12.0 slice-start
  1106.8 11.9 slice-start.3
  1163.2 8.9 copy-start.27
  1163.3 8.9 copy-start.21
  1166.6 23.4 %copy-start.3 = (f32[256,1024]{1,0:T(8,128)S(1)}, f32[256,1024]{1,0:T(8,128)}, u32[]{:S(2)}) copy-start(f32[256,1024]{1,0:T(8,128)} %copy-done.2) | copy-start | bytes 3145732 | tf_op jit(solution)/shard_map/while
  1194.3 60.7 %reduce-scatter.17.cloned.1.call-start = ((), (), s32[]{:S(2)}) async-start(), calls=%async_computation.13 | async-start | bytes 1179648 | tf_op jit(solution)/shard_map/reduce_scatter | solution.py:278
  1195.0 79.1 %reduce-scatter.15.cloned.1.call-start = ((), (), s32[]{:S(2)}) async-start(), calls=%async_computation.12 | async-start | bytes 1179648 | tf_op jit(solution)/shard_map/reduce_scatter | solution.py:272
  1198.7 115.3 %reduce-scatter.11.cloned.1.call-start = ((), (), s32[]{:S(2)}) async-start(), calls=%async_computation.10 | async-start | bytes 1179648 | tf_op jit(solution)/shard_map/reduce_scatter | solution.py:268
  1199.4 154.2 %reduce-scatter.13.cloned.1.call-start = ((), (), s32[]{:S(2)}) async-start(), calls=%async_computation.11 | async-start | bytes 1179648 | tf_op jit(solution)/shard_map/reduce_scatter | solution.py:269
  1200.0 208.9 %reduce-scatter.19.cloned.1.call-start = ((), (), s32[]{:S(2)}) async-start(), calls=%async_computation.14 | async-start | bytes 4718592 | tf_op jit(solution)/shard_map/reduce_scatter | solution.py:275
  1200.1 15.4 %copy-start.22 = (f32[1024]{0:T(1024)S(1)}, f32[1024]{0:T(1024)}, u32[]{:S(2)}) copy-start(f32[1024]{0:T(1024)} %get-tuple-element.216) | copy-start | bytes 12292
  1200.1 15.3 %copy-start.25 = (f32[1024]{0:T(1024)S(1)}, f32[1024]{0:T(1024)}, u32[]{:S(2)}) copy-start(f32[1024]{0:T(1024)} %get-tuple-element.215) | copy-start | bytes 12292
  1200.1 15.3 %copy-start.28 = (f32[1024]{0:T(1024)S(1)}, f32[1024]{0:T(1024)}, u32[]{:S(2)}) copy-start(f32[1024]{0:T(1024)} %get-tuple-element.214) | copy-start | bytes 12292
  1200.7 263.7 %reduce-scatter.21.cloned.1.call-start = ((), (), s32[]{:S(2)}) async-start(), calls=%async_computation.15 | async-start | bytes 4718592 | tf_op jit(solution)/shard_map/reduce_scatter | solution.py:279
  (65 other events, 288.8 us)
Sparse Core Ops, SparseCore 0:
  17.2 48.6 all-gather.10
  85.0 75.4 reduce-scatter.22
  330.1 46.3 all-gather.18
  390.8 75.4 reduce-scatter.26
  607.9 45.1 all-gather.10
  672.2 75.4 reduce-scatter.22
  917.3 46.3 all-gather.18
  978.0 75.4 reduce-scatter.26
  1198.9 35.5 reduce-scatter.16
  1238.1 36.0 reduce-scatter.14
  1277.9 36.0 reduce-scatter.10
  1317.5 36.0 reduce-scatter.12
  1357.5 51.2 reduce-scatter.18
  1413.0 51.3 reduce-scatter.20
Sparse Core Ops, SparseCore 1:
  87.2 26.4 all-gather.14
  163.4 46.0 all-gather.12
  211.4 26.8 all-gather.16
  245.0 76.7 reduce-scatter.24
  470.9 46.0 all-gather.20
  560.3 42.3 reduce-scatter.28
  674.4 26.4 all-gather.14
  750.6 46.0 all-gather.12
  798.6 26.8 all-gather.16
  832.2 76.7 reduce-scatter.24
  1058.1 46.0 all-gather.20
  1147.7 42.3 reduce-scatter.28
where the time goes:
time: 1470 us
  waiting for transfers between devices  1030 us (70%)
  matrix products  206 us (14%)
  blocking collectives  132 us (9%)
  other arithmetic  63.6 us (4%)
  local copies, waits for them, and re-layouts  21.4 us (1%)
  between operations  15.7 us (1%)
    reduce_scatter x2, waiting for transfers between devices, one_batch(): lax.psum_scatter(jnp.dot(hidden_low, matrix_back, preferred_element_type=...  152 us
    reduce_scatter x2, waiting for transfers between devices, one_batch(): lax.psum_scatter(contract_cols(grad_pre_low, matrix_in), 'tensor', scatte...  151 us
    reduce_scatter x2, waiting for transfers between devices, one_batch(): lax.psum_scatter(jnp.dot(context_low, matrix_out, preferred_element_type=...  150 us
    all_gather x2, waiting for transfers between devices, one_batch(): lax.all_gather(grad_mixed.astype(bf16), 'tensor', axis=0, tiled=True)  92.9 us
    all_gather x2, waiting for transfers between devices, one_batch(): lax.all_gather(grad_att.astype(bf16), 'tensor', axis=0, tiled=True)  91.8 us
    all_gather x2, waiting for transfers between devices, one_batch(): full_first = lax.all_gather(first_low, 'tensor', axis=0, tiled=True)  90.3 us
    reduce_scatter x1, waiting for transfers between devices, on_device(): lax.psum_scatter(totals[3], 'dp', scatter_dimension=1, tiled=True)  55.5 us
    reduce_scatter x1, waiting for transfers between devices, on_device(): lax.psum_scatter(totals[2], 'dp', scatter_dimension=0, tiled=True)  55.3 us
  transfers between devices with their start and end apart: 26, of which 23 were waited for; matrix products, arithmetic and copies ran while one was open for 6% of the time, Pallas kernels for 0%

commit v1 on v0

v1 whole, which is shorter than its diff:
```python
import jax
import jax.numpy as jnp
from jax import lax
from jax.experimental import pallas as pl
from jax.experimental.pallas import tpu as pltpu
from jax.sharding import Mesh, PartitionSpec as P

HD = 64
EPSILON = 1e-05
NEGATIVE = -1e30
f32 = jnp.float32
bf16 = jnp.bfloat16
SWAP = [(0, 1), (1, 0)]


def nt(a, b):
    return lax.dot_general(a, b, (((1,), (1,)), ((), ())), preferred_element_type=f32)


def tn(a, b):
    return lax.dot_general(a, b, (((0,), (0,)), ((), ())), preferred_element_type=f32)


def nn(a, b):
    return lax.dot_general(a, b, (((1,), (0,)), ((), ())), preferred_element_type=f32)


def attend_fwd_kernel(block, qkv_ref, kb_ref, ctx_ref, lse_ref):
    rows = qkv_ref.shape[0]
    lane = lax.broadcasted_iota(jnp.int32, (1, 2 * HD), 1)
    keys = qkv_ref[:, 2 * HD : 4 * HD]
    values_t = qkv_ref[:, 4 * HD : 6 * HD].T
    key_bias = kb_ref[...]
    for start in range(0, rows, block):
        query = qkv_ref[start : start + block, 0 : 2 * HD]
        parts = []
        for h in range(2):
            query_h = jnp.where(lane // HD == h, query, jnp.zeros_like(query))
            scores = nt(keys, query_h) + key_bias
            largest = jnp.max(scores, axis=0, keepdims=True)
            weights = jnp.exp(scores - largest)
            total = jnp.sum(weights, axis=0, keepdims=True)
            part = nn(values_t[h * HD : (h + 1) * HD], weights.astype(bf16))
            parts.append(part / total)
            lse_ref[0, h : h + 1, start : start + block] = largest + jnp.log(total)
        ctx_ref[start : start + block, :] = jnp.concatenate(parts, axis=0).T.astype(bf16)


def attend_fwd(qkv, key_bias):
    rows = qkv.shape[0]
    groups = qkv.shape[1] // (6 * HD)
    block = min(512, rows)
    return pl.pallas_call(
        lambda *refs: attend_fwd_kernel(block, *refs),
        grid=(groups,),
        in_specs=[
            pl.BlockSpec((rows, 6 * HD), lambda j: (0, j)),
            pl.BlockSpec((rows, 1), lambda j: (0, 0)),
        ],
        out_specs=[
            pl.BlockSpec((rows, 2 * HD), lambda j: (0, j)),
            pl.BlockSpec((1, 2, rows), lambda j: (j, 0, 0)),
        ],
        out_shape=[
            jax.ShapeDtypeStruct((rows, groups * 2 * HD), bf16),
            jax.ShapeDtypeStruct((groups, 2, rows), f32),
        ],
        compiler_params=pltpu.CompilerParams(vmem_limit_bytes=48 << 20),
        cost_estimate=pl.CostEstimate(
            flops=groups * 8 * rows * rows * HD * 4,
            bytes_accessed=rows * groups * 8 * HD * 2,
            transcendentals=groups * 2 * rows * rows,
        ),
        name="attend_fwd",
    )(qkv, key_bias)


def attend_bwd_kernel(block, qkv_ref, g_ref, lse_ref, kb_ref, d_ref, dk_acc, dv_acc):
    rows = qkv_ref.shape[0]
    lane = lax.broadcasted_iota(jnp.int32, (1, 2 * HD), 1)
    keys = qkv_ref[:, 2 * HD : 4 * HD]
    keys_t = keys.T
    values = qkv_ref[:, 4 * HD : 6 * HD]
    key_bias = kb_ref[...]
    for start in range(0, rows, block):
        query = qkv_ref[start : start + block, 0 : 2 * HD]
        grad = g_ref[start : start + block, :]
        parts = []
        for h in range(2):
            here = lane // HD == h
            query_h = jnp.where(here, query, jnp.zeros_like(query))
            grad_h = jnp.where(here, grad, jnp.zeros_like(grad))
            scores = nt(keys, query_h) + key_bias
            chances = jnp.exp(scores - lse_ref[0, h : h + 1, start : start + block])
            grad_chances = nt(values, grad_h)
            inner = jnp.sum(chances * grad_chances, axis=0, keepdims=True)
            grad_scores = (chances * (grad_chances - inner)).astype(bf16)
            dv = nn(chances.astype(bf16), grad_h)
            dk = nn(grad_scores, query_h)
            if start == 0 and h == 0:
                dv_acc[...] = dv
                dk_acc[...] = dk
            else:
                dv_acc[...] += dv
                dk_acc[...] += dk
            parts.append(nn(keys_t[h * HD : (h + 1) * HD], grad_scores))
        d_ref[start : start + block, 0 : 2 * HD] = jnp.concatenate(parts, axis=0).T.astype(bf16)
    d_ref[:, 2 * HD : 4 * HD] = dk_acc[...].astype(bf16)
    d_ref[:, 4 * HD : 6 * HD] = dv_acc[...].astype(bf16)


def attend_bwd(qkv, grad_context, lse, key_bias):
    rows = qkv.shape[0]
    groups = qkv.shape[1] // (6 * HD)
    block = min(512, rows)
    return pl.pallas_call(
        lambda *refs: attend_bwd_kernel(block, *refs),
        grid=(groups,),
        in_specs=[
            pl.BlockSpec((rows, 6 * HD), lambda j: (0, j)),
            pl.BlockSpec((rows, 2 * HD), lambda j: (0, j)),
            pl.BlockSpec((1, 2, rows), lambda j: (j, 0, 0)),
            pl.BlockSpec((rows, 1), lambda j: (0, 0)),
        ],
        out_specs=pl.BlockSpec((rows, 6 * HD), lambda j: (0, j)),
        out_shape=jax.ShapeDtypeStruct((rows, groups * 6 * HD), bf16),
        scratch_shapes=[pltpu.VMEM((rows, 2 * HD), f32), pltpu.VMEM((rows, 2 * HD), f32)],
        compiler_params=pltpu.CompilerParams(vmem_limit_bytes=48 << 20),
        cost_estimate=pl.CostEstimate(
            flops=groups * 20 * rows * rows * HD * 4,
            bytes_accessed=rows * groups * 14 * HD * 2,
            transcendentals=groups * 2 * rows * rows,
        ),
        name="attend_bwd",
    )(qkv, grad_context, lse, key_bias)


def swap_cores(value):
    return lax.ppermute(value, "core", SWAP)


def on_device(
    inputs,
    lengths,
    w_query,
    w_key,
    w_value,
    b_query,
    b_value,
    w_out,
    b_out,
    gain_one,
    shift_one,
    w_in,
    b_in,
    w_back,
    b_back,
    gain_two,
    shift_two,
    cotangent,
):
    planes = lax.axis_size("plane")
    n_t = lax.axis_size("tensor")
    plane = lax.axis_index("plane")
    core = lax.axis_index("core")
    place = lax.axis_index("tensor")
    seqs, slots_here, width = inputs.shape
    slots = slots_here * n_t
    half_slots = slots_here // 2
    own = slots // 2
    assert seqs * 2 == n_t
    head_cols = w_query.shape[1] // 2
    ff_cols = w_in.shape[1] // 2
    scale = HD ** (-0.5)
    quad = planes == 4
    ring = [(i, (i + 1) % n_t) for i in range(n_t)]
    x_pairs = [(i, i ^ 1) for i in range(planes)]
    y_pairs = [(i, i ^ 2) for i in range(planes)]

    def reorder(value, axis):
        if not quad:
            return value
        size = value.shape[axis] // 4
        return jnp.concatenate(
            [lax.dynamic_slice_in_dim(value, (plane ^ k) * size, size, axis) for k in range(4)],
            axis=axis,
        )

    def by_core(mine, theirs, axis=0):
        first = jnp.where(core == 0, mine, theirs)
        second = jnp.where(core == 0, theirs, mine)
        return jnp.concatenate([first, second], axis=axis)

    def to_chip(rows_here):
        value = reorder(rows_here, 2).reshape(seqs, 2, half_slots, width)
        mine = lax.dynamic_index_in_dim(value, core, 1, keepdims=False)
        other = lax.dynamic_index_in_dim(value, 1 - core, 1, keepdims=False)
        both = by_core(mine, swap_cores(other))
        return lax.all_to_all(both, "tensor", 0, 0, tiled=True).reshape(own, width)

    def from_chip(rows_own):
        value = rows_own.reshape(n_t, half_slots, width)
        value = lax.all_to_all(value, "tensor", 0, 0, tiled=True)
        value = value.reshape(2, seqs, half_slots, width)
        mine = lax.dynamic_index_in_dim(value, core, 0, keepdims=False)
        other = lax.dynamic_index_in_dim(value, 1 - core, 0, keepdims=False)
        got = swap_cores(other)
        value = jnp.stack(
            [jnp.where(core == 0, mine, got), jnp.where(core == 0, got, mine)], axis=1
        )
        return reorder(value.reshape(seqs, slots_here, width), 2)

    own_x = to_chip(inputs)
    their_lengths = swap_cores(lengths)
    all_lengths = by_core(lengths, their_lengths)
    length = lax.dynamic_index_in_dim(all_lengths, place, 0, keepdims=False)
    index = jnp.arange(slots)
    position = (
        (index % own) // half_slots * slots_here
        + ((index // own) ^ core) * half_slots
        + index % half_slots
    )
    valid = position < length
    key_bias = jnp.where(valid, 0.0, NEGATIVE).astype(f32)[:, None]
    own_valid = valid[:own, None]

    def halves(value, cols):
        return (
            lax.dynamic_slice_in_dim(value, core * cols, cols, 1),
            lax.dynamic_slice_in_dim(value, (1 - core) * cols, cols, 1),
        )

    pieces = [
        halves(w_query, head_cols),
        halves(w_key, head_cols),
        halves(w_value, head_cols),
        halves(w_out.T, head_cols),
        halves(w_in, ff_cols),
        halves(w_back.T, ff_cols),
    ]
    keep = jnp.concatenate([piece[0] for piece in pieces], axis=1)
    give = jnp.concatenate([piece[1] for piece in pieces], axis=1)
    packed = by_core(keep, swap_cores(give))
    cuts = (4 * head_cols, 4 * head_cols + ff_cols)
    bundle_a = packed[:, : cuts[0]]
    bundle_b = packed[:, cuts[0] : cuts[1]]
    bundle_c = packed[:, cuts[1] :]

    def gather_z(own_piece):
        got = [own_piece]
        for _ in range(n_t - 1):
            got.append(lax.ppermute(got[-1], "tensor", ring))
        return jnp.stack(got)

    def gather_planes(mine):
        if not quad:
            return lax.all_gather(mine, "plane", axis=1, tiled=True)
        half = n_t // 2
        from_x = lax.ppermute(mine, "plane", x_pairs)
        from_y = lax.ppermute(mine, "plane", y_pairs)
        low = lax.ppermute(from_y[:half], "plane", x_pairs)
        high = lax.ppermute(from_x[half:], "plane", y_pairs)
        return jnp.concatenate([mine, from_x, from_y, jnp.concatenate([low, high])], axis=1)

    def flat(gathered):
        return jnp.concatenate([gathered[j] for j in range(n_t)], axis=1)

    bias_row = jnp.concatenate(
        [
            lax.dynamic_slice_in_dim(b_query, core * head_cols, head_cols),
            lax.dynamic_slice_in_dim(b_value, core * head_cols, head_cols),
            lax.dynamic_slice_in_dim(b_in, core * ff_cols, ff_cols),
        ]
    )[None]
    biases = gather_z(bias_row)[:, 0].astype(f32)
    z_a = gather_z(bundle_a)
    full_a = gather_planes(z_a)
    w_qkv = flat(full_a[:, :, : 3 * head_cols])
    w_o = flat(full_a[:, :, 3 * head_cols :])
    w_1 = flat(gather_planes(gather_z(bundle_b)))
    w_2 = flat(gather_planes(gather_z(bundle_c)))

    zeros_k = jnp.zeros((n_t, head_cols), f32)
    qkv_bias = jnp.concatenate(
        [biases[:, :head_cols], zeros_k, biases[:, head_cols : 2 * head_cols]], axis=1
    ).reshape(1, -1)
    qkv_scale = jnp.tile(
        jnp.concatenate([jnp.full((head_cols,), scale, f32), jnp.ones((2 * head_cols,), f32)]), n_t
    )[None]
    in_bias = biases[:, 2 * head_cols :].reshape(1, -1)
    out_bias = reorder(b_out, 0).astype(f32)
    back_bias = reorder(b_back, 0).astype(f32)
    gain_first = reorder(gain_one, 0).astype(f32)
    shift_first = reorder(shift_one, 0).astype(f32)
    gain_second = reorder(gain_two, 0).astype(f32)
    shift_second = reorder(shift_two, 0).astype(f32)

    def both_rows(value):
        return jnp.concatenate([value, swap_cores(value)], axis=0)

    def own_sum(partial):
        return partial[:own] + swap_cores(partial[own:])

    def normalize(value):
        average = jnp.mean(value, axis=-1, keepdims=True)
        centered = value - average
        variance = jnp.mean(centered * centered, axis=-1, keepdims=True)
        inverse = lax.rsqrt(variance + EPSILON)
        return centered * inverse, inverse

    def normalize_back(grad, gain, normed, inverse):
        e = grad * gain
        return (
            e
            - jnp.mean(e, axis=-1, keepdims=True)
            - normed * jnp.mean(e * normed, axis=-1, keepdims=True)
        ) * inverse

    x_full = both_rows(own_x)
    qkv = ((nn(x_full, w_qkv) + qkv_bias) * qkv_scale).astype(bf16)
    context, lse = attend_fwd(qkv, key_bias)
    attended = own_sum(nt(context, w_o))
    normed_one, inverse_one = normalize(own_x.astype(f32) + attended + out_bias)
    first_norm = normed_one * gain_first + shift_first
    first_full = both_rows(first_norm.astype(bf16))
    pre_act = nn(first_full, w_1) + in_bias
    activated, gelu_back = jax.vjp(lambda v: jax.nn.gelu(v, approximate=False), pre_act)
    hidden = activated.astype(bf16)
    mixed = own_sum(nt(hidden, w_2))
    normed_two, inverse_two = normalize(first_norm + mixed + back_bias)
    second = normed_two * gain_second + shift_second
    layer_out = from_chip(jnp.where(own_valid, second, 0.0).astype(bf16))

    grad_second = jnp.where(own_valid, to_chip(cotangent).astype(f32), 0.0)
    grad_mixed = normalize_back(grad_second, gain_second, normed_two, inverse_two)
    grad_mixed_full = both_rows(grad_mixed.astype(bf16))
    grad_w2 = tn(grad_mixed_full, hidden)
    (grad_pre,) = gelu_back(nn(grad_mixed_full, w_2))
    grad_pre_low = grad_pre.astype(bf16)
    grad_w1 = tn(first_full, grad_pre_low)
    grad_first = grad_mixed + own_sum(nt(grad_pre_low, w_1))
    grad_att = normalize_back(grad_first, gain_first, normed_one, inverse_one)
    grad_att_full = both_rows(grad_att.astype(bf16))
    grad_context = nn(grad_att_full, w_o).astype(bf16)
    grad_wo = tn(grad_att_full, context)
    grad_qkv = attend_bwd(qkv, grad_context, lse, key_bias)
    grad_qkv = grad_qkv * qkv_scale.astype(bf16)
    grad_wqkv = tn(x_full, grad_qkv)
    grad_rows = grad_att + own_sum(nt(grad_qkv, w_qkv))
    grad_inputs = from_chip(grad_rows.astype(bf16)).astype(f32)

    def scatter(grad):
        cols = grad.shape[1] // n_t
        if quad:
            rows = width // 4
            blocks = grad.reshape(4, rows, n_t, cols).transpose(0, 2, 1, 3)
            half = n_t // 2
            low = lax.ppermute(blocks[3, :half].astype(bf16), "plane", x_pairs)
            high = lax.ppermute(blocks[3, half:].astype(bf16), "plane", y_pairs)
            for_y = jnp.concatenate([blocks[2, :half] + low.astype(f32), blocks[2, half:]])
            for_x = jnp.concatenate([blocks[1, :half], blocks[1, half:] + high.astype(f32)])
            from_x = lax.ppermute(for_x.astype(bf16), "plane", x_pairs)
            from_y = lax.ppermute(for_y.astype(bf16), "plane", y_pairs)
            mine = blocks[0] + from_x.astype(f32) + from_y.astype(f32)
        else:
            blocks = grad.reshape(width, n_t, cols).transpose(1, 0, 2)
            mine = lax.psum_scatter(
                blocks.astype(bf16), "plane", scatter_dimension=1, tiled=True
            ).astype(f32)
        back = [(b, a) for a, b in ring]
        total = mine[n_t - 1]
        for j in range(n_t - 2, -1, -1):
            total = mine[j] + lax.ppermute(total.astype(bf16), "tensor", back).astype(f32)
        return total

    home_c = scatter(grad_w2)
    home_b = scatter(grad_w1)
    grad_a = jnp.concatenate(
        [
            grad_wqkv.reshape(width, n_t, 3 * head_cols),
            grad_wo.reshape(width, n_t, head_cols),
        ],
        axis=2,
    ).reshape(width, -1)
    home_a = scatter(grad_a)
    home = jnp.concatenate([home_a, home_b, home_c], axis=1)
    home = home.reshape(2, -1, home.shape[1])
    mine = lax.dynamic_index_in_dim(home, core, 0, keepdims=False)
    other = lax.dynamic_index_in_dim(home, 1 - core, 0, keepdims=False)
    got = swap_cores(other)

    def columns(start, cols):
        return by_core(mine[:, start : start + cols], got[:, start : start + cols], axis=1)

    grad_w_query = columns(0, head_cols)
    grad_w_key = columns(head_cols, head_cols)
    grad_w_value = columns(2 * head_cols, head_cols)
    grad_w_out = columns(3 * head_cols, head_cols).T
    grad_w_in = columns(cuts[0], ff_cols)
    grad_w_back = columns(cuts[1], ff_cols).T

    def row_sum(value):
        return reorder(jnp.sum(value, axis=0), 0)

    norm_sums = jnp.concatenate(
        [
            row_sum(grad_att),
            row_sum(grad_first * normed_one),
            row_sum(grad_first),
            row_sum(grad_mixed),
            row_sum(grad_second * normed_two),
            row_sum(grad_second),
        ]
    )
    qkv_sum = jnp.sum(grad_qkv.astype(f32), axis=0).reshape(n_t, 3 * head_cols)
    pre_sum = jnp.sum(grad_pre_low.astype(f32), axis=0).reshape(n_t, ff_cols)
    bias_sum = jnp.concatenate([qkv_sum[:, :head_cols], qkv_sum[:, 2 * head_cols :], pre_sum], axis=1)
    at_home = lax.rem(place - jnp.arange(n_t) + n_t, n_t)
    spread = (at_home[:, None] == jnp.arange(n_t)[None]).astype(f32)
    by_place = jnp.sum(spread[:, :, None] * bias_sum[:, None, :], axis=0)
    both = jnp.where(
        (jnp.arange(2) == core)[None, :, None], by_place[:, None, :], 0.0
    )
    sums = lax.psum(jnp.concatenate([norm_sums, both.reshape(-1)]), ("plane", "core", "tensor"))
    norms = sums[: 6 * width].reshape(6, width)
    biases_out = lax.dynamic_index_in_dim(
        sums[6 * width :].reshape(n_t, 2, -1), place, 0, keepdims=False
    )
    grad_b_query = biases_out[:, :head_cols].reshape(-1)
    grad_b_value = biases_out[:, head_cols : 2 * head_cols].reshape(-1)
    grad_b_in = biases_out[:, 2 * head_cols :].reshape(-1)
    return (
        layer_out,
        grad_inputs,
        grad_w_query,
        grad_w_key,
        grad_w_value,
        grad_b_query,
        grad_b_value,
        grad_w_out,
        norms[0],
        norms[1],
        norms[2],
        grad_w_in,
        grad_b_in,
        grad_w_back,
        norms[3],
        norms[4],
        norms[5],
    )


def solution(mesh):
    devices = mesh.devices.reshape(mesh.shape["dp"] // 2, 2, mesh.shape["tensor"])
    inner = Mesh(devices, ("plane", "core", "tensor"))
    dp = ("plane", "core")
    row = P(dp, "tensor")
    column = P("tensor", dp)
    rows3 = P(dp, "tensor", None)
    shard = P("tensor")
    whole = P()
    return jax.shard_map(
        on_device,
        mesh=inner,
        in_specs=(
            rows3, P(dp), row, row, row, shard, shard, column, whole, whole, whole,
            row, shard, column, whole, whole, whole, rows3,
        ),
        out_specs=(
            rows3, rows3, row, row, row, shard, shard, column, whole, whole, whole,
            row, shard, column, whole, whole, whole,
        ),
        check_vma=False,
    )
```

time: 1470 us -> 642 us (0.44)
  waiting for transfers between devices: 1030 us -> 182 us
  matrix products: 206 us -> 97.3 us
  blocking collectives: 132 us -> 40.2 us
  local copies, waits for them, and re-layouts: 21.4 us -> 109 us
  starting transfers between devices: 2.16 us -> 82.4 us
  Pallas kernels: 0 us -> 41.8 us
  other arithmetic: 63.6 us -> 80.7 us
    reduce_scatter x14 -> x0, waiting for transfers between devices: 705 us -> none  [the longest x2 152 us: one_batch(): lax.psum_scatter(jnp.dot(hidden_low, matrix_back, preferred_element_type=...]
    all_gather x12 -> x0, waiting for transfers between devices: 316 us -> none  [the longest x2 92.9 us: one_batch(): lax.all_gather(grad_mixed.astype(bf16), 'tensor', axis=0, tiled=True)]
    ppermute x0 -> x60, waiting for transfers between devices: none -> 157 us  [the longest x12 55.5 us: gather_z(): got.append(lax.ppermute(got[-1], 'tensor', ring))]
    dot_general x48 -> x12, matrix products: 206 us -> 97.3 us  [the longest x4 51.4 us: nn(): lax.dot_general(a, b, (((1,), (0,)), ((), ())), preferred_element_type=f32)]
    all_gather x8 -> x0, blocking collectives: 78.4 us -> none  [the longest x2 21.9 us: fetch_weights(): lax.all_gather(w_out, 'dp', axis=1, tiled=True)]
    ppermute x0 -> x60, starting transfers between devices: none -> 67.2 us  [the longest x9 25.8 us: scatter(): lax.ppermute(total.astype(bf16), 'tensor', back).astype(f32)]
    reshape x0 -> x9, local copies, waits for them, and re-layouts: none -> 45.5 us  [the longest x6 45 us: scatter(): blocks = grad.reshape(4, rows, n_t, cols).transpose(0, 2, 1, 3)]
    pallas_call x0 -> x2, Pallas kernels: none -> 41.8 us  [the longest x1 25.8 us: attend_bwd(): pl.pallas_call(lambda *refs: attend_bwd_kernel(block, *refs), grid=(group...]
  transfers between devices with their start and end apart: 26 -> 64, of which waited for: 23 -> 26; matrix products, arithmetic and copies ran while one was open for 6% -> 34% of each run, Pallas kernels for 0% -> 7%
where the time goes in v1:
time: 642 us; the launch traced here: 635 us
  waiting for transfers between devices  182 us (28%)
  local copies, waits for them, and re-layouts  109 us (17%)
  matrix products  97.3 us (15%)
  starting transfers between devices  82.4 us (13%)
  other arithmetic  80.7 us (13%)
  Pallas kernels  41.8 us (7%)
  blocking collectives  40.2 us (6%)
    ppermute x12, waiting for transfers between devices, gather_z(): got.append(lax.ppermute(got[-1], 'tensor', ring))  55.5 us
    dot_general x4, matrix products, nn(): lax.dot_general(a, b, (((1,), (0,)), ((), ())), preferred_element_type=f32)  51.4 us
    ppermute x3, waiting for transfers between devices, scatter(): from_x = lax.ppermute(for_x.astype(bf16), 'plane', x_pairs)  45.2 us
    reshape x6, local copies, waits for them, and re-layouts, scatter(): blocks = grad.reshape(4, rows, n_t, cols).transpose(0, 2, 1, 3)  45 us
    psum x1, blocking collectives, on_device(): lax.psum(jnp.concatenate([norm_sums, both.reshape(-1)]), ('plane', 'core'...  40.2 us
    dot_general x4, matrix products, tn(): lax.dot_general(a, b, (((0,), (0,)), ((), ())), preferred_element_type=f32)  26 us
    pallas_call x1, Pallas kernels, attend_bwd(): pl.pallas_call(lambda *refs: attend_bwd_kernel(block, *refs), grid=(group...  25.8 us
    ppermute x9, starting transfers between devices, scatter(): lax.ppermute(total.astype(bf16), 'tensor', back).astype(f32)  25.8 us
  transfers between devices with their start and end apart: 64, of which 26 were waited for; matrix products, arithmetic and copies ran while one was open for 34% of the time, Pallas kernels for 7%

profile of v1, /device:TPU:0, one launch (start us, length us, event | category | flops | bytes accessed | tf_op | source)
XLA Modules:
  0.0 635.4 jit_solution(14471210480092756909)
XLA Ops:
  9.4 3.0 collective-permute-start.4
  13.5 7.5 %collective-permute-done.4 = bf16[256,512]{0,1:T(8,128)(2,1)S(1)} collective-permute-done((bf16[256,512]{0,1:T(8,128)(2,1)S(1)}, bf16[256,512]{0,1:T(8,128)(2,1)S(1)}, u32[]{:S(2)}, u32[]{:S(2)}) %collective-permute-start.4) | collective-permute-done | bytes 262176 | tf_op jit(solution)/shard_map/ppermute | solution.py:252
  22.3 8.3 %collective-permute-done.5 = bf16[256,512]{0,1:T(8,128)(2,1)S(1)} collective-permute-done((bf16[256,512]{0,1:T(8,128)(2,1)S(1)}, bf16[256,512]{0,1:T(8,128)(2,1)S(1)}, u32[]{:S(2)}, u32[]{:S(2)}) %collective-permute-start.5) | collective-permute-done | bytes 262176 | tf_op jit(solution)/shard_map/ppermute | solution.py:252
  31.2 8.3 %collective-permute-done.6 = bf16[256,512]{0,1:T(8,128)(2,1)S(1)} collective-permute-done((bf16[256,512]{0,1:T(8,128)(2,1)S(1)}, bf16[256,512]{0,1:T(8,128)(2,1)S(1)}, u32[]{:S(2)}, u32[]{:S(2)}) %collective-permute-start.6) | collective-permute-done | bytes 262176 | tf_op jit(solution)/shard_map/ppermute | solution.py:252
  46.0 4.2 all-to-all-start
  58.2 19.1 %collective-permute-done.12 = bf16[1,768]{1,0:T(2,128)(2,1)S(1)} collective-permute-done((bf16[1,768]{1,0:T(2,128)(2,1)S(1)}, bf16[1,768]{1,0:T(2,128)(2,1)S(1)}, u32[]{:S(2)}, u32[]{:S(2)}) %collective-permute-start.12) | collective-permute-done | bytes 1568 | tf_op jit(solution)/shard_map/ppermute | solution.py:252
  77.3 3.3 collective-permute-start.13
  95.5 5.2 collective-permute-done.25
  115.8 5.3 multiply_convert_fusion.1.refs_0_
  121.2 16.1 %attend_fwd.1 = (bf16[1024,512]{1,0:T(8,128)(2,1)S(1)}, f32[4,2,1024]{2,1,0:T(2,128)S(1)}) custom-call(bf16[1024,1536]{1,0:T(8,128)(2,1)S(1)} %multiply_convert_fusion.1.refs_0_, f32[1024,1]{1,0:T(8,128)S(1)} %fusion.82.refs_1_.refs_3_), custom_call_target="tpu_custom_call" | custom-call | flops 8589934592 | bytes 4194304 | tf_op jit(solution)/shard_map/attend_fwd/pallas_call | solution.py:53
  145.1 6.8 %collective-permute-done.20 = bf16[4,256,512]{1,2,0:T(8,128)(2,1)} collective-permute-done((bf16[4,256,512]{1,2,0:T(8,128)(2,1)}, bf16[4,256,512]{1,2,0:T(8,128)(2,1)}, u32[]{:S(2)}, u32[]{:S(2)}) %collective-permute-start.20) | collective-permute-done | bytes 1048608 | tf_op jit(solution)/shard_map/ppermute | solution.py:260
  155.3 10.6 %collective-permute-done.28 = bf16[2,256,512]{1,2,0:T(8,128)(2,1)S(1)} collective-permute-done((bf16[2,256,512]{1,2,0:T(8,128)(2,1)S(1)}, bf16[2,256,512]{1,2,0:T(8,128)(2,1)S(1)}, u32[]{:S(2)}, u32[]{:S(2)}) %collective-permute-start.28) | collective-permute-done | bytes 524320 | tf_op jit(solution)/shard_map/ppermute | solution.py:261
  180.7 30.3 %multiply_convert_fusion = (bf16[1024,2048]{1,0:T(8,128)(2,1)}, f32[1024,2048]{1,0:T(8,128)}, f32[1024,2048]{1,0:T(8,128)}) fusion(f32[2048]{0:T(1024)S(1)} %bitcast.341, bf16[1024,512]{0,1:T(8,128)(2,1)S(1)} %get-tuple-element.114, bf16[1024,512]{0,1:T(8,128)(2,1)S(1)} %get-tuple-element.115, bf16[1024,512]{0,1:T(8,128)(2,1)} %get-tuple-element.116, ...), kind=kOutput, calls=%fused_computation.7 | convolution fusion | flops 4454350848 | bytes 27271168 | tf_op jit(solution)/shard_map/dot_general | solution.py:25
  211.1 6.7 %fusion.45 = f32[1024,1024]{1,0:T(8,128)S(1)} fusion(bf16[1024,2048]{1,0:T(8,128)(2,1)} %get-tuple-element.87, bf16[1024,512]{0,1:T(8,128)(2,1)S(1)} %get-tuple-element.110, bf16[1024,512]{0,1:T(8,128)(2,1)S(1)} %copy-done.47, bf16[1024,512]{0,1:T(8,128)(2,1)S(1)} %copy-done.48, bf16[1024,512]{0,1:T(8,128)(2,1)S(1)} %get-tuple-element.109), kind=kOutput, calls=%fused_computation.146 | convolution fusion | flops 4311744512 | bytes 12582912 | tf_op jit(solution)/shard_map/dot_general | solution.py:17
  222.4 3.7 all-to-all-start.2
  227.6 25.0 %all-to-all-done.2 = bf16[4,128,1024]{2,1,0:T(8,128)(2,1)S(1)} async-done(((bf16[4,128,1024]{2,1,0:T(8,128)(2,1)}), bf16[4,128,1024]{2,1,0:T(8,128)(2,1)S(1)}, u32[]{:S(2)}, u32[]{:S(2)}) %all-to-all-start.2) | async-done | bytes 1048608 | tf_op jit(solution)/shard_map/all_to_all | solution.py:199
  253.1 3.0 fusion.146
  262.9 3.7 all-to-all-start.1
  266.6 14.5 %convert_reduce_fusion = (f32[2048]{0:T(1024)S(1)}, bf16[1024,2048]{1,0:T(8,128)(2,1)}) fusion(f32[1024,2048]{1,0:T(8,128)} %get-tuple-element.88, bf16[1024,512]{0,1:T(8,128)(2,1)} %copy-done.46, bf16[1024,512]{0,1:T(8,128)(2,1)} %get-tuple-element.111, bf16[1024,512]{0,1:T(8,128)(2,1)} %get-tuple-element.112, bf16[1024,512]{0,1:T(8,128)(2,1)} %copy-done.45, ...), kind=kOutput, calls=%fused_computation.5 | convolution fusion | flops 4351588352 | bytes 27279360 | tf_op jit(solution)/shard_map/dot_general | solution.py:25
  281.2 8.5 %fusion.46 = f32[1024,1024]{1,0:T(8,128)} fusion(bf16[1024,2048]{1,0:T(8,128)(2,1)} %get-tuple-element.221, bf16[1024,512]{0,1:T(8,128)(2,1)S(1)} %copy-done.52, bf16[1024,512]{0,1:T(8,128)(2,1)S(1)} %copy-done.54, bf16[1024,512]{0,1:T(8,128)(2,1)S(1)} %copy-done.55, bf16[1024,512]{0,1:T(8,128)(2,1)S(1)} %copy-done.50), kind=kOutput, calls=%fused_computation.147 | convolution fusion | flops 4311744512 | bytes 12582912 | tf_op jit(solution)/shard_map/dot_general | solution.py:17
  289.7 7.0 %fusion.31 = f32[1024,2048]{1,0:T(8,128)} fusion(bf16[1024,2048]{1,0:T(8,128)(2,1)S(1)} %copy-done.95, bf16[512,1024]{1,0:T(8,128)(2,1)S(1)} %copy-done.89, bf16[512,1024]{1,0:T(8,128)(2,1)S(1)} %copy-done.38), kind=kOutput, calls=%fused_computation.83 | convolution fusion | flops 4299161600 | bytes 14680064 | tf_op jit(solution)/shard_map/dot_general | solution.py:21
  296.7 10.8 %reshape.567 = f32[4,256,4,512]{3,2,1,0:T(4,128)} reshape(f32[1024,2048]{1,0:T(8,128)} %fusion.31) | data formatting | bytes 16777216 | tf_op jit(solution)/shard_map/reshape | solution.py:356
  307.5 5.7 copy.117
  316.4 9.6 %fusion.29 = f32[1024,2048]{1,0:T(8,128)} fusion(bf16[1024,2048]{1,0:T(8,128)(2,1)S(1)} %copy-done.94, bf16[512,1024]{1,0:T(8,128)(2,1)} %collective-permute-done.33, bf16[512,1024]{1,0:T(8,128)(2,1)} %convert_element_type.251), kind=kOutput, calls=%fused_computation.81 | convolution fusion | flops 4299161600 | bytes 14680064 | tf_op jit(solution)/shard_map/dot_general | solution.py:21
  326.0 5.9 copy.115
  331.9 10.8 %reshape.568 = f32[4,256,4,512]{3,2,1,0:T(4,128)} reshape(f32[1024,2048]{1,0:T(8,128)} %fusion.29) | data formatting | bytes 16777216 | tf_op jit(solution)/shard_map/reshape | solution.py:356
  342.7 9.5 %copy.114 = f32[4,256,4,512]{3,1,2,0:T(8,128)} copy(f32[4,256,4,512]{3,2,1,0:T(4,128)} %reshape.568) | data formatting | bytes 16777216 | tf_op jit(solution)/shard_map/reshape | solution.py:356
  366.2 6.4 %collective-permute-done.52 = bf16[2,256,512]{2,1,0:T(8,128)(2,1)} collective-permute-done((bf16[2,256,512]{2,1,0:T(8,128)(2,1)}, bf16[2,256,512]{2,1,0:T(8,128)(2,1)}, u32[]{:S(2)}, u32[]{:S(2)}) %collective-permute-start.52) | collective-permute-done | bytes 524320 | tf_op jit(solution)/shard_map/ppermute | solution.py:359
  377.8 17.4 %collective-permute-done.46 = bf16[4,256,512]{2,1,0:T(8,128)(2,1)} collective-permute-done((bf16[4,256,512]{2,1,0:T(8,128)(2,1)}, bf16[4,256,512]{2,1,0:T(8,128)(2,1)}, u32[]{:S(2)}, u32[]{:S(2)}) %collective-permute-start.46) | collective-permute-done | bytes 1048608 | tf_op jit(solution)/shard_map/ppermute | solution.py:362
  397.9 3.9 collective-permute-start.49
  401.8 15.1 %collective-permute-done.53 = bf16[4,256,512]{2,1,0:T(8,128)(2,1)S(1)} collective-permute-done((bf16[4,256,512]{2,1,0:T(8,128)(2,1)S(1)}, bf16[4,256,512]{2,1,0:T(8,128)(2,1)S(1)}, u32[]{:S(2)}, u32[]{:S(2)}) %collective-permute-start.53) | collective-permute-done | bytes 1048608 | tf_op jit(solution)/shard_map/ppermute | solution.py:362
  419.0 3.9 collective-permute-start.56
  424.7 4.9 collective-permute-done.56
  429.7 4.3 collective-permute-start.57
  440.4 4.2 collective-permute-start.58
  458.2 25.8 %attend_bwd.1 = bf16[1024,1536]{1,0:T(8,128)(2,1)S(1)} custom-call(bf16[1024,1536]{1,0:T(8,128)(2,1)} %copy-done.4, bf16[1024,512]{1,0:T(8,128)(2,1)S(1)} %convolution_convert_fusion.refs_1_, f32[4,2,1024]{2,1,0:T(2,128)S(1)} %get-tuple-element.20.refs_2_, f32[1024,1]{1,0:T(8,128)S(1)} %copy-done.1), custom_call_target="tpu_custom_call" | custom-call | flops 21474836480 | bytes 7340032 | tf_op jit(solution)/shard_map/attend_bwd/pallas_call | solution.py:116
  484.0 6.8 %fusion.6 = f32[1024,1536]{1,0:T(8,128)} fusion(bf16[1024,1536]{1,0:T(8,128)(2,1)S(1)} %attend_bwd.1, bf16[1536]{0:T(1024)(128)(2,1)S(1)} %convert_element_type.255, bf16[512,1024]{1,0:T(8,128)(2,1)S(1)} %copy-done.87, bf16[512,1024]{1,0:T(8,128)(2,1)} %bitcast.4), kind=kOutput, calls=%fused_computation.29 | convolution fusion | flops 3226992640 | bytes 11537408 | tf_op jit(solution)/shard_map/dot_general | solution.py:21
  490.9 7.8 %concatenate.211 = f32[4,256,4,384]{3,2,1,0:T(4,128)} reshape(f32[1024,1536]{1,0:T(8,128)} %fusion.6) | data formatting | bytes 12582912 | tf_op jit(solution)/shard_map/concatenate | solution.py:378
  498.7 3.7 copy.86
  508.9 8.3 %collective-permute-done.38 = bf16[2,256,512]{2,1,0:T(8,128)(2,1)S(1)} collective-permute-done((bf16[2,256,512]{2,1,0:T(8,128)(2,1)}, bf16[2,256,512]{2,1,0:T(8,128)(2,1)S(1)}, u32[]{:S(2)}, u32[]{:S(2)}) %collective-permute-start.38) | collective-permute-done | bytes 524320 | tf_op jit(solution)/shard_map/ppermute | solution.py:359
  524.3 3.4 fusion.8
  532.1 12.6 %collective-permute-done.39 = bf16[4,256,512]{2,1,0:T(8,128)(2,1)} collective-permute-done((bf16[4,256,512]{2,1,0:T(8,128)(2,1)}, bf16[4,256,512]{2,1,0:T(8,128)(2,1)}, u32[]{:S(2)}, u32[]{:S(2)}) %collective-permute-start.39) | collective-permute-done | bytes 1048608 | tf_op jit(solution)/shard_map/ppermute | solution.py:362
  551.6 5.6 collective-permute-done.42
  559.9 4.0 collective-permute-done.43
  565.7 4.1 collective-permute-start.44
  569.8 3.7 fusion.17
  573.5 3.5 all-to-all-start.3
  579.6 40.2 %psum.7 = f32[12288]{0:T(1024)S(1)} all-reduce(f32[12288]{0:T(1024)S(1)} %constant_dynamic-update-slice_fusion.12), channel_id=1, replica_groups=mesh['plane'=4,'core'=2,'tensor'=4] {'plane','core','tensor'}, use_global_device_ids=true, to_apply=%region_17.18 | all-reduce | flops 12288 | bytes 98304 | tf_op jit(solution)/shard_map/psum | solution.py:424
  (511 shorter events, 190.5 us)
Async XLA Ops:
  9.4 11.6 %collective-permute-start.4 = (bf16[256,512]{0,1:T(8,128)(2,1)S(1)}, bf16[256,512]{0,1:T(8,128)(2,1)S(1)}, u32[]{:S(2)}, u32[]{:S(2)}) collective-permute-start(bf16[256,512]{0,1:T(8,128)(2,1)S(1)} %get-tuple-element.165), channel_id=1, source_target_pairs={{0,1},{1,2},{2,3},{3,0},{4,5},{5,6},{6,7},{7,4},{8,9},{9,10},{10,1... | collective-permute-start | bytes 786440 | tf_op jit(solution)/shard_map/ppermute | solution.py:252
  22.1 21.6 %collective-permute-start.1 = (bf16[2,128,1024]{2,1,0:T(8,128)(2,1)}, bf16[2,128,1024]{2,1,0:T(8,128)(2,1)}, u32[]{:S(2)}, u32[]{:S(2)}) collective-permute-start(bf16[2,128,1024]{2,1,0:T(8,128)(2,1)} %dynamic-slice_bitcast_fusion.3), channel_id=1, source_target_pairs={{0,4},{4,0},{1,5},{5,1},{2,6},{6,2},{3,7},{7,3},{8,12},{12,8},{9,1... | collective-permute-start | bytes 1572872 | tf_op jit(solution)/shard_map/ppermute | solution.py:139
  30.9 23.6 %collective-permute-start.11 = (bf16[1,768]{1,0:T(2,128)(2,1)S(1)}, bf16[1,768]{1,0:T(2,128)(2,1)S(1)}, u32[]{:S(2)}, u32[]{:S(2)}) collective-permute-start(bf16[1,768]{1,0:T(2,128)(2,1)S(1)} %broadcast_in_dim.79), channel_id=1, source_target_pairs={{0,1},{1,2},{2,3},{3,0},{4,5},{5,6},{6,7},{7,4},{8,9},{9,10},{10,1... | collective-permute-start | bytes 4616 | tf_op jit(solution)/shard_map/ppermute | solution.py:252
  31.0 23.5 %collective-permute-start = (s32[2]{0:T(128)S(1)}, s32[2]{0:T(128)S(1)}, u32[]{:S(2)}, u32[]{:S(2)}) collective-permute-start(s32[2]{0:T(128)S(1)} %copy-done.84), channel_id=1, source_target_pairs={{0,4},{4,0},{1,5},{5,1},{2,6},{6,2},{3,7},{7,3},{8,12},{12,8},{9,1... | collective-permute-start | bytes 32 | tf_op jit(solution)/shard_map/ppermute | solution.py:139
  41.2 48.3 %collective-permute-start.7 = (bf16[4,256,512]{1,2,0:T(8,128)(2,1)}, bf16[4,256,512]{1,2,0:T(8,128)(2,1)S(1)}, u32[]{:S(2)}, u32[]{:S(2)}) collective-permute-start(bf16[4,256,512]{1,2,0:T(8,128)(2,1)} %pad_maximum_fusion.20), channel_id=1, source_target_pairs={{0,8},{8,0},{16,24},{24,16},{1,9},{9,1},{17,25},{25,17},{2,10},{10... | collective-permute-start | bytes 3145736 | tf_op jit(solution)/shard_map/ppermute | solution.py:259
  42.2 48.7 %collective-permute-start.8 = (bf16[4,256,512]{1,2,0:T(8,128)(2,1)}, bf16[4,256,512]{1,2,0:T(8,128)(2,1)S(1)}, u32[]{:S(2)}, u32[]{:S(2)}) collective-permute-start(bf16[4,256,512]{1,2,0:T(8,128)(2,1)} %pad_maximum_fusion.20), channel_id=1, source_target_pairs={{0,16},{8,24},{16,0},{24,8},{1,17},{9,25},{17,1},{25,9},{2,18},{10... | collective-permute-start | bytes 3145736 | tf_op jit(solution)/shard_map/ppermute | solution.py:260
  46.0 64.0 %all-to-all-start = ((bf16[4,128,1024]{2,1,0:T(8,128)(2,1)}), bf16[4,128,1024]{2,1,0:T(8,128)(2,1)}, u32[]{:S(2)}, u32[]{:S(2)}) async-start(bf16[4,128,1024]{2,1,0:T(8,128)(2,1)} %pad_maximum_fusion.19), calls=%async_computation | async-start | bytes 2097152 | tf_op jit(solution)/shard_map/all_to_all | solution.py:199
  52.5 28.0 %collective-permute-start.23 = (bf16[256,512]{0,1:T(8,128)(2,1)S(1)}, bf16[256,512]{0,1:T(8,128)(2,1)S(1)}, u32[]{:S(2)}, u32[]{:S(2)}) collective-permute-start(bf16[256,512]{0,1:T(8,128)(2,1)S(1)} %get-tuple-element.164), channel_id=1, source_target_pairs={{0,1},{1,2},{2,3},{3,0},{4,5},{5,6},{6,7},{7,4},{8,9},{9,10},{10,1... | collective-permute-start | bytes 786440 | tf_op jit(solution)/shard_map/ppermute | solution.py:252
  54.5 22.7 %collective-permute-start.12 = (bf16[1,768]{1,0:T(2,128)(2,1)S(1)}, bf16[1,768]{1,0:T(2,128)(2,1)S(1)}, u32[]{:S(2)}, u32[]{:S(2)}) collective-permute-start(bf16[1,768]{1,0:T(2,128)(2,1)S(1)} %collective-permute-done.11), channel_id=1, source_target_pairs={{0,1},{1,2},{2,3},{3,0},{4,5},{5,6},{6,7},{7,4},{8,9},{9,10},{10,1... | collective-permute-start | bytes 4616 | tf_op jit(solution)/shard_map/ppermute | solution.py:252
  56.0 28.0 %collective-permute-start.16 = (bf16[256,512]{0,1:T(8,128)(2,1)S(1)}, bf16[256,512]{0,1:T(8,128)(2,1)S(1)}, u32[]{:S(2)}, u32[]{:S(2)}) collective-permute-start(bf16[256,512]{0,1:T(8,128)(2,1)S(1)} %get-tuple-element.166), channel_id=1, source_target_pairs={{0,1},{1,2},{2,3},{3,0},{4,5},{5,6},{6,7},{7,4},{8,9},{9,10},{10,1... | collective-permute-start | bytes 786440 | tf_op jit(solution)/shard_map/ppermute | solution.py:252
  83.9 58.6 %collective-permute-start.32 = (bf16[2,128,1024]{2,1,0:T(8,128)(2,1)}, bf16[2,128,1024]{2,1,0:T(8,128)(2,1)}, u32[]{:S(2)}, u32[]{:S(2)}) collective-permute-start(bf16[2,128,1024]{2,1,0:T(8,128)(2,1)} %dynamic-slice_bitcast_fusion.1), channel_id=1, source_target_pairs={{0,4},{4,0},{1,5},{5,1},{2,6},{6,2},{3,7},{7,3},{8,12},{12,8},{9,1... | collective-permute-start | bytes 1572872 | tf_op jit(solution)/shard_map/ppermute | solution.py:139
  84.0 11.1 %collective-permute-start.17 = (bf16[256,512]{0,1:T(8,128)(2,1)S(1)}, bf16[256,512]{0,1:T(8,128)(2,1)}, u32[]{:S(2)}, u32[]{:S(2)}) collective-permute-start(bf16[256,512]{0,1:T(8,128)(2,1)S(1)} %collective-permute-done.16), channel_id=1, source_target_pairs={{0,1},{1,2},{2,3},{3,0},{4,5},{5,6},{6,7},{7,4},{8,9},{9,10},{10,1... | collective-permute-start | bytes 786440 | tf_op jit(solution)/shard_map/ppermute | solution.py:252
  88.9 11.8 %collective-permute-start.25 = (bf16[256,512]{0,1:T(8,128)(2,1)}, bf16[256,512]{0,1:T(8,128)(2,1)}, u32[]{:S(2)}, u32[]{:S(2)}) collective-permute-start(bf16[256,512]{0,1:T(8,128)(2,1)} %collective-permute-done.24), channel_id=1, source_target_pairs={{0,1},{1,2},{2,3},{3,0},{4,5},{5,6},{6,7},{7,4},{8,9},{9,10},{10,1... | collective-permute-start | bytes 786440 | tf_op jit(solution)/shard_map/ppermute | solution.py:252
  90.4 18.3 %collective-permute-start.10 = (bf16[2,256,512]{1,2,0:T(8,128)(2,1)}, bf16[2,256,512]{1,2,0:T(8,128)(2,1)S(1)}, u32[]{:S(2)}, u32[]{:S(2)}) collective-permute-start(bf16[2,256,512]{1,2,0:T(8,128)(2,1)} %slice.432), channel_id=1, source_target_pairs={{0,16},{8,24},{16,0},{24,8},{1,17},{9,25},{17,1},{25,9},{2,18},{10... | collective-permute-start | bytes 1572872 | tf_op jit(solution)/shard_map/ppermute | solution.py:262
  91.7 18.3 %collective-permute-start.9 = (bf16[2,256,512]{1,2,0:T(8,128)(2,1)}, bf16[2,256,512]{1,2,0:T(8,128)(2,1)}, u32[]{:S(2)}, u32[]{:S(2)}) collective-permute-start(bf16[2,256,512]{1,2,0:T(8,128)(2,1)} %slice.431), channel_id=1, source_target_pairs={{0,8},{8,0},{16,24},{24,16},{1,9},{9,1},{17,25},{25,17},{2,10},{10... | collective-permute-start | bytes 1572872 | tf_op jit(solution)/shard_map/ppermute | solution.py:261
  95.1 10.8 %collective-permute-start.18 = (bf16[256,512]{0,1:T(8,128)(2,1)}, bf16[256,512]{0,1:T(8,128)(2,1)}, u32[]{:S(2)}, u32[]{:S(2)}) collective-permute-start(bf16[256,512]{0,1:T(8,128)(2,1)} %collective-permute-done.17), channel_id=1, source_target_pairs={{0,1},{1,2},{2,3},{3,0},{4,5},{5,6},{6,7},{7,4},{8,9},{9,10},{10,1... | collective-permute-start | bytes 786440 | tf_op jit(solution)/shard_map/ppermute | solution.py:252
  103.0 35.9 %collective-permute-start.27 = (bf16[4,256,512]{1,2,0:T(8,128)(2,1)}, bf16[4,256,512]{1,2,0:T(8,128)(2,1)}, u32[]{:S(2)}, u32[]{:S(2)}) collective-permute-start(bf16[4,256,512]{1,2,0:T(8,128)(2,1)} %pad_maximum_fusion.23), channel_id=1, source_target_pairs={{0,16},{8,24},{16,0},{24,8},{1,17},{9,25},{17,1},{25,9},{2,18},{10... | collective-permute-start | bytes 3145736 | tf_op jit(solution)/shard_map/ppermute | solution.py:260
  105.9 34.7 %collective-permute-start.26 = (bf16[4,256,512]{1,2,0:T(8,128)(2,1)}, bf16[4,256,512]{1,2,0:T(8,128)(2,1)}, u32[]{:S(2)}, u32[]{:S(2)}) collective-permute-start(bf16[4,256,512]{1,2,0:T(8,128)(2,1)} %pad_maximum_fusion.23), channel_id=1, source_target_pairs={{0,8},{8,0},{16,24},{24,16},{1,9},{9,1},{17,25},{25,17},{2,10},{10... | collective-permute-start | bytes 3145736 | tf_op jit(solution)/shard_map/ppermute | solution.py:259
  108.7 43.2 %collective-permute-start.20 = (bf16[4,256,512]{1,2,0:T(8,128)(2,1)}, bf16[4,256,512]{1,2,0:T(8,128)(2,1)}, u32[]{:S(2)}, u32[]{:S(2)}) collective-permute-start(bf16[4,256,512]{1,2,0:T(8,128)(2,1)} %pad_maximum_fusion.22), channel_id=1, source_target_pairs={{0,16},{8,24},{16,0},{24,8},{1,17},{9,25},{17,1},{25,9},{2,18},{10... | collective-permute-start | bytes 3145736 | tf_op jit(solution)/shard_map/ppermute | solution.py:260
  115.0 39.6 %collective-permute-start.19 = (bf16[4,256,512]{1,2,0:T(8,128)(2,1)}, bf16[4,256,512]{1,2,0:T(8,128)(2,1)S(1)}, u32[]{:S(2)}, u32[]{:S(2)}) collective-permute-start(bf16[4,256,512]{1,2,0:T(8,128)(2,1)} %pad_maximum_fusion.22), channel_id=1, source_target_pairs={{0,8},{8,0},{16,24},{24,16},{1,9},{9,1},{17,25},{25,17},{2,10},{10... | collective-permute-start | bytes 3145736 | tf_op jit(solution)/shard_map/ppermute | solution.py:259
  138.9 31.5 %collective-permute-start.14 = (f32[512,1024]{1,0:T(8,128)S(1)}, f32[512,1024]{1,0:T(8,128)S(1)}, u32[]{:S(2)}, u32[]{:S(2)}) collective-permute-start(f32[512,1024]{1,0:T(8,128)S(1)} %slice.440), channel_id=1, source_target_pairs={{0,4},{4,0},{1,5},{5,1},{2,6},{6,2},{3,7},{7,3},{8,12},{12,8},{9,1... | collective-permute-start | bytes 6291464 | tf_op jit(solution)/shard_map/ppermute | solution.py:139
  140.6 25.3 %collective-permute-start.28 = (bf16[2,256,512]{1,2,0:T(8,128)(2,1)S(1)}, bf16[2,256,512]{1,2,0:T(8,128)(2,1)S(1)}, u32[]{:S(2)}, u32[]{:S(2)}) collective-permute-start(bf16[2,256,512]{1,2,0:T(8,128)(2,1)S(1)} %slice.450), channel_id=1, source_target_pairs={{0,8},{8,0},{16,24},{24,16},{1,9},{9,1},{17,25},{25,17},{2,10},{10... | collective-permute-start | bytes 1572872 | tf_op jit(solution)/shard_map/ppermute | solution.py:261
  142.6 23.3 %collective-permute-start.29 = (bf16[2,256,512]{1,2,0:T(8,128)(2,1)S(1)}, bf16[2,256,512]{1,2,0:T(8,128)(2,1)S(1)}, u32[]{:S(2)}, u32[]{:S(2)}) collective-permute-start(bf16[2,256,512]{1,2,0:T(8,128)(2,1)S(1)} %slice.451), channel_id=1, source_target_pairs={{0,16},{8,24},{16,0},{24,8},{1,17},{9,25},{17,1},{25,9},{2,18},{10... | collective-permute-start | bytes 1572872 | tf_op jit(solution)/shard_map/ppermute | solution.py:262
  153.0 22.6 %collective-permute-start.21 = (bf16[2,256,512]{1,2,0:T(8,128)(2,1)S(1)}, bf16[2,256,512]{1,2,0:T(8,128)(2,1)S(1)}, u32[]{:S(2)}, u32[]{:S(2)}) collective-permute-start(bf16[2,256,512]{1,2,0:T(8,128)(2,1)S(1)} %slice.443), channel_id=1, source_target_pairs={{0,8},{8,0},{16,24},{24,16},{1,9},{9,1},{17,25},{25,17},{2,10},{10... | collective-permute-start | bytes 1572872 | tf_op jit(solution)/shard_map/ppermute | solution.py:261
  154.7 20.9 %collective-permute-start.22 = (bf16[2,256,512]{1,2,0:T(8,128)(2,1)S(1)}, bf16[2,256,512]{1,2,0:T(8,128)(2,1)S(1)}, u32[]{:S(2)}, u32[]{:S(2)}) collective-permute-start(bf16[2,256,512]{1,2,0:T(8,128)(2,1)S(1)} %slice.444), channel_id=1, source_target_pairs={{0,16},{8,24},{16,0},{24,8},{1,17},{9,25},{17,1},{25,9},{2,18},{10... | collective-permute-start | bytes 1572872 | tf_op jit(solution)/shard_map/ppermute | solution.py:262
  221.3 31.8 %collective-permute-start.30 = (f32[512,1024]{1,0:T(8,128)}, f32[512,1024]{1,0:T(8,128)}, u32[]{:S(2)}, u32[]{:S(2)}) collective-permute-start(f32[512,1024]{1,0:T(8,128)} %slice.457), channel_id=1, source_target_pairs={{0,4},{4,0},{1,5},{5,1},{2,6},{6,2},{3,7},{7,3},{8,12},{12,8},{9,1... | collective-permute-start | bytes 6291464 | tf_op jit(solution)/shard_map/ppermute | solution.py:139
  222.4 30.2 %all-to-all-start.2 = ((bf16[4,128,1024]{2,1,0:T(8,128)(2,1)}), bf16[4,128,1024]{2,1,0:T(8,128)(2,1)S(1)}, u32[]{:S(2)}, u32[]{:S(2)}) async-start(bf16[4,128,1024]{2,1,0:T(8,128)(2,1)} %pad_maximum_fusion.27), calls=%async_computation.2 | async-start | bytes 2097152 | tf_op jit(solution)/shard_map/all_to_all | solution.py:199
  262.9 103.3 %all-to-all-start.1 = ((bf16[4,128,1024]{2,1,0:T(8,128)(2,1)}), bf16[4,128,1024]{2,1,0:T(8,128)(2,1)S(1)}, u32[]{:S(2)}, u32[]{:S(2)}) async-start(bf16[4,128,1024]{2,1,0:T(8,128)(2,1)} %bitcast.323), calls=%async_computation.1 | async-start | bytes 2097152 | tf_op jit(solution)/shard_map/all_to_all | solution.py:203
  314.6 44.9 %collective-permute-start.45 = (bf16[2,256,512]{2,1,0:T(8,128)(2,1)}, bf16[2,256,512]{2,1,0:T(8,128)(2,1)}, u32[]{:S(2)}, u32[]{:S(2)}) collective-permute-start(bf16[2,256,512]{2,1,0:T(8,128)(2,1)} %get-tuple-element.104), channel_id=1, source_target_pairs={{0,16},{8,24},{16,0},{24,8},{1,17},{9,25},{17,1},{25,9},{2,18},{10... | collective-permute-start | bytes 1572872 | tf_op jit(solution)/shard_map/ppermute | solution.py:359
  315.1 44.4 %collective-permute-start.47 = (bf16[2,256,512]{2,1,0:T(8,128)(2,1)}, bf16[2,256,512]{2,1,0:T(8,128)(2,1)}, u32[]{:S(2)}, u32[]{:S(2)}) collective-permute-start(bf16[2,256,512]{2,1,0:T(8,128)(2,1)} %get-tuple-element.103), channel_id=1, source_target_pairs={{0,8},{8,0},{16,24},{24,16},{1,9},{9,1},{17,25},{25,17},{2,10},{10... | collective-permute-start | bytes 1572872 | tf_op jit(solution)/shard_map/ppermute | solution.py:358
  356.0 78.0 %collective-permute-start.34 = (f32[512,1024]{1,0:T(8,128)}, f32[512,1024]{1,0:T(8,128)}, u32[]{:S(2)}, u32[]{:S(2)}) collective-permute-start(f32[512,1024]{1,0:T(8,128)} %slice.459), channel_id=1, source_target_pairs={{0,4},{4,0},{1,5},{5,1},{2,6},{6,2},{3,7},{7,3},{8,12},{12,8},{9,1... | collective-permute-start | bytes 6291464 | tf_op jit(solution)/shard_map/ppermute | solution.py:139
  357.5 15.1 %collective-permute-start.52 = (bf16[2,256,512]{2,1,0:T(8,128)(2,1)}, bf16[2,256,512]{2,1,0:T(8,128)(2,1)}, u32[]{:S(2)}, u32[]{:S(2)}) collective-permute-start(bf16[2,256,512]{2,1,0:T(8,128)(2,1)} %get-tuple-element.108), channel_id=1, source_target_pairs={{0,16},{8,24},{16,0},{24,8},{1,17},{9,25},{17,1},{25,9},{2,18},{10... | collective-permute-start | bytes 1572872 | tf_op jit(solution)/shard_map/ppermute | solution.py:359
  357.7 15.1 %collective-permute-start.54 = (bf16[2,256,512]{2,1,0:T(8,128)(2,1)}, bf16[2,256,512]{2,1,0:T(8,128)(2,1)}, u32[]{:S(2)}, u32[]{:S(2)}) collective-permute-start(bf16[2,256,512]{2,1,0:T(8,128)(2,1)} %get-tuple-element.107), channel_id=1, source_target_pairs={{0,8},{8,0},{16,24},{24,16},{1,9},{9,1},{17,25},{25,17},{2,10},{10... | collective-permute-start | bytes 1572872 | tf_op jit(solution)/shard_map/ppermute | solution.py:358
  362.9 32.3 %collective-permute-start.46 = (bf16[4,256,512]{2,1,0:T(8,128)(2,1)}, bf16[4,256,512]{2,1,0:T(8,128)(2,1)}, u32[]{:S(2)}, u32[]{:S(2)}) collective-permute-start(bf16[4,256,512]{2,1,0:T(8,128)(2,1)} %pad_maximum_fusion.31), channel_id=1, source_target_pairs={{0,8},{8,0},{16,24},{24,16},{1,9},{9,1},{17,25},{25,17},{2,10},{10... | collective-permute-start | bytes 3145736 | tf_op jit(solution)/shard_map/ppermute | solution.py:362
  364.3 31.0 %collective-permute-start.48 = (bf16[4,256,512]{2,1,0:T(8,128)(2,1)}, bf16[4,256,512]{2,1,0:T(8,128)(2,1)}, u32[]{:S(2)}, u32[]{:S(2)}) collective-permute-start(bf16[4,256,512]{2,1,0:T(8,128)(2,1)} %pad_maximum_fusion.32), channel_id=1, source_target_pairs={{0,16},{8,24},{16,0},{24,8},{1,17},{9,25},{17,1},{25,9},{2,18},{10... | collective-permute-start | bytes 3145736 | tf_op jit(solution)/shard_map/ppermute | solution.py:363
  375.1 41.8 %collective-permute-start.53 = (bf16[4,256,512]{2,1,0:T(8,128)(2,1)S(1)}, bf16[4,256,512]{2,1,0:T(8,128)(2,1)S(1)}, u32[]{:S(2)}, u32[]{:S(2)}) collective-permute-start(bf16[4,256,512]{2,1,0:T(8,128)(2,1)S(1)} %pad_maximum_fusion.33), channel_id=1, source_target_pairs={{0,8},{8,0},{16,24},{24,16},{1,9},{9,1},{17,25},{25,17},{2,10},{10... | collective-permute-start | bytes 3145736 | tf_op jit(solution)/shard_map/ppermute | solution.py:362
  377.1 39.8 %collective-permute-start.55 = (bf16[4,256,512]{2,1,0:T(8,128)(2,1)S(1)}, bf16[4,256,512]{2,1,0:T(8,128)(2,1)S(1)}, u32[]{:S(2)}, u32[]{:S(2)}) collective-permute-start(bf16[4,256,512]{2,1,0:T(8,128)(2,1)S(1)} %pad_maximum_fusion.34), channel_id=1, source_target_pairs={{0,16},{8,24},{16,0},{24,8},{1,17},{9,25},{17,1},{25,9},{2,18},{10... | collective-permute-start | bytes 3145736 | tf_op jit(solution)/shard_map/ppermute | solution.py:363
  397.9 26.0 %collective-permute-start.49 = (bf16[256,512]{1,0:T(8,128)(2,1)S(1)}, bf16[256,512]{1,0:T(8,128)(2,1)S(1)}, u32[]{:S(2)}, u32[]{:S(2)}) collective-permute-start(bf16[256,512]{1,0:T(8,128)(2,1)S(1)} %fusion.85), channel_id=1, source_target_pairs={{1,0},{2,1},{3,2},{0,3},{5,4},{6,5},{7,6},{4,7},{9,8},{10,9},{11,1... | collective-permute-start | bytes 786440 | tf_op jit(solution)/shard_map/ppermute | solution.py:373
  424.1 15.1 %collective-permute-start.50 = (bf16[256,512]{1,0:T(8,128)(2,1)S(1)}, bf16[256,512]{1,0:T(8,128)(2,1)S(1)}, u32[]{:S(2)}, u32[]{:S(2)}) collective-permute-start(bf16[256,512]{1,0:T(8,128)(2,1)S(1)} %fusion.61), channel_id=1, source_target_pairs={{1,0},{2,1},{3,2},{0,3},{5,4},{6,5},{7,6},{4,7},{9,8},{10,9},{11,1... | collective-permute-start | bytes 786440 | tf_op jit(solution)/shard_map/ppermute | solution.py:373
  440.4 65.5 %collective-permute-start.58 = (bf16[256,512]{1,0:T(8,128)(2,1)}, bf16[256,512]{1,0:T(8,128)(2,1)}, u32[]{:S(2)}, u32[]{:S(2)}) collective-permute-start(bf16[256,512]{1,0:T(8,128)(2,1)} %fusion.58), channel_id=1, source_target_pairs={{1,0},{2,1},{3,2},{0,3},{5,4},{6,5},{7,6},{4,7},{9,8},{10,9},{11,1... | collective-permute-start | bytes 786440 | tf_op jit(solution)/shard_map/ppermute | solution.py:373
  503.9 13.3 %collective-permute-start.38 = (bf16[2,256,512]{2,1,0:T(8,128)(2,1)}, bf16[2,256,512]{2,1,0:T(8,128)(2,1)S(1)}, u32[]{:S(2)}, u32[]{:S(2)}) collective-permute-start(bf16[2,256,512]{2,1,0:T(8,128)(2,1)} %get-tuple-element.100), channel_id=1, source_target_pairs={{0,16},{8,24},{16,0},{24,8},{1,17},{9,25},{17,1},{25,9},{2,18},{10... | collective-permute-start | bytes 1572872 | tf_op jit(solution)/shard_map/ppermute | solution.py:359
  505.5 13.0 %collective-permute-start.40 = (bf16[2,256,512]{2,1,0:T(8,128)(2,1)S(1)}, bf16[2,256,512]{2,1,0:T(8,128)(2,1)}, u32[]{:S(2)}, u32[]{:S(2)}) collective-permute-start(bf16[2,256,512]{2,1,0:T(8,128)(2,1)S(1)} %get-tuple-element.99), channel_id=1, source_target_pairs={{0,8},{8,0},{16,24},{24,16},{1,9},{9,1},{17,25},{25,17},{2,10},{10... | collective-permute-start | bytes 1572872 | tf_op jit(solution)/shard_map/ppermute | solution.py:358
  521.2 23.5 %collective-permute-start.39 = (bf16[4,256,512]{2,1,0:T(8,128)(2,1)}, bf16[4,256,512]{2,1,0:T(8,128)(2,1)}, u32[]{:S(2)}, u32[]{:S(2)}) collective-permute-start(bf16[4,256,512]{2,1,0:T(8,128)(2,1)} %pad_maximum_fusion.29), channel_id=1, source_target_pairs={{0,8},{8,0},{16,24},{24,16},{1,9},{9,1},{17,25},{25,17},{2,10},{10... | collective-permute-start | bytes 3145736 | tf_op jit(solution)/shard_map/ppermute | solution.py:362
  523.4 23.6 %collective-permute-start.41 = (bf16[4,256,512]{2,1,0:T(8,128)(2,1)}, bf16[4,256,512]{2,1,0:T(8,128)(2,1)}, u32[]{:S(2)}, u32[]{:S(2)}) collective-permute-start(bf16[4,256,512]{2,1,0:T(8,128)(2,1)} %pad_maximum_fusion.30), channel_id=1, source_target_pairs={{0,16},{8,24},{16,0},{24,8},{1,17},{9,25},{17,1},{25,9},{2,18},{10... | collective-permute-start | bytes 3145736 | tf_op jit(solution)/shard_map/ppermute | solution.py:363
  531.4 38.4 %collective-permute-start.36 = (f32[512,1024]{1,0:T(8,128)}, f32[512,1024]{1,0:T(8,128)}, u32[]{:S(2)}, u32[]{:S(2)}) collective-permute-start(f32[512,1024]{1,0:T(8,128)} %slice.461), channel_id=1, source_target_pairs={{0,4},{4,0},{1,5},{5,1},{2,6},{6,2},{3,7},{7,3},{8,12},{12,8},{9,1... | collective-permute-start | bytes 6291464 | tf_op jit(solution)/shard_map/ppermute | solution.py:139
  565.7 11.3 %collective-permute-start.44 = (bf16[256,512]{1,0:T(8,128)(2,1)}, bf16[256,512]{1,0:T(8,128)(2,1)S(1)}, u32[]{:S(2)}, u32[]{:S(2)}) collective-permute-start(bf16[256,512]{1,0:T(8,128)(2,1)} %fusion.68), channel_id=1, source_target_pairs={{1,0},{2,1},{3,2},{0,3},{5,4},{6,5},{7,6},{4,7},{9,8},{10,9},{11,1... | collective-permute-start | bytes 786440 | tf_op jit(solution)/shard_map/ppermute | solution.py:373
  573.5 52.1 %all-to-all-start.3 = ((bf16[4,128,1024]{2,1,0:T(8,128)(2,1)}), bf16[4,128,1024]{2,1,0:T(8,128)(2,1)S(1)}, u32[]{:S(2)}, u32[]{:S(2)}) async-start(bf16[4,128,1024]{2,1,0:T(8,128)(2,1)} %bitcast.52), calls=%async_computation.3 | async-start | bytes 2097152 | tf_op jit(solution)/shard_map/all_to_all | solution.py:203
  579.6 42.3 %collective-permute-start.59 = (f32[128,1536]{0,1:T(8,128)}, f32[128,1536]{0,1:T(8,128)S(1)}, u32[]{:S(2)}, u32[]{:S(2)}) collective-permute-start(f32[128,1536]{0,1:T(8,128)} %bitcast.338), channel_id=1, source_target_pairs={{0,4},{4,0},{1,5},{5,1},{2,6},{6,2},{3,7},{7,3},{8,12},{12,8},{9,1... | collective-permute-start | bytes 2359304 | tf_op jit(solution)/shard_map/ppermute | solution.py:139
  (114 other events, 1454.8 us)

commit v2 on v1

--- a/solution.py
+++ b/solution.py
@@ -133,6 +133,546 @@
         ),
         name="attend_bwd",
     )(qkv, grad_context, lse, key_bias)
+
+POLY = (
+    0.30995978221815235,
+    0.31100346478903146,
+    0.2699660979585953,
+    0.2765467936611628,
+    -0.03831584737802812,
+    0.38967711658103854,
+    -0.3554874111653827,
+    0.08996434684501212,
+)
+POLY_AT = 0.31
+DENSITY = 0.3989422804014327
+MESH = pl.DeviceIdType.MESH
+
+
+def gelu_and_slope(v):
+    density = jnp.exp(-0.5 * v * v) * DENSITY
+    t = 1.0 / (1.0 + POLY_AT * jnp.abs(v))
+    tail = jnp.full_like(v, POLY[-1])
+    for coefficient in POLY[-2::-1]:
+        tail = tail * t + coefficient
+    tail = tail * t * density
+    below = jnp.where(v > 0, 1.0 - tail, tail)
+    return v * below, below + v * density
+
+
+def forward_kernel(
+    length_ref, xp_ref, cp_ref, keep_ref, give_ref, bias_in_ref, vec_ref,
+    w_out, xf_out, qkv_out, lse_ref, ctx_out, ff_out, hid_out, dg_out, n1_out, inv1_ref, gm_ref,
+    lo_ref, sums_ref,
+    w, xf, bias, qkv, ctx, ff, hid, dg, n1, first, other_part, own_part, att_got, mix_got, cot, lo_own,
+    z_s, z_r, x_s, x_r, y_s, y_r, f_s, f_r, pre_l, pre_s, pre_r, b_s, b_r,
+    xa_s, xa_r, ca_s, ca_r, la_s, la_r, e_s, e_r, o_s,
+):
+    plane = lax.axis_index("plane")
+    core = lax.axis_index("core")
+    place = lax.axis_index("tensor")
+    partner = {"core": 1 - core}
+    x_side = {"plane": plane + 1 - 2 * (plane % 2)}
+    y_side = {"plane": (plane + 2) % 4}
+    z_next = {"tensor": (place + 1) % 4}
+    rows = xf.shape[0]
+    own = rows // 2
+    part = own // 4
+    piece = w.shape[2] // 4
+
+    def remote(source, target, send, recv, to):
+        return pltpu.make_async_remote_copy(
+            source, target, send, recv, device_id=to, device_id_type=MESH
+        )
+
+    def z_copy(b, s):
+        return remote(
+            w.at[b, s, 0:piece], w.at[b, s + 1, 0:piece], z_s.at[b, s], z_r.at[b, s], z_next
+        )
+
+    def x_copy(b, j):
+        return remote(
+            w.at[b, j, 0:piece], w.at[b, j, piece : 2 * piece], x_s.at[b, j], x_r.at[b, j], x_side
+        )
+
+    def y_copy(b, j):
+        return remote(
+            w.at[b, j, 0:piece], w.at[b, j, 2 * piece : 3 * piece], y_s.at[b, j], y_r.at[b, j], y_side
+        )
+
+    def f_copy(b, j):
+        start = 2 * piece if j < 2 else piece
+        return remote(
+            w.at[b, j, start : start + piece],
+            w.at[b, j, 3 * piece : 4 * piece],
+            f_s.at[b, j],
+            f_r.at[b, j],
+            x_side if j < 2 else y_side,
+        )
+
+    def pre_copy(b):
+        rows_at = pl.ds(core * (piece // 2), piece // 2)
+        return remote(give_ref.at[b], w.at[b, 0, rows_at], pre_s.at[b], pre_r.at[b], partner)
+
+    def pre_got(b):
+        rows_at = pl.ds((1 - core) * (piece // 2), piece // 2)
+        return remote(give_ref.at[b], w.at[b, 0, rows_at], pre_s.at[b], pre_r.at[b], partner)
+
+    def keep_copy(b):
+        rows_at = pl.ds(core * (piece // 2), piece // 2)
+        return pltpu.make_async_copy(keep_ref.at[b], w.at[b, 0, rows_at], pre_l.at[b])
+
+    def bias_copy(s):
+        return remote(
+            bias.at[0], bias.at[s], b_s.at[s], b_r.at[s], {"tensor": (place + s) % 4}
+        )
+
+    def spread(source, target, send, recv, l, h):
+        at = pl.ds(place * part, part)
+        to = {"core": h, "tensor": 2 * core + l}
+        return remote(
+            source.at[2 * l + h], target.at[at], send.at[2 * l + h], recv.at[place], to
+        )
+
+    def spread_local(source, target, recv, l, h):
+        at = pl.ds(place * part, part)
+        return pltpu.make_async_copy(source.at[2 * l + h], target.at[at], recv.at[place])
+
+    def is_here(l, h):
+        return jnp.logical_and(core == h, place == 2 * core + l)
+
+    def spread_start(source, target, send, recv):
+        for l in range(2):
+            for h in range(2):
+                @pl.when(is_here(l, h))
+                def _():
+                    spread_local(source, target, recv, l, h).start()
+
+                @pl.when(jnp.logical_not(is_here(l, h)))
+                def _():
+                    spread(source, target, send, recv, l, h).start()
+
+    def spread_wait(source, target, recv):
+        for s in range(4):
+            pltpu.make_async_copy(
+                source.at[s], target.at[s * part : (s + 1) * part], recv.at[s]
+            ).wait()
+
+    def spread_sent(source, target, send, recv):
+        for l in range(2):
+            for h in range(2):
+                @pl.when(jnp.logical_not(is_here(l, h)))
+                def _():
+                    spread(source, target, send, recv, l, h).wait_send()
+
+    def home(s):
+        to = {"core": place // 2, "tensor": s}
+        return remote(
+            lo_own.at[s * part : (s + 1) * part],
+            lo_ref.at[2 * (place % 2) + core],
+            la_s.at[s],
+            la_r.at[2 * (place % 2) + core],
+            to,
+        )
+
+    def home_local(s):
+        return pltpu.make_async_copy(
+            lo_own.at[s * part : (s + 1) * part],
+            lo_ref.at[2 * (place % 2) + core],
+            la_r.at[2 * (place % 2) + core],
+        )
+
+    def is_home(s):
+        return jnp.logical_and(core == place // 2, place == s)
+
+    def exchange(source, target, n):
+        return remote(source, target, e_s.at[n], e_r.at[n], partner)
+
+    outs = []
+
+    def save(source, target):
+        copy = pltpu.make_async_copy(source, target, o_s.at[len(outs)])
+        copy.start()
+        outs.append(copy)
+
+    barrier = pltpu.get_barrier_semaphore()
+    friends = [x_side, y_side, partner]
+    for s in range(1, 4):
+        friends.append({"tensor": (place + s) % 4})
+        friends.append({"tensor": (place + s) % 4, "core": 1 - core})
+    for friend in friends:
+        pl.semaphore_signal(barrier, inc=1, device_id=friend, device_id_type=MESH)
+    keep_all = [keep_copy(b) for b in range(3)]
+    for copy in keep_all:
+        copy.start()
+    pl.semaphore_wait(barrier, len(friends))
+
+    for b in range(3):
+        pre_copy(b).start()
+    bias[0] = bias_in_ref[...]
+    spread_start(xp_ref, xf, xa_s, xa_r)
+    keep_all[0].wait()
+    pre_got(0).wait_recv()
+    z_copy(0, 0).start()
+    x_copy(0, 0).start()
+    y_copy(0, 0).start()
+    for s in range(1, 4):
+        bias_copy(s).start()
+    for b in (1, 2):
+        keep_all[b].wait()
+        pre_got(b).wait_recv()
+        x_copy(b, 0).start()
+        y_copy(b, 0).start()
+    z_copy(0, 0).wait_recv()
+    z_copy(0, 1).start()
+    x_copy(0, 1).start()
+    y_copy(0, 1).start()
+    y_copy(0, 0).wait_recv()
+    f_copy(0, 0).start()
+    z_copy(0, 1).wait_recv()
+    z_copy(0, 2).start()
+    x_copy(0, 2).start()
+    y_copy(0, 2).start()
+    z_copy(0, 2).wait_recv()
+    z_copy(1, 0).start()
+    z_copy(2, 0).start()
+    x_copy(0, 3).start()
+    y_copy(0, 3).start()
+
+    spread_wait(xp_ref, xf, xa_r)
+    share_x = exchange(xf.at[0:own], xf.at[own : 2 * own], 0)
+    share_x.start()
+    y_copy(0, 1).wait_recv()
+    f_copy(0, 1).start()
+    y_copy(1, 0).wait_recv()
+    f_copy(1, 0).start()
+    y_copy(2, 0).wait_recv()
+    f_copy(2, 0).start()
+    for s in range(1, 4):
+        bias_copy(s).wait_recv()
+    share_x.wait_recv()
+    save(xf, xf_out)
+
+    index = lax.broadcasted_iota(jnp.int32, (rows, 1), 0)
+    length = length_ref[0]
+    half = jnp.where(index < own, core, 1 - core)
+    inside = index % own
+    position = (inside // part) * (2 * part) + half * part + inside % part
+    key_bias = jnp.where(position < length, 0.0, NEGATIVE).astype(f32)
+    lane = lax.broadcasted_iota(jnp.int32, (1, 2 * HD), 1)
+    head_cols = 2 * HD
+    tile = 256
+
+    def project(j):
+        columns = lax.broadcasted_iota(jnp.int32, (1, 3 * head_cols), 1)
+        zero = jnp.zeros((1, head_cols), f32)
+        add = jnp.concatenate(
+            [bias[j, 0:1, 0:head_cols], zero, bias[j, 0:1, head_cols : 2 * head_cols]], axis=1
+        )
+        times = jnp.where(columns < head_cols, HD ** (-0.5), 1.0).astype(f32)
+
+        def body(i, _):
+            at = pl.ds(pl.multiple_of(i * tile, tile), tile)
+            value = nn(xf[at, :], w[0, j, :, 0 : 3 * head_cols])
+            qkv[j, at, :] = ((value + add) * times).astype(bf16)
+            return 0
+
+        lax.fori_loop(0, rows // tile, body, 0)
+        save(qkv.at[j], qkv_out.at[j])
+
+    def attend(j):
+        keys = qkv[j, :, head_cols : 2 * head_cols]
+        values_t = qkv[j, :, 2 * head_cols : 3 * head_cols].T
+
+        def body(i, _):
+            at = pl.ds(pl.multiple_of(i * tile, tile), tile)
+            query = qkv[j, at, 0:head_cols]
+            parts = []
+            for h in range(2):
+                query_h = jnp.where(lane // HD == h, query, jnp.zeros_like(query))
+                scores = nt(keys, query_h) + key_bias
+                largest = jnp.max(scores, axis=0, keepdims=True)
+                weights = jnp.exp(scores - largest)
+                total = jnp.sum(weights, axis=0, keepdims=True)
+                out = nn(values_t[h * HD : (h + 1) * HD], weights.astype(bf16))
+                parts.append(out / total)
+                lse_ref[2 * j + h, :, at] = largest + jnp.log(total)
+            ctx[j, at, :] = jnp.concatenate(parts, axis=0).T.astype(bf16)
+            return 0
+
+        lax.fori_loop(0, rows // tile, body, 0)
+        save(ctx.at[j], ctx_out.at[j])
+
+    def ready(b, j):
+        x_copy(b, j).wait_recv() if not (b, j, "x") in seen else None
+        seen.add((b, j, "x"))
+        y_copy(b, j).wait_recv() if not (b, j, "y") in seen else None
+        seen.add((b, j, "y"))
+        f_copy(b, j).wait_recv()
+        save(w.at[b, j], w_out.at[b, j])
+
+    seen = {(0, 0, "y"), (0, 1, "y"), (1, 0, "y"), (2, 0, "y")}
+
+    def forward_on(b, j):
+        side = "y" if j < 2 else "x"
+        (y_copy if j < 2 else x_copy)(b, j).wait_recv()
+        seen.add((b, j, side))
+        f_copy(b, j).start()
+
+    ready(0, 0)
+    project(0)
+    attend(0)
+    forward_on(0, 2)
+    z_copy(1, 0).wait_recv()
+    z_copy(1, 1).start()
+    x_copy(1, 1).start()
+    y_copy(1, 1).start()
+    forward_on(0, 3)
+    z_copy(2, 0).wait_recv()
+    z_copy(2, 1).start()
+    ready(0, 1)
+    project(1)
+    attend(1)
+    z_copy(1, 1).wait_recv()
+    z_copy(1, 2).start()
+    x_copy(1, 2).start()
+    y_copy(1, 2).start()
+    ready(0, 2)
+    project(2)
+    attend(2)
+    z_copy(2, 1).wait_recv()
+    z_copy(2, 2).start()
+    forward_on(1, 1)
+    ready(0, 3)
+    project(3)
+    attend(3)
+    z_copy(1, 2).wait_recv()
+    x_copy(1, 3).start()
+    y_copy(1, 3).start()
+    forward_on(1, 2)
+
+    def out_rows(start, target):
+        def body(i, _):
+            at = pl.ds(pl.multiple_of(start + i * tile, tile), tile)
+            to = pl.ds(pl.multiple_of(i * tile, tile), tile)
+            total = nt(ctx[0, at, :], w[0, 0, :, 3 * head_cols :])
+            for j in range(1, 4):
+                total += nt(ctx[j, at, :], w[0, j, :, 3 * head_cols :])
+            target[to, :] = total
+            return 0
+
+        lax.fori_loop(0, own // tile, body, 0)
+
+    out_rows(own, other_part)
+    share_att = exchange(other_part, att_got, 1)
+    share_att.start()
+    out_rows(0, own_part)
+    x_copy(2, 1).start()
+    y_copy(2, 1).start()
+    spread_start(cp_ref, cot, ca_s, ca_r)
+    share_att.wait_recv()
+    small = 32
+
+    def mean(value):
+        return jnp.sum(value, axis=-1, keepdims=True) * (1.0 / value.shape[-1])
+
+    def first_body(i, _):
+        at = pl.ds(pl.multiple_of(i * small, small), small)
+        total = xf[at, :].astype(f32) + (own_part[at, :] + att_got[at, :]) + vec_ref[0:1, :]
+        centered = total - mean(total)
+        inverse = lax.rsqrt(mean(centered * centered) + EPSILON)
+        normed = centered * inverse
+        n1[at, :] = normed
+        inv1_ref[at, :] = inverse
+        value = normed * vec_ref[1:2, :] + vec_ref[2:3, :]
+        first[at, :] = value
+        ff[at, :] = value.astype(bf16)
+        return 0
+
+    lax.fori_loop(0, own // small, first_body, 0)
+    share_first = exchange(ff.at[0:own], ff.at[own : 2 * own], 2)
+    share_first.start()
+    save(n1, n1_out)
+    forward_on(1, 3)
+    z_copy(2, 2).wait_recv()
+    for j in (2, 3):
+        x_copy(2, j).start()
+        y_copy(2, j).start()
+    share_first.wait_recv()
+    save(ff, ff_out)
+
+    def expand(j):
+        add = bias[j, 0:1, 2 * head_cols :]
+
+        def body(i, _):
+            at = pl.ds(pl.multiple_of(i * tile, tile), tile)
+            value = nn(ff[at, :], w[1, j]) + add
+            active, slope = gelu_and_slope(value)
+            hid[j, at, :] = active.astype(bf16)
+            dg[j, at, :] = slope.astype(bf16)
+            return 0
+
+        lax.fori_loop(0, rows // tile, body, 0)
+        save(hid.at[j], hid_out.at[j])
+        save(dg.at[j], dg_out.at[j])
+
+    ready(1, 0)
+    expand(0)
+    ready(1, 1)
+    expand(1)
+    forward_on(2, 1)
+    ready(1, 2)
+    expand(2)
+    forward_on(2, 2)
+    ready(1, 3)
+    expand(3)
+    share_att.wait_send()
+
+    def contract(js, start, target, fresh):
+        def body(i, _):
+            at = pl.ds(pl.multiple_of(start + i * tile, tile), tile)
+            to = pl.ds(pl.multiple_of(i * tile, tile), tile)
+            total = nt(hid[js[0], at, :], w[2, js[0]])
+            for j in js[1:]:
+                total += nt(hid[j, at, :], w[2, j])
+            target[to, :] = total if fresh else target[to, :] + total
+            return 0
+
+        lax.fori_loop(0, own // tile, body, 0)
+
+    ready(2, 0)
+    ready(2, 1)
+    contract((0, 1), own, other_part, True)
+    contract((0, 1), 0, own_part, True)
+    forward_on(2, 3)
+    ready(2, 2)
+    contract((2,), own, other_part, False)
+    contract((2,), 0, own_part, False)
+    ready(2, 3)
+    contract((3,), own, other_part, False)
+    share_mix = exchange(other_part, mix_got, 3)
+    share_mix.start()
+    contract((3,), 0, own_part, False)
+    spread_wait(cp_ref, cot, ca_r)
+    share_mix.wait_recv()
+    sums_ref[...] = jnp.zeros_like(sums_ref)
+
+    def second_body(i, _):
+        at = pl.ds(pl.multiple_of(i * small, small), small)
+        spot = i * small + lax.broadcasted_iota(jnp.int32, (small, 1), 0)
+        where = (spot // part) * (2 * part) + core * part + spot % part
+        alive = where < length
+        total = first[at, :] + (own_part[at, :] + mix_got[at, :]) + vec_ref[3:4, :]
+        centered = total - mean(total)
+        inverse = lax.rsqrt(mean(centered * centered) + EPSILON)
+        normed = centered * inverse
+        value = normed * vec_ref[4:5, :] + vec_ref[5:6, :]
+        lo_own[at, :] = jnp.where(alive, value, 0.0).astype(bf16)
+        grad = jnp.where(alive, cot[at, :].astype(f32), 0.0)
+        e = grad * vec_ref[4:5, :]
+        back = (e - mean(e) - normed * mean(e * normed)) * inverse
+        gm_ref[at, :] = back
+        sums_ref[0:1, :] += jnp.sum(back, axis=0, keepdims=True)
+        sums_ref[1:2, :] += jnp.sum(grad * normed, axis=0, keepdims=True)
+        sums_ref[2:3, :] += jnp.sum(grad, axis=0, keepdims=True)
+        return 0
+
+    lax.fori_loop(0, own // small, second_body, 0)
+    for s in range(4):
+        @pl.when(is_home(s))
+        def _():
+            home_local(s).start()
+
+        @pl.when(jnp.logical_not(is_home(s)))
+        def _():
+            home(s).start()
+
+    for b in range(3):
+        pre_copy(b).wait_send()
+        for s in range(3):
+            z_copy(b, s).wait_send()
+        for j in range(4):
+            x_copy(b, j).wait_send()
+            y_copy(b, j).wait_send()
+            f_copy(b, j).wait_send()
+    for s in range(1, 4):
+        bias_copy(s).wait_send()
+    spread_sent(xp_ref, xf, xa_s, xa_r)
+    spread_sent(cp_ref, cot, ca_s, ca_r)
+    share_x.wait_send()
+    share_first.wait_send()
+    share_mix.wait_send()
+    for copy in outs:
+        copy.wait()
+    for s in range(4):
+        @pl.when(jnp.logical_not(is_home(s)))
+        def _():
+            home(s).wait_send()
+    for s in range(4):
+        pltpu.make_async_copy(lo_own.at[0:part], lo_ref.at[s], la_r.at[s]).wait()
+
+
+def forward(length, xp, cp, keep, give, bias, vec):
+    part, width = xp.shape[1:]
+    own = 4 * part
+    rows = 2 * own
+    cols = keep.shape[2]
+    head_cols = 2 * HD
+    any_ = pl.BlockSpec(memory_space=pltpu.HBM)
+    vm = pl.BlockSpec(memory_space=pltpu.VMEM)
+    sm = pl.BlockSpec(memory_space=pltpu.SMEM)
+    shape = jax.ShapeDtypeStruct
+    dma = pltpu.SemaphoreType.DMA
+    flops = 2 * rows * width * cols * 12 + 16 * rows * rows * HD * 4
+    return pl.pallas_call(
+        forward_kernel,
+        in_specs=[sm, any_, any_, any_, any_, vm, vm],
+        out_specs=[any_, any_, any_, vm, any_, any_, any_, any_, any_, vm, vm, any_, vm],
+        out_shape=[
+            shape((3, 4, width, cols), bf16),
+            shape((rows, width), bf16),
+            shape((4, rows, 3 * head_cols), bf16),
+            shape((8, 1, rows), f32),
+            shape((4, rows, head_cols), bf16),
+            shape((rows, width), bf16),
+            shape((4, rows, cols), bf16),
+            shape((4, rows, cols), bf16),
+            shape((own, width), f32),
+            shape((own, 1), f32),
+            shape((own, width), f32),
+            shape((4, part, width), bf16),
+            shape((8, width), f32),
+        ],
+        scratch_shapes=[
+            pltpu.VMEM((3, 4, width, cols), bf16),
+            pltpu.VMEM((rows, width), bf16),
+            pltpu.VMEM((4, 8, bias.shape[1]), f32),
+            pltpu.VMEM((4, rows, 3 * head_cols), bf16),
+            pltpu.VMEM((4, rows, head_cols), bf16),
+            pltpu.VMEM((rows, width), bf16),
+            pltpu.VMEM((4, rows, cols), bf16),
+            pltpu.VMEM((4, rows, cols), bf16),
+            pltpu.VMEM((own, width), f32),
+            pltpu.VMEM((own, width), f32),
+            pltpu.VMEM((own, width), f32),
+            pltpu.VMEM((own, width), f32),
+            pltpu.VMEM((own, width), f32),
+            pltpu.VMEM((own, width), f32),
+            pltpu.VMEM((own, width), bf16),
+            pltpu.VMEM((own, width), bf16),
+            dma((3, 3)), dma((3, 3)), dma((3, 4)), dma((3, 4)), dma((3, 4)), dma((3, 4)),
+            dma((3, 4)), dma((3, 4)), dma((3,)), dma((3,)), dma((3,)), dma((4,)), dma((4,)),
+            dma((4,)), dma((4,)), dma((4,)), dma((4,)), dma((4,)), dma((4,)),
+            dma((4,)), dma((4,)), dma((32,)),
+        ],
+        compiler_params=pltpu.CompilerParams(
+            collective_id=0, has_side_effects=True, vmem_limit_bytes=60 << 20
+        ),
+        cost_estimate=pl.CostEstimate(
+            flops=flops, bytes_accessed=60 << 20, transcendentals=8 * rows * rows
+        ),
+        name="forward_layer",
+    )(length, xp, cp, keep, give, bias, vec)
 
 
 def swap_cores(value):
@@ -210,7 +750,6 @@
         )
         return reorder(value.reshape(seqs, slots_here, width), 2)
 
-    own_x = to_chip(inputs)
     their_lengths = swap_cores(lengths)
     all_lengths = by_core(lengths, their_lengths)
     length = lax.dynamic_index_in_dim(all_lengths, place, 0, keepdims=False)
@@ -240,31 +779,17 @@
     ]
     keep = jnp.concatenate([piece[0] for piece in pieces], axis=1)
     give = jnp.concatenate([piece[1] for piece in pieces], axis=1)
-    packed = by_core(keep, swap_cores(give))
     cuts = (4 * head_cols, 4 * head_cols + ff_cols)
-    bundle_a = packed[:, : cuts[0]]
-    bundle_b = packed[:, cuts[0] : cuts[1]]
-    bundle_c = packed[:, cuts[1] :]
-
-    def gather_z(own_piece):
-        got = [own_piece]
-        for _ in range(n_t - 1):
-            got.append(lax.ppermute(got[-1], "tensor", ring))
-        return jnp.stack(got)
-
-    def gather_planes(mine):
-        if not quad:
-            return lax.all_gather(mine, "plane", axis=1, tiled=True)
-        half = n_t // 2
-        from_x = lax.ppermute(mine, "plane", x_pairs)
-        from_y = lax.ppermute(mine, "plane", y_pairs)
-        low = lax.ppermute(from_y[:half], "plane", x_pairs)
-        high = lax.ppermute(from_x[half:], "plane", y_pairs)
-        return jnp.concatenate([mine, from_x, from_y, jnp.concatenate([low, high])], axis=1)
 
     def flat(gathered):
         return jnp.concatenate([gathered[j] for j in range(n_t)], axis=1)
 
+    out_bias = reorder(b_out, 0).astype(f32)
+    back_bias = reorder(b_back, 0).astype(f32)
+    gain_first = reorder(gain_one, 0).astype(f32)
+    shift_first = reorder(shift_one, 0).astype(f32)
+    gain_second = reorder(gain_two, 0).astype(f32)
+    shift_second = reorder(shift_two, 0).astype(f32)
     bias_row = jnp.concatenate(
         [
             lax.dynamic_slice_in_dim(b_query, core * head_cols, head_cols),
@@ -272,29 +797,9 @@
             lax.dynamic_slice_in_dim(b_in, core * ff_cols, ff_cols),
         ]
     )[None]
-    biases = gather_z(bias_row)[:, 0].astype(f32)
-    z_a = gather_z(bundle_a)
-    full_a = gather_planes(z_a)
-    w_qkv = flat(full_a[:, :, : 3 * head_cols])
-    w_o = flat(full_a[:, :, 3 * head_cols :])
-    w_1 = flat(gather_planes(gather_z(bundle_b)))
-    w_2 = flat(gather_planes(gather_z(bundle_c)))
-
-    zeros_k = jnp.zeros((n_t, head_cols), f32)
-    qkv_bias = jnp.concatenate(
-        [biases[:, :head_cols], zeros_k, biases[:, head_cols : 2 * head_cols]], axis=1
-    ).reshape(1, -1)
     qkv_scale = jnp.tile(
         jnp.concatenate([jnp.full((head_cols,), scale, f32), jnp.ones((2 * head_cols,), f32)]), n_t
     )[None]
-    in_bias = biases[:, 2 * head_cols :].reshape(1, -1)
-    out_bias = reorder(b_out, 0).astype(f32)
-    back_bias = reorder(b_back, 0).astype(f32)
-    gain_first = reorder(gain_one, 0).astype(f32)
-    shift_first = reorder(shift_one, 0).astype(f32)
-    gain_second = reorder(gain_two, 0).astype(f32)
-    shift_second = reorder(shift_two, 0).astype(f32)
-
     def both_rows(value):
         return jnp.concatenate([value, swap_cores(value)], axis=0)
 
@@ -316,27 +821,89 @@
             - normed * jnp.mean(e * normed, axis=-1, keepdims=True)
         ) * inverse
 
-    x_full = both_rows(own_x)
-    qkv = ((nn(x_full, w_qkv) + qkv_bias) * qkv_scale).astype(bf16)
-    context, lse = attend_fwd(qkv, key_bias)
-    attended = own_sum(nt(context, w_o))
-    normed_one, inverse_one = normalize(own_x.astype(f32) + attended + out_bias)
-    first_norm = normed_one * gain_first + shift_first
-    first_full = both_rows(first_norm.astype(bf16))
-    pre_act = nn(first_full, w_1) + in_bias
-    activated, gelu_back = jax.vjp(lambda v: jax.nn.gelu(v, approximate=False), pre_act)
-    hidden = activated.astype(bf16)
-    mixed = own_sum(nt(hidden, w_2))
-    normed_two, inverse_two = normalize(first_norm + mixed + back_bias)
-    second = normed_two * gain_second + shift_second
-    layer_out = from_chip(jnp.where(own_valid, second, 0.0).astype(bf16))
-
-    grad_second = jnp.where(own_valid, to_chip(cotangent).astype(f32), 0.0)
-    grad_mixed = normalize_back(grad_second, gain_second, normed_two, inverse_two)
+    if quad:
+        def blocks_of(value):
+            return reorder(value, 2).reshape(4, half_slots, width)
+
+        pack = lambda value: jnp.stack(
+            [value[:, : cuts[0]], value[:, cuts[0] : cuts[1]], value[:, cuts[1] :]]
+        )
+        vec = jnp.stack(
+            [out_bias, gain_first, shift_first, back_bias, gain_second, shift_second,
+             out_bias, out_bias]
+        )
+        (w_all, x_full, qkv4, lse8, ctx4, first_full, hid4, dg4, normed_one, inverse_one,
+         grad_mixed, lo_blocks, second_sums) = forward(
+            length.reshape(1), blocks_of(inputs), blocks_of(cotangent), pack(keep), pack(give),
+            jnp.broadcast_to(bias_row.astype(f32), (8, bias_row.shape[1])), vec,
+        )
+        layer_out = reorder(lo_blocks.reshape(seqs, slots_here, width), 2)
+        w_qkv = flat(w_all[0][:, :, : 3 * head_cols])
+        w_o = flat(w_all[0][:, :, 3 * head_cols :])
+        w_1 = flat(w_all[1])
+        w_2 = flat(w_all[2])
+        qkv = flat(qkv4)
+        lse = lse8.reshape(n_t, 2, slots)
+        context = flat(ctx4)
+        hidden = flat(hid4)
+        slope = flat(dg4)
+    else:
+        packed = by_core(keep, swap_cores(give))
+        bundle_a = packed[:, : cuts[0]]
+        bundle_b = packed[:, cuts[0] : cuts[1]]
+        bundle_c = packed[:, cuts[1] :]
+        def gather_z(own_piece):
+            got = [own_piece]
+            for _ in range(n_t - 1):
+                got.append(lax.ppermute(got[-1], "tensor", ring))
+            return jnp.stack(got)
+
+        def gather_planes(mine):
+            if not quad:
+                return lax.all_gather(mine, "plane", axis=1, tiled=True)
+            half = n_t // 2
+            from_x = lax.ppermute(mine, "plane", x_pairs)
+            from_y = lax.ppermute(mine, "plane", y_pairs)
+            low = lax.ppermute(from_y[:half], "plane", x_pairs)
+            high = lax.ppermute(from_x[half:], "plane", y_pairs)
+            return jnp.concatenate([mine, from_x, from_y, jnp.concatenate([low, high])], axis=1)
+
+        biases = gather_z(bias_row)[:, 0].astype(f32)
+        z_a = gather_z(bundle_a)
+        full_a = gather_planes(z_a)
+        w_qkv = flat(full_a[:, :, : 3 * head_cols])
+        w_o = flat(full_a[:, :, 3 * head_cols :])
+        w_1 = flat(gather_planes(gather_z(bundle_b)))
+        w_2 = flat(gather_planes(gather_z(bundle_c)))
+
+        zeros_k = jnp.zeros((n_t, head_cols), f32)
+        qkv_bias = jnp.concatenate(
+            [biases[:, :head_cols], zeros_k, biases[:, head_cols : 2 * head_cols]], axis=1
+        ).reshape(1, -1)
+        in_bias = biases[:, 2 * head_cols :].reshape(1, -1)
+
+        own_x = to_chip(inputs)
+        x_full = both_rows(own_x)
+        qkv = ((nn(x_full, w_qkv) + qkv_bias) * qkv_scale).astype(bf16)
+        context, lse = attend_fwd(qkv, key_bias)
+        attended = own_sum(nt(context, w_o))
+        normed_one, inverse_one = normalize(own_x.astype(f32) + attended + out_bias)
+        first_norm = normed_one * gain_first + shift_first
+        first_full = both_rows(first_norm.astype(bf16))
+        pre_act = nn(first_full, w_1) + in_bias
+        activated, slope = gelu_and_slope(pre_act)
+        hidden = activated.astype(bf16)
+        mixed = own_sum(nt(hidden, w_2))
+        normed_two, inverse_two = normalize(first_norm + mixed + back_bias)
+        second = normed_two * gain_second + shift_second
+        layer_out = from_chip(jnp.where(own_valid, second, 0.0).astype(bf16))
+
+        grad_second = jnp.where(own_valid, to_chip(cotangent).astype(f32), 0.0)
+        grad_mixed = normalize_back(grad_second, gain_second, normed_two, inverse_two)
+
     grad_mixed_full = both_rows(grad_mixed.astype(bf16))
     grad_w2 = tn(grad_mixed_full, hidden)
-    (grad_pre,) = gelu_back(nn(grad_mixed_full, w_2))
-    grad_pre_low = grad_pre.astype(bf16)
+    grad_pre_low = (nn(grad_mixed_full, w_2) * slope.astype(f32)).astype(bf16)
     grad_w1 = tn(first_full, grad_pre_low)
     grad_first = grad_mixed + own_sum(nt(grad_pre_low, w_1))
     grad_att = normalize_back(grad_first, gain_first, normed_one, inverse_one)
@@ -402,14 +969,18 @@
     def row_sum(value):
         return reorder(jnp.sum(value, axis=0), 0)
 
+    if quad:
+        second_rows = [reorder(second_sums[i], 0) for i in range(3)]
+    else:
+        second_rows = [
+            row_sum(grad_mixed), row_sum(grad_second * normed_two), row_sum(grad_second)
+        ]
     norm_sums = jnp.concatenate(
         [
             row_sum(grad_att),
             row_sum(grad_first * normed_one),
             row_sum(grad_first),
-            row_sum(grad_mixed),
-            row_sum(grad_second * normed_two),
-            row_sum(grad_second),
+            *second_rows,
         ]
     )
     qkv_sum = jnp.sum(grad_qkv.astype(f32), axis=0).reshape(n_t, 3 * head_cols)

time: 642 us -> 585 us (0.911)
  Pallas kernels: 41.8 us -> 202 us
  waiting for transfers between devices: 182 us -> 61.8 us
  matrix products: 97.3 us -> 48.1 us
  other arithmetic: 80.7 us -> 47.9 us
  starting transfers between devices: 82.4 us -> 62.8 us
  local copies, waits for them, and re-layouts: 109 us -> 117 us
    pallas_call x1, Pallas kernels: 16.1 us -> 176 us  [forward(): pl.pallas_call(forward_kernel, in_specs=[sm, any_, any_, any_, any_, vm,...]
    ppermute x24 -> x0, waiting for transfers between devices: 75.9 us -> none  [the longest x12 55.5 us: gather_z(): got.append(lax.ppermute(got[-1], 'tensor', ring))]
    ppermute x3, waiting for transfers between devices: 45.2 us -> 3.55 us  [scatter(): from_x = lax.ppermute(for_x.astype(bf16), 'plane', x_pairs)]
    dot_general x4 -> x2, matrix products: 51.4 us -> 11.9 us  [nn(): lax.dot_general(a, b, (((1,), (0,)), ((), ())), preferred_element_type=f32)]
    ppermute x24 -> x0, starting transfers between devices: 27.8 us -> none  [the longest x12 17 us: gather_z(): got.append(lax.ppermute(got[-1], 'tensor', ring))]
    all_to_all x2 -> x0, waiting for transfers between devices: 25 us -> none  [to_chip(): return lax.all_to_all(both, 'tensor', 0, 0, tiled=True).reshape(own, width)]
    ppermute x9, starting transfers between devices: 25.8 us -> 45.3 us  [scatter(): lax.ppermute(total.astype(bf16), 'tensor', back).astype(f32)]
    ppermute x3, waiting for transfers between devices: 2.3 us -> 21.3 us  [scatter(): from_y = lax.ppermute(for_y.astype(bf16), 'plane', y_pairs)]
  transfers between devices with their start and end apart: 64 -> 29, of which waited for: 26 -> 14; matrix products, arithmetic and copies ran while one was open for 34% -> 28% of each run, Pallas kernels for 7% -> 4%
where the time goes in v2:
time: 585 us; the launch traced here: 580 us
  Pallas kernels  202 us (35%)
  local copies, waits for them, and re-layouts  117 us (20%)
  starting transfers between devices  62.8 us (11%)
  waiting for transfers between devices  61.8 us (11%)
  matrix products  48.1 us (8%)
  other arithmetic  47.9 us (8%)
  blocking collectives  38.4 us (7%)
    pallas_call x1, Pallas kernels, forward(): pl.pallas_call(forward_kernel, in_specs=[sm, any_, any_, any_, any_, vm,...  176 us
    ppermute x9, starting transfers between devices, scatter(): lax.ppermute(total.astype(bf16), 'tensor', back).astype(f32)  45.3 us
    reshape x6, local copies, waits for them, and re-layouts, scatter(): blocks = grad.reshape(4, rows, n_t, cols).transpose(0, 2, 1, 3)  42 us
    psum x1, blocking collectives, on_device(): lax.psum(jnp.concatenate([norm_sums, both.reshape(-1)]), ('plane', 'core'...  38.4 us
    dot_general x4, matrix products, tn(): lax.dot_general(a, b, (((0,), (0,)), ((), ())), preferred_element_type=f32)  26 us
    pallas_call x1, Pallas kernels, attend_bwd(): pl.pallas_call(lambda *refs: attend_bwd_kernel(block, *refs), grid=(group...  25.8 us
    ppermute x9, waiting for transfers between devices, scatter(): lax.ppermute(total.astype(bf16), 'tensor', back).astype(f32)  23.5 us
    ppermute x3, waiting for transfers between devices, scatter(): from_y = lax.ppermute(for_y.astype(bf16), 'plane', y_pairs)  21.3 us
  transfers between devices with their start and end apart: 29, of which 14 were waited for; matrix products, arithmetic and copies ran while one was open for 28% of the time, Pallas kernels for 4%

profile of v2, /device:TPU:0, one launch (start us, length us, event | category | flops | bytes accessed | tf_op | source)
XLA Modules:
  0.0 579.9 jit_solution(669836057591449874)
XLA Ops:
  21.6 2.2 pad_maximum_fusion.8
  27.8 176.1 %forward_layer.1 = (bf16[3,4,1024,512]{3,2,1,0:T(8,128)(2,1)}, bf16[1024,1024]{1,0:T(8,128)(2,1)}, bf16[4,1024,384]{2,1,0:T(8,128)(2,1)}, f32[8,1,1024]{2,1,0:T(...) custom-call(s32[1]{0:T(128)} %dynamic_slice.283.length_ref, ...), custom_call_target="tpu_custom_call" | custom-call | flops 17179869184 | bytes 62914560 | tf_op jit(solution)/shard_map/forward_layer/pallas_call | solution.py:627
  203.9 2.5 slice_bitcast_fusion
  210.6 2.1 slice_bitcast_fusion.21
  215.1 2.0 fusion.105.refs_3_
  222.3 3.4 slice_bitcast_fusion.17
  225.6 7.2 %fusion.15 = f32[1024,2048]{1,0:T(8,128)} fusion(bf16[1024,512]{1,0:T(8,128)(2,1)S(1)} %get-tuple-element.128, bf16[1024,512]{1,0:T(8,128)(2,1)S(1)} %get-tuple-element.129, bf16[1024,512]{1,0:T(8,128)(2,1)S(1)} %get-tuple-element.130, bf16[1024,512]{1,0:T(8,128)(2,1)S(1)} %get-tuple-element.127, bf16[512,1024]{1,0:T(8,128)(2,1)S(1)} %collective-permute-done.1, ...), kind=kOutput, calls=%fused_computation.21 | convolution fusion | flops 4315938816 | bytes 14680064 | tf_op jit(solution)/shard_map/dot_general | solution.py:21
  232.8 10.8 %reshape.709 = f32[4,256,4,512]{3,2,1,0:T(4,128)} reshape(f32[1024,2048]{1,0:T(8,128)} %fusion.15) | data formatting | bytes 16777216 | tf_op jit(solution)/shard_map/reshape | solution.py:923
  243.6 5.7 copy.96
  252.7 10.6 %convert_reduce_fusion = (f32[2048]{0:T(1024)S(1)}, bf16[1024,2048]{1,0:T(8,128)(2,1)}) fusion(bf16[1024,512]{1,0:T(8,128)(2,1)} %get-tuple-element.140, bf16[1024,512]{1,0:T(8,128)(2,1)} %get-tuple-element.141, bf16[1024,512]{1,0:T(8,128)(2,1)} %get-tuple-element.142, bf16[1024,512]{1,0:T(8,128)(2,1)} %get-tuple-element.139, ...), kind=kOutput, calls=%fused_computation.3 | convolution fusion | flops 4341102592 | bytes 14688256 | tf_op jit(solution)/shard_map/dot_general | solution.py:25
  263.4 10.7 %fusion.133 = f32[1024,2048]{1,0:T(8,128)} fusion(bf16[1024,1024]{1,0:T(8,128)(2,1)} %get-tuple-element.40, bf16[1024,2048]{1,0:T(8,128)(2,1)} %get-tuple-element.247), kind=kOutput, calls=%fused_computation.354 | convolution fusion | flops 4294967296 | bytes 14680064 | tf_op jit(solution)/shard_map/dot_general | solution.py:21
  274.1 5.9 %copy.93 = f32[4,256,4,512]{3,1,2,0:T(8,128)} copy(f32[4,256,4,512]{3,2,1,0:T(4,128)S(1)} %bitcast.285) | data formatting | bytes 16777216 | tf_op jit(solution)/shard_map/reshape | solution.py:923
  280.0 11.2 %reshape.708 = f32[4,256,4,512]{3,2,1,0:T(4,128)} reshape(f32[1024,2048]{1,0:T(8,128)} %fusion.133) | data formatting | bytes 16777216 | tf_op jit(solution)/shard_map/reshape | solution.py:923
  291.2 6.1 %copy.94 = f32[4,256,4,512]{3,1,2,0:T(8,128)S(1)} copy(f32[4,256,4,512]{3,2,1,0:T(4,128)} %reshape.708) | data formatting | bytes 16777216 | tf_op jit(solution)/shard_map/reshape | solution.py:923
  297.3 2.3 copy.95
  301.5 2.2 fusion.49
  306.4 8.3 %collective-permute-done.13 = bf16[2,256,512]{2,1,0:T(8,128)(2,1)S(1)} collective-permute-done((bf16[2,256,512]{2,1,0:T(8,128)(2,1)S(1)}, bf16[2,256,512]{2,1,0:T(8,128)(2,1)S(1)}, u32[]{:S(2)}, u32[]{:S(2)}) %collective-permute-start.13) | collective-permute-done | bytes 524320 | tf_op jit(solution)/shard_map/ppermute | solution.py:926
  318.2 6.7 %fusion.7 = f32[1024,1024]{1,0:T(8,128)S(1)} fusion(bf16[1024,2048]{1,0:T(8,128)(2,1)} %get-tuple-element.247, bf16[1024,512]{1,0:T(8,128)(2,1)S(1)} %copy-done.21, bf16[1024,512]{1,0:T(8,128)(2,1)S(1)} %copy-done.22, bf16[1024,512]{1,0:T(8,128)(2,1)S(1)} %copy-done.23, bf16[1024,512]{1,0:T(8,128)(2,1)S(1)} %copy-done.20), kind=kOutput, calls=%fused_computation.13 | convolution fusion | flops 4311744512 | bytes 12582912 | tf_op jit(solution)/shard_map/dot_general | solution.py:17
  327.6 9.5 %collective-permute-done.23 = bf16[4,256,512]{2,1,0:T(8,128)(2,1)S(1)} collective-permute-done((bf16[4,256,512]{2,1,0:T(8,128)(2,1)S(1)}, bf16[4,256,512]{2,1,0:T(8,128)(2,1)S(1)}, u32[]{:S(2)}, u32[]{:S(2)}) %collective-permute-start.23) | collective-permute-done | bytes 1048608 | tf_op jit(solution)/shard_map/ppermute | solution.py:930
  338.2 2.1 fusion.35
  341.1 13.6 %collective-permute-start.24 = (bf16[256,512]{1,0:T(8,128)(2,1)}, bf16[256,512]{1,0:T(8,128)(2,1)}, u32[]{:S(2)}, u32[]{:S(2)}) collective-permute-start(bf16[256,512]{1,0:T(8,128)(2,1)} %fusion.109), channel_id=1, source_target_pairs={{1,0},{2,1},{3,2},{0,3},{5,4},{6,5},{7,6},{4,7},{9,8},{10,9},{11,1... | collective-permute-start | bytes 786440 | tf_op jit(solution)/shard_map/ppermute | solution.py:940
  354.8 3.0 collective-permute-done.16
  360.3 13.7 %collective-permute-start.17 = (bf16[256,512]{1,0:T(8,128)(2,1)S(1)}, bf16[256,512]{1,0:T(8,128)(2,1)S(1)}, u32[]{:S(2)}, u32[]{:S(2)}) collective-permute-start(bf16[256,512]{1,0:T(8,128)(2,1)S(1)} %fusion.108), channel_id=1, source_target_pairs={{1,0},{2,1},{3,2},{0,3},{5,4},{6,5},{7,6},{4,7},{9,8},{10,9},{11,1... | collective-permute-start | bytes 786440 | tf_op jit(solution)/shard_map/ppermute | solution.py:940
  376.3 4.2 collective-permute-done.17
  381.6 4.5 collective-permute-start.18
  386.2 3.2 multiply_reduce_fusion
  390.3 2.0 copy-done.11
  397.3 4.4 collective-permute-done.26
  403.5 2.6 fusion.45
  406.1 1.9 concatenate.277
  411.6 25.8 %attend_bwd.1 = bf16[1024,1536]{1,0:T(8,128)(2,1)S(1)} custom-call(bf16[1024,1536]{1,0:T(8,128)(2,1)} %pad_maximum_fusion.refs_0_, bf16[1024,512]{1,0:T(8,128)(2,1)S(1)} %convolution_convert_fusion.refs_1_, f32[4,2,1024]{2,1,0:T(2,128)S(1)} %reshape.704.refs_2_, f32[1024,1]{1,0:T(8,128)S(1)} %copy-done), custom_call_target="tpu_custom_call" | custom-call | flops 21474836480 | bytes 7340032 | tf_op jit(solution)/shard_map/attend_bwd/pallas_call | solution.py:116
  437.5 5.5 fusion.31
  443.0 7.9 %concatenate.275 = f32[4,256,4,384]{3,2,1,0:T(4,128)} reshape(f32[1024,1536]{1,0:T(8,128)} %fusion.31) | data formatting | bytes 12582912 | tf_op jit(solution)/shard_map/concatenate | solution.py:945
  450.9 3.7 copy.71
  458.5 1.9 fusion.89
  461.3 4.2 collective-permute-done.6
  472.6 3.5 fusion.23
  479.5 8.8 %collective-permute-done.9 = bf16[4,256,512]{2,1,0:T(8,128)(2,1)} collective-permute-done((bf16[4,256,512]{2,1,0:T(8,128)(2,1)}, bf16[4,256,512]{2,1,0:T(8,128)(2,1)}, u32[]{:S(2)}, u32[]{:S(2)}) %collective-permute-start.9) | collective-permute-done | bytes 1048608 | tf_op jit(solution)/shard_map/ppermute | solution.py:930
  490.1 2.6 fusion.39
  492.8 2.8 collective-permute-start.10
  495.6 6.2 %collective-permute-done.10 = bf16[256,512]{1,0:T(8,128)(2,1)S(1)} collective-permute-done((bf16[256,512]{1,0:T(8,128)(2,1)S(1)}, bf16[256,512]{1,0:T(8,128)(2,1)S(1)}, u32[]{:S(2)}, u32[]{:S(2)}) %collective-permute-start.10) | collective-permute-done | bytes 262176 | tf_op jit(solution)/shard_map/ppermute | solution.py:940
  502.0 4.3 collective-permute-start.11
  506.4 6.5 %collective-permute-done.11 = bf16[256,512]{1,0:T(8,128)(2,1)S(1)} collective-permute-done((bf16[256,512]{1,0:T(8,128)(2,1)S(1)}, bf16[256,512]{1,0:T(8,128)(2,1)S(1)}, u32[]{:S(2)}, u32[]{:S(2)}) %collective-permute-start.11) | collective-permute-done | bytes 262176 | tf_op jit(solution)/shard_map/ppermute | solution.py:940
  514.0 4.3 collective-permute-start.12
  518.3 3.7 fusion.41
  522.1 3.6 all-to-all-start
  525.7 2.1 collective-permute-done.12
  530.4 38.4 %psum.7 = f32[12288]{0:T(1024)S(1)} all-reduce(f32[12288]{0:T(1024)S(1)} %constant_dynamic-update-slice_fusion), channel_id=1, replica_groups=mesh['plane'=4,'core'=2,'tensor'=4] {'plane','core','tensor'}, use_global_device_ids=true, to_apply=%region_8.9 | all-reduce | flops 12288 | bytes 98304 | tf_op jit(solution)/shard_map/psum | solution.py:995
  (372 shorter events, 101.0 us)
Async XLA Ops:
  0.7 19.0 %copy-start.30 = (bf16[2,256,1024]{2,1,0:T(8,128)(2,1)S(1)}, bf16[2,256,1024]{2,1,0:T(8,128)(2,1)}, u32[]{:S(2)}) copy-start(bf16[2,256,1024]{2,1,0:T(8,128)(2,1)} %param.35) | copy-start | bytes 3145732
  0.7 19.0 %copy-start.31 = (bf16[2,256,1024]{2,1,0:T(8,128)(2,1)S(1)}, bf16[2,256,1024]{2,1,0:T(8,128)(2,1)}, u32[]{:S(2)}) copy-start(bf16[2,256,1024]{2,1,0:T(8,128)(2,1)} %param.18) | copy-start | bytes 3145732
  0.7 25.4 %collective-permute-start = (s32[2]{0:T(128)}, s32[2]{0:T(128)S(1)}, u32[]{:S(2)}, u32[]{:S(2)}) collective-permute-start(s32[2]{0:T(128)} %param.19), channel_id=1, source_target_pairs={{0,4},{4,0},{1,5},{5,1},{2,6},{6,2},{3,7},{7,3},{8,12},{12,8},{9,1... | collective-permute-start | bytes 32 | tf_op jit(solution)/shard_map/ppermute | solution.py:679
  213.7 11.9 %collective-permute-start.1 = (bf16[512,1024]{1,0:T(8,128)(2,1)S(1)}, bf16[512,1024]{1,0:T(8,128)(2,1)S(1)}, u32[]{:S(2)}, u32[]{:S(2)}) collective-permute-start(bf16[512,1024]{1,0:T(8,128)(2,1)S(1)} %convert_element_type.227), channel_id=1, source_target_pairs={{0,4},{4,0},{1,5},{5,1},{2,6},{6,2},{3,7},{7,3},{8,12},{12,8},{9,1... | collective-permute-start | bytes 3145736 | tf_op jit(solution)/shard_map/ppermute | solution.py:679
  249.4 24.7 %slice-start = ((s8[8388608]{0:T(1024)(128)(4,1)}), s8[4194304]{0:T(1024)(128)(4,1)S(1)}, s32[]{:S(2)}) async-start(s8[8388608]{0:T(1024)(128)(4,1)} %bitcast.284), calls=%async_computation.1 | async-start | bytes 8388608
  250.3 51.1 %collective-permute-start.20 = (bf16[2,256,512]{2,1,0:T(8,128)(2,1)}, bf16[2,256,512]{2,1,0:T(8,128)(2,1)}, u32[]{:S(2)}, u32[]{:S(2)}) collective-permute-start(bf16[2,256,512]{2,1,0:T(8,128)(2,1)} %get-tuple-element.126), channel_id=1, source_target_pairs={{0,16},{8,24},{16,0},{24,8},{1,17},{9,25},{17,1},{25,9},{2,18},{10... | collective-permute-start | bytes 1572872 | tf_op jit(solution)/shard_map/ppermute | solution.py:926
  251.3 50.2 %collective-permute-start.22 = (bf16[2,256,512]{2,1,0:T(8,128)(2,1)S(1)}, bf16[2,256,512]{2,1,0:T(8,128)(2,1)}, u32[]{:S(2)}, u32[]{:S(2)}) collective-permute-start(bf16[2,256,512]{2,1,0:T(8,128)(2,1)S(1)} %get-tuple-element.125), channel_id=1, source_target_pairs={{0,8},{8,0},{16,24},{24,16},{1,9},{9,1},{17,25},{25,17},{2,10},{10... | collective-permute-start | bytes 1572872 | tf_op jit(solution)/shard_map/ppermute | solution.py:925
  252.7 21.3 %slice-start.1 = ((s8[8388608]{0:T(1024)(128)(4,1)}), s8[4194304]{0:T(1024)(128)(4,1)S(1)}, s32[]{:S(2)}) async-start(s8[8388608]{0:T(1024)(128)(4,1)} %bitcast.284), calls=%async_computation.2 | async-start | bytes 8388608
  299.7 14.9 %collective-permute-start.13 = (bf16[2,256,512]{2,1,0:T(8,128)(2,1)S(1)}, bf16[2,256,512]{2,1,0:T(8,128)(2,1)S(1)}, u32[]{:S(2)}, u32[]{:S(2)}) collective-permute-start(bf16[2,256,512]{2,1,0:T(8,128)(2,1)S(1)} %get-tuple-element.122), channel_id=1, source_target_pairs={{0,16},{8,24},{16,0},{24,8},{1,17},{9,25},{17,1},{25,9},{2,18},{10... | collective-permute-start | bytes 1572872 | tf_op jit(solution)/shard_map/ppermute | solution.py:926
  300.8 14.9 %collective-permute-start.15 = (bf16[2,256,512]{2,1,0:T(8,128)(2,1)S(1)}, bf16[2,256,512]{2,1,0:T(8,128)(2,1)S(1)}, u32[]{:S(2)}, u32[]{:S(2)}) collective-permute-start(bf16[2,256,512]{2,1,0:T(8,128)(2,1)S(1)} %get-tuple-element.121), channel_id=1, source_target_pairs={{0,8},{8,0},{16,24},{24,16},{1,9},{9,1},{17,25},{25,17},{2,10},{10... | collective-permute-start | bytes 1572872 | tf_op jit(solution)/shard_map/ppermute | solution.py:925
  303.7 33.4 %collective-permute-start.23 = (bf16[4,256,512]{2,1,0:T(8,128)(2,1)S(1)}, bf16[4,256,512]{2,1,0:T(8,128)(2,1)S(1)}, u32[]{:S(2)}, u32[]{:S(2)}) collective-permute-start(bf16[4,256,512]{2,1,0:T(8,128)(2,1)S(1)} %pad_maximum_fusion.17), channel_id=1, source_target_pairs={{0,16},{8,24},{16,0},{24,8},{1,17},{9,25},{17,1},{25,9},{2,18},{10... | collective-permute-start | bytes 3145736 | tf_op jit(solution)/shard_map/ppermute | solution.py:930
  304.9 33.3 %collective-permute-start.21 = (bf16[4,256,512]{2,1,0:T(8,128)(2,1)S(1)}, bf16[4,256,512]{2,1,0:T(8,128)(2,1)S(1)}, u32[]{:S(2)}, u32[]{:S(2)}) collective-permute-start(bf16[4,256,512]{2,1,0:T(8,128)(2,1)S(1)} %pad_maximum_fusion.16), channel_id=1, source_target_pairs={{0,8},{8,0},{16,24},{24,16},{1,9},{9,1},{17,25},{25,17},{2,10},{10... | collective-permute-start | bytes 3145736 | tf_op jit(solution)/shard_map/ppermute | solution.py:929
  316.2 41.5 %collective-permute-start.16 = (bf16[4,256,512]{2,1,0:T(8,128)(2,1)S(1)}, bf16[4,256,512]{2,1,0:T(8,128)(2,1)S(1)}, u32[]{:S(2)}, u32[]{:S(2)}) collective-permute-start(bf16[4,256,512]{2,1,0:T(8,128)(2,1)S(1)} %pad_maximum_fusion.15), channel_id=1, source_target_pairs={{0,16},{8,24},{16,0},{24,8},{1,17},{9,25},{17,1},{25,9},{2,18},{10... | collective-permute-start | bytes 3145736 | tf_op jit(solution)/shard_map/ppermute | solution.py:930
  317.4 41.1 %collective-permute-start.14 = (bf16[4,256,512]{2,1,0:T(8,128)(2,1)S(1)}, bf16[4,256,512]{2,1,0:T(8,128)(2,1)S(1)}, u32[]{:S(2)}, u32[]{:S(2)}) collective-permute-start(bf16[4,256,512]{2,1,0:T(8,128)(2,1)S(1)} %pad_maximum_fusion.14), channel_id=1, source_target_pairs={{0,8},{8,0},{16,24},{24,16},{1,9},{9,1},{17,25},{25,17},{2,10},{10... | collective-permute-start | bytes 3145736 | tf_op jit(solution)/shard_map/ppermute | solution.py:929
  325.0 15.3 %copy-start.13 = (f32[1024,1024]{1,0:T(8,128)}, f32[1024,1024]{1,0:T(8,128)S(1)}, u32[]{:S(2)}) copy-start(f32[1024,1024]{1,0:T(8,128)S(1)} %fusion.7) | copy-start | bytes 12582916
  326.6 59.6 %collective-permute-start.2 = (f32[512,1024]{1,0:T(8,128)}, f32[512,1024]{1,0:T(8,128)}, u32[]{:S(2)}, u32[]{:S(2)}) collective-permute-start(f32[512,1024]{1,0:T(8,128)} %slice.457), channel_id=1, source_target_pairs={{0,4},{4,0},{1,5},{5,1},{2,6},{6,2},{3,7},{7,3},{8,12},{12,8},{9,1... | collective-permute-start | bytes 6291464 | tf_op jit(solution)/shard_map/ppermute | solution.py:679
  340.3 18.6 %copy-start.10 = (f32[4,256,512]{2,1,0:T(8,128)}, f32[4,256,512]{2,1,0:T(8,128)S(1)}, u32[]{:S(2)}) copy-start(f32[4,256,512]{2,1,0:T(8,128)S(1)} %fusion.35) | copy-start | bytes 6291460
  341.1 33.5 %copy-start.40 = (f32[512,1]{1,0:T(8,128)S(1)}, f32[512,1]{1,0:T(8,128)}, u32[]{:S(2)}) copy-start(f32[512,1]{1,0:T(8,128)} %get-tuple-element.35) | copy-start | bytes 6148
  341.1 33.6 %copy-start.58 = (f32[8,1,1024]{2,1,0:T(1,128)S(1)}, f32[8,1,1024]{2,1,0:T(1,128)}, u32[]{:S(2)}) copy-start(f32[8,1,1024]{2,1,0:T(1,128)} %get-tuple-element.37) | copy-start | bytes 98308
  341.1 45.0 %copy-start.6 = (f32[512,1024]{1,0:T(8,128)S(1)}, f32[512,1024]{1,0:T(8,128)}, u32[]{:S(2)}) copy-start(f32[512,1024]{1,0:T(8,128)} %get-tuple-element.34) | copy-start | bytes 6291460
  341.1 33.8 %collective-permute-start.24 = (bf16[256,512]{1,0:T(8,128)(2,1)}, bf16[256,512]{1,0:T(8,128)(2,1)}, u32[]{:S(2)}, u32[]{:S(2)}) collective-permute-start(bf16[256,512]{1,0:T(8,128)(2,1)} %fusion.109), channel_id=1, source_target_pairs={{1,0},{2,1},{3,2},{0,3},{5,4},{6,5},{7,6},{4,7},{9,8},{10,9},{11,1... | collective-permute-start | bytes 786440 | tf_op jit(solution)/shard_map/ppermute | solution.py:940
  360.3 20.2 %collective-permute-start.17 = (bf16[256,512]{1,0:T(8,128)(2,1)S(1)}, bf16[256,512]{1,0:T(8,128)(2,1)S(1)}, u32[]{:S(2)}, u32[]{:S(2)}) collective-permute-start(bf16[256,512]{1,0:T(8,128)(2,1)S(1)} %fusion.108), channel_id=1, source_target_pairs={{1,0},{2,1},{3,2},{0,3},{5,4},{6,5},{7,6},{4,7},{9,8},{10,9},{11,1... | collective-permute-start | bytes 786440 | tf_op jit(solution)/shard_map/ppermute | solution.py:940
  376.2 14.1 %collective-permute-start.25 = (bf16[256,512]{1,0:T(8,128)(2,1)S(1)}, bf16[256,512]{1,0:T(8,128)(2,1)S(1)}, u32[]{:S(2)}, u32[]{:S(2)}) collective-permute-start(bf16[256,512]{1,0:T(8,128)(2,1)S(1)} %fusion.81), channel_id=1, source_target_pairs={{1,0},{2,1},{3,2},{0,3},{5,4},{6,5},{7,6},{4,7},{9,8},{10,9},{11,1... | collective-permute-start | bytes 786440 | tf_op jit(solution)/shard_map/ppermute | solution.py:940
  381.6 10.8 %collective-permute-start.18 = (bf16[256,512]{1,0:T(8,128)(2,1)S(1)}, bf16[256,512]{1,0:T(8,128)(2,1)S(1)}, u32[]{:S(2)}, u32[]{:S(2)}) collective-permute-start(bf16[256,512]{1,0:T(8,128)(2,1)S(1)} %fusion.86), channel_id=1, source_target_pairs={{1,0},{2,1},{3,2},{0,3},{5,4},{6,5},{7,6},{4,7},{9,8},{10,9},{11,1... | collective-permute-start | bytes 786440 | tf_op jit(solution)/shard_map/ppermute | solution.py:940
  389.9 12.6 %copy-start.3 = (f32[512,1024]{1,0:T(8,128)}, f32[512,1024]{1,0:T(8,128)S(1)}, u32[]{:S(2)}) copy-start(f32[512,1024]{1,0:T(8,128)S(1)} %get-tuple-element.99) | copy-start | bytes 6291460
  390.0 13.5 %copy-start.45 = (bf16[1024,128]{1,0:T(8,128)(2,1)S(1)}, bf16[1024,128]{1,0:T(8,128)(2,1)}, u32[]{:S(2)}) copy-start(bf16[1024,128]{1,0:T(8,128)(2,1)} %get-tuple-element.163) | copy-start | bytes 786436
  390.0 13.5 %copy-start.46 = (bf16[1024,128]{1,0:T(8,128)(2,1)S(1)}, bf16[1024,128]{1,0:T(8,128)(2,1)}, u32[]{:S(2)}) copy-start(bf16[1024,128]{1,0:T(8,128)(2,1)} %get-tuple-element.164) | copy-start | bytes 786436
  390.0 13.5 %copy-start.47 = (bf16[1024,128]{1,0:T(8,128)(2,1)S(1)}, bf16[1024,128]{1,0:T(8,128)(2,1)}, u32[]{:S(2)}) copy-start(bf16[1024,128]{1,0:T(8,128)(2,1)} %get-tuple-element.165) | copy-start | bytes 786436
  390.0 13.5 %copy-start.48 = (bf16[1024,128]{1,0:T(8,128)(2,1)S(1)}, bf16[1024,128]{1,0:T(8,128)(2,1)}, u32[]{:S(2)}) copy-start(bf16[1024,128]{1,0:T(8,128)(2,1)} %get-tuple-element.166) | copy-start | bytes 786436
  390.2 12.3 %collective-permute-start.3 = (bf16[512,1024]{1,0:T(8,128)(2,1)S(1)}, bf16[512,1024]{1,0:T(8,128)(2,1)S(1)}, u32[]{:S(2)}, u32[]{:S(2)}) collective-permute-start(bf16[512,1024]{1,0:T(8,128)(2,1)S(1)} %convert_element_type.231), channel_id=1, source_target_pairs={{0,4},{4,0},{1,5},{5,1},{2,6},{6,2},{3,7},{7,3},{8,12},{12,8},{9,1... | collective-permute-start | bytes 3145736 | tf_op jit(solution)/shard_map/ppermute | solution.py:679
  392.3 9.3 %collective-permute-start.26 = (bf16[256,512]{1,0:T(8,128)(2,1)S(1)}, bf16[256,512]{1,0:T(8,128)(2,1)S(1)}, u32[]{:S(2)}, u32[]{:S(2)}) collective-permute-start(bf16[256,512]{1,0:T(8,128)(2,1)S(1)} %fusion.83), channel_id=1, source_target_pairs={{1,0},{2,1},{3,2},{0,3},{5,4},{6,5},{7,6},{4,7},{9,8},{10,9},{11,1... | collective-permute-start | bytes 786440 | tf_op jit(solution)/shard_map/ppermute | solution.py:940
  394.3 64.2 %collective-permute-start.19 = (bf16[256,512]{1,0:T(8,128)(2,1)}, bf16[256,512]{1,0:T(8,128)(2,1)S(1)}, u32[]{:S(2)}, u32[]{:S(2)}) collective-permute-start(bf16[256,512]{1,0:T(8,128)(2,1)} %fusion.88), channel_id=1, source_target_pairs={{1,0},{2,1},{3,2},{0,3},{5,4},{6,5},{7,6},{4,7},{9,8},{10,9},{11,1... | collective-permute-start | bytes 786440 | tf_op jit(solution)/shard_map/ppermute | solution.py:940
  411.6 25.9 %copy-start.59 = (bf16[1536]{0:T(1024)(128)(2,1)S(1)}, bf16[1536]{0:T(1024)(128)(2,1)}, u32[]{:S(2)}) copy-start(bf16[1536]{0:T(1024)(128)(2,1)} %convert_element_type.233) | copy-start | bytes 9220
  411.6 25.9 %copy-start.72 = (bf16[1024,1024]{1,0:T(8,128)(2,1)S(1)}, bf16[1024,1024]{1,0:T(8,128)(2,1)}, u32[]{:S(2)}) copy-start(bf16[1024,1024]{1,0:T(8,128)(2,1)} %get-tuple-element.38) | copy-start | bytes 6291460
  456.1 9.4 %collective-permute-start.6 = (bf16[2,256,512]{2,1,0:T(8,128)(2,1)}, bf16[2,256,512]{2,1,0:T(8,128)(2,1)S(1)}, u32[]{:S(2)}, u32[]{:S(2)}) collective-permute-start(bf16[2,256,512]{2,1,0:T(8,128)(2,1)} %get-tuple-element.118), channel_id=1, source_target_pairs={{0,16},{8,24},{16,0},{24,8},{1,17},{9,25},{17,1},{25,9},{2,18},{10... | collective-permute-start | bytes 1572872 | tf_op jit(solution)/shard_map/ppermute | solution.py:926
  457.0 9.3 %collective-permute-start.8 = (bf16[2,256,512]{2,1,0:T(8,128)(2,1)S(1)}, bf16[2,256,512]{2,1,0:T(8,128)(2,1)}, u32[]{:S(2)}, u32[]{:S(2)}) collective-permute-start(bf16[2,256,512]{2,1,0:T(8,128)(2,1)S(1)} %get-tuple-element.117), channel_id=1, source_target_pairs={{0,8},{8,0},{16,24},{24,16},{1,9},{9,1},{17,25},{25,17},{2,10},{10... | collective-permute-start | bytes 1572872 | tf_op jit(solution)/shard_map/ppermute | solution.py:925
  461.3 14.7 %copy-start.2 = (f32[4,4,256,512]{3,2,1,0:T(8,128)}, f32[4,4,256,512]{3,2,1,0:T(8,128)S(1)}, u32[]{:S(2)}) copy-start(f32[4,4,256,512]{3,2,1,0:T(8,128)S(1)} %maximum_bitcast_fusion) | copy-start | bytes 25165828
  469.0 19.3 %collective-permute-start.9 = (bf16[4,256,512]{2,1,0:T(8,128)(2,1)}, bf16[4,256,512]{2,1,0:T(8,128)(2,1)}, u32[]{:S(2)}, u32[]{:S(2)}) collective-permute-start(bf16[4,256,512]{2,1,0:T(8,128)(2,1)} %pad_maximum_fusion.13), channel_id=1, source_target_pairs={{0,16},{8,24},{16,0},{24,8},{1,17},{9,25},{17,1},{25,9},{2,18},{10... | collective-permute-start | bytes 3145736 | tf_op jit(solution)/shard_map/ppermute | solution.py:930
  471.2 18.9 %collective-permute-start.7 = (bf16[4,256,512]{2,1,0:T(8,128)(2,1)}, bf16[4,256,512]{2,1,0:T(8,128)(2,1)}, u32[]{:S(2)}, u32[]{:S(2)}) collective-permute-start(bf16[4,256,512]{2,1,0:T(8,128)(2,1)} %pad_maximum_fusion.12), channel_id=1, source_target_pairs={{0,8},{8,0},{16,24},{24,16},{1,9},{9,1},{17,25},{25,17},{2,10},{10... | collective-permute-start | bytes 3145736 | tf_op jit(solution)/shard_map/ppermute | solution.py:929
  478.8 39.5 %collective-permute-start.4 = (f32[512,1024]{1,0:T(8,128)}, f32[512,1024]{1,0:T(8,128)}, u32[]{:S(2)}, u32[]{:S(2)}) collective-permute-start(f32[512,1024]{1,0:T(8,128)} %slice.467), channel_id=1, source_target_pairs={{0,4},{4,0},{1,5},{5,1},{2,6},{6,2},{3,7},{7,3},{8,12},{12,8},{9,1... | collective-permute-start | bytes 6291464 | tf_op jit(solution)/shard_map/ppermute | solution.py:679
  479.5 26.8 %copy-start.67 = (pred[2]{0:T(512)(128)(4,1)S(1)}, pred[2]{0:T(512)(128)(4,1)}, u32[]{:S(2)}) copy-start(pred[2]{0:T(512)(128)(4,1)} %iota_compare_fusion.1) | copy-start | bytes 10
  479.5 38.8 %copy-start.4 = (f32[512,1024]{1,0:T(8,128)S(1)}, f32[512,1024]{1,0:T(8,128)}, u32[]{:S(2)}) copy-start(f32[512,1024]{1,0:T(8,128)} %copy-done.3) | copy-start | bytes 6291460
  492.8 9.1 %collective-permute-start.10 = (bf16[256,512]{1,0:T(8,128)(2,1)S(1)}, bf16[256,512]{1,0:T(8,128)(2,1)S(1)}, u32[]{:S(2)}, u32[]{:S(2)}) collective-permute-start(bf16[256,512]{1,0:T(8,128)(2,1)S(1)} %fusion.107), channel_id=1, source_target_pairs={{1,0},{2,1},{3,2},{0,3},{5,4},{6,5},{7,6},{4,7},{9,8},{10,9},{11,1... | collective-permute-start | bytes 786440 | tf_op jit(solution)/shard_map/ppermute | solution.py:940
  502.0 10.9 %collective-permute-start.11 = (bf16[256,512]{1,0:T(8,128)(2,1)S(1)}, bf16[256,512]{1,0:T(8,128)(2,1)S(1)}, u32[]{:S(2)}, u32[]{:S(2)}) collective-permute-start(bf16[256,512]{1,0:T(8,128)(2,1)S(1)} %fusion.91), channel_id=1, source_target_pairs={{1,0},{2,1},{3,2},{0,3},{5,4},{6,5},{7,6},{4,7},{9,8},{10,9},{11,1... | collective-permute-start | bytes 786440 | tf_op jit(solution)/shard_map/ppermute | solution.py:940
  514.0 13.9 %collective-permute-start.12 = (bf16[256,512]{1,0:T(8,128)(2,1)S(1)}, bf16[256,512]{1,0:T(8,128)(2,1)S(1)}, u32[]{:S(2)}, u32[]{:S(2)}) collective-permute-start(bf16[256,512]{1,0:T(8,128)(2,1)S(1)} %fusion.93), channel_id=1, source_target_pairs={{1,0},{2,1},{3,2},{0,3},{5,4},{6,5},{7,6},{4,7},{9,8},{10,9},{11,1... | collective-permute-start | bytes 786440 | tf_op jit(solution)/shard_map/ppermute | solution.py:940
  522.1 51.2 %all-to-all-start = ((bf16[4,128,1024]{2,1,0:T(8,128)(2,1)}), bf16[4,128,1024]{2,1,0:T(8,128)(2,1)S(1)}, u32[]{:S(2)}, u32[]{:S(2)}) async-start(bf16[4,128,1024]{2,1,0:T(8,128)(2,1)} %bitcast.39), calls=%async_computation | async-start | bytes 2097152 | tf_op jit(solution)/shard_map/all_to_all | solution.py:743
  530.4 40.5 %collective-permute-start.27 = (f32[128,1536]{0,1:T(8,128)}, f32[128,1536]{0,1:T(8,128)S(1)}, u32[]{:S(2)}, u32[]{:S(2)}) collective-permute-start(f32[128,1536]{0,1:T(8,128)} %bitcast.303), channel_id=1, source_target_pairs={{0,4},{4,0},{1,5},{5,1},{2,6},{6,2},{3,7},{7,3},{8,12},{12,8},{9,1... | collective-permute-start | bytes 2359304 | tf_op jit(solution)/shard_map/ppermute | solution.py:679
  574.1 2.6 collective-permute-start.5
  (59 other events, 245.1 us)

commit v3 on v2

--- a/solution.py
+++ b/solution.py
@@ -675,6 +675,505 @@
     )(length, xp, cp, keep, give, bias, vec)
 
 
+def backward_kernel(
+    w_ref, xf_ref, qkv_ref, lse_ref, ctx_ref, ff_ref, hid_ref, dg_ref, n1_ref, inv1_ref, gm_ref,
+    vec_ref, sums_ref, length_ref,
+    gi_ref, mine_ref, got_ref, total_ref,
+    w, grad_c, pad, pre, gmf, gaf, act, turned, gm, n1, own_part, other, got, gi_own,
+    d_got, rx, ry, rz, home, dk_acc, dv_acc, vz, zg, xg, yg, cg, tot,
+    d_s, d_r, x_s, x_r, y_s, y_r, z_s, z_r, h_s, h_r, h_l, e_s, e_r, g_s, g_r, v_s, v_r, l_s,
+):
+    plane = lax.axis_index("plane")
+    core = lax.axis_index("core")
+    place = lax.axis_index("tensor")
+    partner = {"core": 1 - core}
+    x_side = {"plane": plane + 1 - 2 * (plane % 2)}
+    y_side = {"plane": (plane + 2) % 4}
+    z_back = {"tensor": (place + 3) % 4}
+    rows, width = gmf.shape
+    own = rows // 2
+    part = own // 4
+    piece = width // 4
+    head_cols = 2 * HD
+    tile = 256
+    small = 32
+
+    def remote(source, target, send, recv, to):
+        return pltpu.make_async_remote_copy(
+            source, target, send, recv, device_id=to, device_id_type=MESH
+        )
+
+    def block(b, j, k):
+        at = slice(k * piece, (k + 1) * piece)
+        if b == 2:
+            return grad_c.at[j, at]
+        return w.at[b + 1, j, at]
+
+    def d_copy(b, j):
+        to = x_side if j < 2 else y_side
+        return remote(block(b, j, 3), d_got.at[b, j], d_s.at[b, j], d_r.at[b, j], to)
+
+    def x_copy(b, j):
+        return remote(block(b, j, 1), rx.at[b, j], x_s.at[b, j], x_r.at[b, j], x_side)
+
+    def y_copy(b, j):
+        return remote(block(b, j, 2), ry.at[b, j], y_s.at[b, j], y_r.at[b, j], y_side)
+
+    def z_copy(b, j):
+        return remote(
+            block(b, j, 0), rz.at[b, j - 1], z_s.at[b, j - 1], z_r.at[b, j - 1], z_back
+        )
+
+    def home_copy(b):
+        at = pl.ds((1 - core) * (piece // 2), piece // 2)
+        return remote(home.at[b, at], got_ref.at[b], h_s.at[b], h_r.at[b], partner)
+
+    def home_keep(b):
+        at = pl.ds(core * (piece // 2), piece // 2)
+        return pltpu.make_async_copy(home.at[b, at], mine_ref.at[b], h_l.at[b])
+
+    def send_first(b, j):
+        d_copy(b, j).start()
+        (x_copy if j < 2 else y_copy)(b, j).start()
+
+    def send_second(b, j):
+        d_copy(b, j).wait_recv()
+        here = block(b, j, 2 if j < 2 else 1)
+        here[...] = (here[...].astype(f32) + d_got[b, j].astype(f32)).astype(bf16)
+        (y_copy if j < 2 else x_copy)(b, j).start()
+
+    def send_third(b, j):
+        x_copy(b, j).wait_recv()
+        y_copy(b, j).wait_recv()
+        total = block(b, j, 0)[...].astype(f32) + rx[b, j].astype(f32) + ry[b, j].astype(f32)
+        if j < 3:
+            z_copy(b, j + 1).wait_recv()
+            total = total + rz[b, j].astype(f32)
+        if j > 0:
+            block(b, j, 0)[...] = total.astype(bf16)
+            z_copy(b, j).start()
+        else:
+            home[b] = total
+            home_copy(b).start()
+            home_keep(b).start()
+
+    def exchange(source, target, n):
+        return remote(source, target, e_s.at[n], e_r.at[n], partner)
+
+    def back(s):
+        to = {"core": place // 2, "tensor": s}
+        slot = 2 * (place % 2) + core
+        return remote(
+            gi_own.at[s * part : (s + 1) * part], gi_ref.at[slot], g_s.at[s], g_r.at[slot], to
+        )
+
+    def back_local(s):
+        slot = 2 * (place % 2) + core
+        return pltpu.make_async_copy(
+            gi_own.at[s * part : (s + 1) * part], gi_ref.at[slot], g_r.at[slot]
+        )
+
+    def is_home(s):
+        return jnp.logical_and(core == place // 2, place == s)
+
+    def v_copy(j):
+        to = {"tensor": (place + 4 - j) % 4}
+        return remote(vz.at[j], zg.at[place], v_s.at[j - 1], v_r.at[place], to)
+
+    def v_got(j):
+        source = (place + j) % 4
+        return remote(vz.at[j], zg.at[source], v_s.at[j - 1], v_r.at[source], z_back)
+
+    coming = {}
+
+    def fetch(name, source, target):
+        copy = pltpu.make_async_copy(source, target, l_s.at[len(coming)])
+        copy.start()
+        coming[name] = copy
+
+    fetch("gm", gm_ref, gm)
+    for j in (3, 2, 1, 0):
+        fetch(("hid", j), hid_ref.at[j], pad.at[j])
+    for j in range(4):
+        fetch(("w2", j), w_ref.at[2, j], w.at[2, j])
+        fetch(("dg", j), dg_ref.at[j], pre.at[j])
+    fetch("w1", w_ref.at[1], w.at[1])
+    fetch("n1", n1_ref, n1)
+    fetch("ff", ff_ref, act)
+    fetch("w0", w_ref.at[0], w.at[0])
+
+    barrier = pltpu.get_barrier_semaphore()
+    friends = [x_side, y_side, partner]
+    for s in range(1, 4):
+        friends.append({"tensor": (place + s) % 4})
+        friends.append({"tensor": (place + s) % 4, "core": 1 - core})
+    for friend in friends:
+        pl.semaphore_signal(barrier, inc=1, device_id=friend, device_id_type=MESH)
+
+    coming["gm"].wait()
+
+    def round_body(i, _):
+        at = pl.ds(pl.multiple_of(i * 128, 128), 128)
+        gmf[at, :] = gm[at, :].astype(bf16)
+        return 0
+
+    lax.fori_loop(0, own // 128, round_body, 0)
+    pl.semaphore_wait(barrier, len(friends))
+    share_gm = exchange(gmf.at[0:own], gmf.at[own : 2 * own], 0)
+    share_gm.start()
+    vz[...] = jnp.zeros_like(vz)
+
+    def turn(source, first, last):
+        def body(i, _):
+            at = pl.ds(pl.multiple_of(i * tile, tile), tile)
+            turned[:, at] = source[at, :].T
+            return 0
+
+        lax.fori_loop(first, last, body, 0)
+
+    def weight_grad(b, j, right, columns):
+        def body(k, _):
+            at = pl.ds(pl.multiple_of(k * tile, tile), tile)
+            value = nn(turned[at, :], right()).astype(bf16)
+            if b == 2:
+                grad_c[j, at, columns] = value
+            else:
+                w[b + 1, j, at, columns] = value
+            return 0
+
+        lax.fori_loop(0, width // tile, body, 0)
+
+    every = slice(None)
+    turn(gmf, 0, own // tile)
+    share_gm.wait_recv()
+    turn(gmf, own // tile, rows // tile)
+    for j in (3, 2, 1, 0):
+        coming[("hid", j)].wait()
+        weight_grad(2, j, lambda: pad[j], every)
+        send_first(2, j)
+
+    def slope_rows(j):
+        coming[("w2", j)].wait()
+        coming[("dg", j)].wait()
+
+        def body(i, _):
+            at = pl.ds(pl.multiple_of(i * tile, tile), tile)
+            value = (nn(gmf[at, :], w[2, j]) * pre[j, at, :].astype(f32)).astype(bf16)
+            pre[j, at, :] = value
+            vz[j, 8:9, 2 * head_cols : 2 * head_cols + value.shape[1]] += jnp.sum(
+                value.astype(f32), axis=0, keepdims=True
+            )
+            return 0
+
+        lax.fori_loop(0, rows // tile, body, 0)
+
+    slope_rows(0)
+    slope_rows(1)
+    send_second(2, 3)
+    slope_rows(2)
+    send_second(2, 2)
+    slope_rows(3)
+    send_second(2, 1)
+    for j in range(4):
+        fetch(("ctx", j), ctx_ref.at[j], pad.at[j, :, pl.ds(3 * head_cols, head_cols)])
+    coming["w1"].wait()
+
+    def first_rows(start, target):
+        def body(i, _):
+            at = pl.ds(pl.multiple_of(start + i * tile, tile), tile)
+            to = pl.ds(pl.multiple_of(i * tile, tile), tile)
+            total = nt(pre[0, at, :], w[1, 0])
+            for j in range(1, 4):
+                total += nt(pre[j, at, :], w[1, j])
+            target[to, :] = total.astype(target.dtype)
+            return 0
+
+        lax.fori_loop(0, own // tile, body, 0)
+
+    first_rows(own, other)
+    share_first = exchange(other, got, 1)
+    share_first.start()
+    first_rows(0, own_part)
+    send_second(2, 0)
+    coming["n1"].wait()
+    share_first.wait_recv()
+
+    def mean(value):
+        return jnp.sum(value, axis=-1, keepdims=True) * (1.0 / value.shape[-1])
+
+    def norm_body(i, _):
+        at = pl.ds(pl.multiple_of(i * small, small), small)
+        grad = gm[at, :] + (own_part[at, :] + got[at, :].astype(f32))
+        normed = n1[at, :]
+        e = grad * vec_ref[1:2, :]
+        value = (e - mean(e) - normed * mean(e * normed)) * inv1_ref[at, :]
+        gm[at, :] = value
+        gaf[at, :] = value.astype(bf16)
+        vz[0, 0:1, :] += jnp.sum(value, axis=0, keepdims=True)
+        vz[0, 1:2, :] += jnp.sum(grad * normed, axis=0, keepdims=True)
+        vz[0, 2:3, :] += jnp.sum(grad, axis=0, keepdims=True)
+        return 0
+
+    lax.fori_loop(0, own // small, norm_body, 0)
+    share_att = exchange(gaf.at[0:own], gaf.at[own : 2 * own], 2)
+    share_att.start()
+    vz[0, 3:6, :] = sums_ref[0:3, :]
+    for j in range(1, 4):
+        vz[j, 0:8, :] = vz[0, 0:8, :]
+    coming["ff"].wait()
+    turn(act, 0, rows // tile)
+    fetch("xf", xf_ref, act)
+    weight_grad(1, 3, lambda: pre[3], every)
+    send_first(1, 3)
+    weight_grad(1, 2, lambda: pre[2], every)
+    send_first(1, 2)
+    send_third(2, 3)
+    weight_grad(1, 1, lambda: pre[1], every)
+    send_first(1, 1)
+    weight_grad(1, 0, lambda: pre[0], every)
+    send_first(1, 0)
+    for j in range(4):
+        fetch(("qkv", j), qkv_ref.at[j], pre.at[j, :, pl.ds(0, 3 * head_cols)])
+    send_third(2, 2)
+    share_att.wait_recv()
+    turn(gaf, 0, rows // tile)
+    coming["w0"].wait()
+    last = slice(3 * head_cols, 4 * head_cols)
+
+    def context_rows(j):
+        def body(i, _):
+            at = pl.ds(pl.multiple_of(i * tile, tile), tile)
+            pre[j, at, last] = nn(gaf[at, :], w[0, j, :, last]).astype(bf16)
+            return 0
+
+        lax.fori_loop(0, rows // tile, body, 0)
+
+    for j in (3, 2, 1, 0):
+        context_rows(j)
+        coming[("ctx", j)].wait()
+        weight_grad(0, j, lambda: pad[j, :, last], last)
+        if j == 2:
+            send_third(2, 1)
+    send_third(2, 0)
+    coming["xf"].wait()
+    turn(act, 0, rows // tile)
+    send_second(1, 3)
+    send_second(1, 2)
+
+    index = lax.broadcasted_iota(jnp.int32, (rows, 1), 0)
+    half = jnp.where(index < own, core, 1 - core)
+    inside = index % own
+    position = (inside // part) * (2 * part) + half * part + inside % part
+    key_bias = jnp.where(position < length_ref[0], 0.0, NEGATIVE).astype(f32)
+    lane = lax.broadcasted_iota(jnp.int32, (1, head_cols), 1)
+    front = slice(0, 3 * head_cols)
+
+    def attend_back(j):
+        keys = pre[j, :, head_cols : 2 * head_cols]
+        keys_t = keys.T
+        values = pre[j, :, 2 * head_cols : 3 * head_cols]
+        dk_acc[...] = jnp.zeros_like(dk_acc)
+        dv_acc[...] = jnp.zeros_like(dv_acc)
+
+        def body(i, _):
+            at = pl.ds(pl.multiple_of(i * tile, tile), tile)
+            query = pre[j, at, 0:head_cols]
+            grad = pre[j, at, last]
+            parts = []
+            for h in range(2):
+                here = lane // HD == h
+                query_h = jnp.where(here, query, jnp.zeros_like(query))
+                grad_h = jnp.where(here, grad, jnp.zeros_like(grad))
+                scores = nt(keys, query_h) + key_bias
+                chances = jnp.exp(scores - lse_ref[2 * j + h, :, at])
+                grad_chances = nt(values, grad_h)
+                inner = jnp.sum(chances * grad_chances, axis=0, keepdims=True)
+                grad_scores = (chances * (grad_chances - inner)).astype(bf16)
+                dv_acc[...] += nn(chances.astype(bf16), grad_h)
+                dk_acc[...] += nn(grad_scores, query_h)
+                parts.append(nn(keys_t[h * HD : (h + 1) * HD], grad_scores))
+            low = jnp.concatenate(parts, axis=0).T.astype(bf16).astype(f32) * HD ** (-0.5)
+            pad[j, at, 0:head_cols] = low.astype(bf16)
+            vz[j, 8:9, 0:head_cols] += jnp.sum(low, axis=0, keepdims=True)
+            return 0
+
+        lax.fori_loop(0, rows // tile, body, 0)
+        pad[j, :, head_cols : 2 * head_cols] = dk_acc[...].astype(bf16)
+        low = dv_acc[...].astype(bf16)
+        pad[j, :, 2 * head_cols : 3 * head_cols] = low
+        vz[j, 8:9, head_cols : 2 * head_cols] = jnp.sum(low.astype(f32), axis=0, keepdims=True)
+
+    for j in (3, 2, 1, 0):
+        coming[("qkv", j)].wait()
+        attend_back(j)
+        if j == 3:
+            send_second(1, 1)
+            send_second(1, 0)
+        weight_grad(0, j, lambda: pad[j, :, front], front)
+        send_first(0, j)
+        if j == 1:
+            send_third(1, 3)
+    for j in range(1, 4):
+        v_copy(j).start()
+    zg[place] = vz[0]
+    send_third(1, 2)
+
+    def input_rows(start, target):
+        def body(i, _):
+            at = pl.ds(pl.multiple_of(start + i * tile, tile), tile)
+            to = pl.ds(pl.multiple_of(i * tile, tile), tile)
+            total = nt(pad[0, at, front], w[0, 0, :, front])
+            for j in range(1, 4):
+                total += nt(pad[j, at, front], w[0, j, :, front])
+            target[to, :] = total.astype(target.dtype)
+            return 0
+
+        lax.fori_loop(0, own // tile, body, 0)
+
+    share_first.wait_send()
+    input_rows(own, other)
+    share_in = exchange(other, got, 3)
+    share_in.start()
+    send_third(1, 1)
+    send_second(0, 3)
+    send_second(0, 2)
+    input_rows(0, own_part)
+    send_third(1, 0)
+    share_in.wait_recv()
+
+    def input_body(i, _):
+        at = pl.ds(pl.multiple_of(i * small, small), small)
+        value = gm[at, :] + (own_part[at, :] + got[at, :].astype(f32))
+        gi_own[at, :] = value.astype(bf16)
+        return 0
+
+    lax.fori_loop(0, own // small, input_body, 0)
+    for s in range(4):
+        @pl.when(is_home(s))
+        def _():
+            back_local(s).start()
+
+        @pl.when(jnp.logical_not(is_home(s)))
+        def _():
+            back(s).start()
+
+    def fold(n, m, arrived, flip):
+        for k in range(4):
+            here = slice(k * piece, (k + 1) * piece)
+            there = slice((k ^ flip) * piece, ((k ^ flip) + 1) * piece)
+            tot[n, 0:8, here] = tot[m, 0:8, here] + arrived[0:8, there]
+        tot[n, 8:16, :] = tot[m, 8:16, :] + arrived[8:16, :]
+
+    for j in range(1, 4):
+        v_got(j).wait_recv()
+    tot[0] = ((zg[0] + zg[1]) + zg[2]) + zg[3]
+    v_x = remote(tot.at[0], xg, e_s.at[4], e_r.at[4], x_side)
+    v_x.start()
+    send_second(0, 1)
+    send_second(0, 0)
+    v_x.wait_recv()
+    fold(1, 0, xg, 1)
+    v_y = remote(tot.at[1], yg, e_s.at[5], e_r.at[5], y_side)
+    v_y.start()
+    send_third(0, 3)
+    v_y.wait_recv()
+    fold(2, 1, yg, 2)
+    v_c = exchange(tot.at[2], cg, 6)
+    v_c.start()
+    send_third(0, 2)
+    send_third(0, 1)
+    send_third(0, 0)
+    v_c.wait_recv()
+    total_ref[0] = tot[2]
+    total_ref[1] = cg[...]
+
+    for b in range(3):
+        for j in range(4):
+            d_copy(b, j).wait_send()
+            x_copy(b, j).wait_send()
+            y_copy(b, j).wait_send()
+            if j > 0:
+                z_copy(b, j).wait_send()
+        home_keep(b).wait()
+        home_copy(b).wait_send()
+        home_copy(b).wait_recv()
+    for j in range(1, 4):
+        v_copy(j).wait_send()
+    for copy in (share_gm, share_att, share_in, v_x, v_y, v_c):
+        copy.wait_send()
+    for s in range(4):
+        @pl.when(jnp.logical_not(is_home(s)))
+        def _():
+            back(s).wait_send()
+    for s in range(4):
+        pltpu.make_async_copy(gi_own.at[0:part], gi_ref.at[s], g_r.at[s]).wait()
+
+
+def backward(w_all, xf, qkv, lse, ctx, ff, hid, dg, n1, inv1, gm, vec, sums, length):
+    rows, width = xf.shape
+    own = rows // 2
+    part = own // 4
+    piece = width // 4
+    cols = hid.shape[2]
+    head_cols = 2 * HD
+    any_ = pl.BlockSpec(memory_space=pltpu.HBM)
+    vm = pl.BlockSpec(memory_space=pltpu.VMEM)
+    sm = pl.BlockSpec(memory_space=pltpu.SMEM)
+    shape = jax.ShapeDtypeStruct
+    dma = pltpu.SemaphoreType.DMA
+    flops = 2 * rows * width * cols * 24 + 40 * rows * rows * HD * 4
+    return pl.pallas_call(
+        backward_kernel,
+        in_specs=[any_, any_, any_, vm, any_, any_, any_, any_, any_, vm, any_, vm, vm, sm],
+        out_specs=[any_, any_, any_, vm],
+        out_shape=[
+            shape((4, part, width), bf16),
+            shape((3, piece // 2, cols), f32),
+            shape((3, piece // 2, cols), f32),
+            shape((2, 16, width), f32),
+        ],
+        scratch_shapes=[
+            pltpu.VMEM((3, 4, width, cols), bf16),
+            pltpu.VMEM((4, width, cols), bf16),
+            pltpu.VMEM((4, rows, cols), bf16),
+            pltpu.VMEM((4, rows, cols), bf16),
+            pltpu.VMEM((rows, width), bf16),
+            pltpu.VMEM((rows, width), bf16),
+            pltpu.VMEM((rows, width), bf16),
+            pltpu.VMEM((width, rows), bf16),
+            pltpu.VMEM((own, width), f32),
+            pltpu.VMEM((own, width), f32),
+            pltpu.VMEM((own, width), f32),
+            pltpu.VMEM((own, width), bf16),
+            pltpu.VMEM((own, width), bf16),
+            pltpu.VMEM((own, width), bf16),
+            pltpu.VMEM((3, 4, piece, cols), bf16),
+            pltpu.VMEM((3, 4, piece, cols), bf16),
+            pltpu.VMEM((3, 4, piece, cols), bf16),
+            pltpu.VMEM((3, 3, piece, cols), bf16),
+            pltpu.VMEM((3, piece, cols), f32),
+            pltpu.VMEM((rows, head_cols), f32),
+            pltpu.VMEM((rows, head_cols), f32),
+            pltpu.VMEM((4, 16, width), f32),
+            pltpu.VMEM((4, 16, width), f32),
+            pltpu.VMEM((16, width), f32),
+            pltpu.VMEM((16, width), f32),
+            pltpu.VMEM((16, width), f32),
+            pltpu.VMEM((3, 16, width), f32),
+            dma((3, 4)), dma((3, 4)), dma((3, 4)), dma((3, 4)), dma((3, 4)), dma((3, 4)),
+            dma((3, 3)), dma((3, 3)), dma((3,)), dma((3,)), dma((3,)), dma((8,)), dma((8,)),
+            dma((4,)), dma((4,)), dma((3,)), dma((4,)), dma((32,)),
+        ],
+        compiler_params=pltpu.CompilerParams(
+            collective_id=1, has_side_effects=True, vmem_limit_bytes=60 << 20
+        ),
+        cost_estimate=pl.CostEstimate(
+            flops=flops, bytes_accessed=60 << 20, transcendentals=8 * rows * rows
+        ),
+        name="backward_layer",
+    )(w_all, xf, qkv, lse, ctx, ff, hid, dg, n1, inv1, gm, vec, sums, length)
+
+
 def swap_cores(value):
     return lax.ppermute(value, "core", SWAP)
 
@@ -838,15 +1337,16 @@
             jnp.broadcast_to(bias_row.astype(f32), (8, bias_row.shape[1])), vec,
         )
         layer_out = reorder(lo_blocks.reshape(seqs, slots_here, width), 2)
-        w_qkv = flat(w_all[0][:, :, : 3 * head_cols])
-        w_o = flat(w_all[0][:, :, 3 * head_cols :])
-        w_1 = flat(w_all[1])
-        w_2 = flat(w_all[2])
-        qkv = flat(qkv4)
-        lse = lse8.reshape(n_t, 2, slots)
-        context = flat(ctx4)
-        hidden = flat(hid4)
-        slope = flat(dg4)
+        gi_blocks, mine, got, totals = backward(
+            w_all, x_full, qkv4, lse8, ctx4, first_full, hid4, dg4, normed_one, inverse_one,
+            grad_mixed, vec, second_sums, length.reshape(1),
+        )
+        grad_inputs = reorder(gi_blocks.reshape(seqs, slots_here, width), 2).astype(f32)
+        mine = jnp.concatenate([mine[0], mine[1], mine[2]], axis=1)
+        got = jnp.concatenate([got[0], got[1], got[2]], axis=1)
+        norms = reorder(totals[0, :6] + totals[1, :6], 1)
+        n_bias = 2 * head_cols + ff_cols
+        biases_out = by_core(totals[0, 8:9, :n_bias], totals[1, 8:9, :n_bias])
     else:
         packed = by_core(keep, swap_cores(give))
         bundle_a = packed[:, : cuts[0]]
@@ -901,61 +1401,87 @@
         grad_second = jnp.where(own_valid, to_chip(cotangent).astype(f32), 0.0)
         grad_mixed = normalize_back(grad_second, gain_second, normed_two, inverse_two)
 
-    grad_mixed_full = both_rows(grad_mixed.astype(bf16))
-    grad_w2 = tn(grad_mixed_full, hidden)
-    grad_pre_low = (nn(grad_mixed_full, w_2) * slope.astype(f32)).astype(bf16)
-    grad_w1 = tn(first_full, grad_pre_low)
-    grad_first = grad_mixed + own_sum(nt(grad_pre_low, w_1))
-    grad_att = normalize_back(grad_first, gain_first, normed_one, inverse_one)
-    grad_att_full = both_rows(grad_att.astype(bf16))
-    grad_context = nn(grad_att_full, w_o).astype(bf16)
-    grad_wo = tn(grad_att_full, context)
-    grad_qkv = attend_bwd(qkv, grad_context, lse, key_bias)
-    grad_qkv = grad_qkv * qkv_scale.astype(bf16)
-    grad_wqkv = tn(x_full, grad_qkv)
-    grad_rows = grad_att + own_sum(nt(grad_qkv, w_qkv))
-    grad_inputs = from_chip(grad_rows.astype(bf16)).astype(f32)
-
-    def scatter(grad):
-        cols = grad.shape[1] // n_t
-        if quad:
-            rows = width // 4
-            blocks = grad.reshape(4, rows, n_t, cols).transpose(0, 2, 1, 3)
-            half = n_t // 2
-            low = lax.ppermute(blocks[3, :half].astype(bf16), "plane", x_pairs)
-            high = lax.ppermute(blocks[3, half:].astype(bf16), "plane", y_pairs)
-            for_y = jnp.concatenate([blocks[2, :half] + low.astype(f32), blocks[2, half:]])
-            for_x = jnp.concatenate([blocks[1, :half], blocks[1, half:] + high.astype(f32)])
-            from_x = lax.ppermute(for_x.astype(bf16), "plane", x_pairs)
-            from_y = lax.ppermute(for_y.astype(bf16), "plane", y_pairs)
-            mine = blocks[0] + from_x.astype(f32) + from_y.astype(f32)
-        else:
-            blocks = grad.reshape(width, n_t, cols).transpose(1, 0, 2)
-            mine = lax.psum_scatter(
-                blocks.astype(bf16), "plane", scatter_dimension=1, tiled=True
-            ).astype(f32)
-        back = [(b, a) for a, b in ring]
-        total = mine[n_t - 1]
-        for j in range(n_t - 2, -1, -1):
-            total = mine[j] + lax.ppermute(total.astype(bf16), "tensor", back).astype(f32)
-        return total
-
-    home_c = scatter(grad_w2)
-    home_b = scatter(grad_w1)
-    grad_a = jnp.concatenate(
-        [
-            grad_wqkv.reshape(width, n_t, 3 * head_cols),
-            grad_wo.reshape(width, n_t, head_cols),
-        ],
-        axis=2,
-    ).reshape(width, -1)
-    home_a = scatter(grad_a)
-    home = jnp.concatenate([home_a, home_b, home_c], axis=1)
-    home = home.reshape(2, -1, home.shape[1])
-    mine = lax.dynamic_index_in_dim(home, core, 0, keepdims=False)
-    other = lax.dynamic_index_in_dim(home, 1 - core, 0, keepdims=False)
-    got = swap_cores(other)
-
+        grad_mixed_full = both_rows(grad_mixed.astype(bf16))
+        grad_w2 = tn(grad_mixed_full, hidden)
+        grad_pre_low = (nn(grad_mixed_full, w_2) * slope.astype(f32)).astype(bf16)
+        grad_w1 = tn(first_full, grad_pre_low)
+        grad_first = grad_mixed + own_sum(nt(grad_pre_low, w_1))
+        grad_att = normalize_back(grad_first, gain_first, normed_one, inverse_one)
+        grad_att_full = both_rows(grad_att.astype(bf16))
+        grad_context = nn(grad_att_full, w_o).astype(bf16)
+        grad_wo = tn(grad_att_full, context)
+        grad_qkv = attend_bwd(qkv, grad_context, lse, key_bias)
+        grad_qkv = grad_qkv * qkv_scale.astype(bf16)
+        grad_wqkv = tn(x_full, grad_qkv)
+        grad_rows = grad_att + own_sum(nt(grad_qkv, w_qkv))
+        grad_inputs = from_chip(grad_rows.astype(bf16)).astype(f32)
+
+        def scatter(grad):
+            cols = grad.shape[1] // n_t
+            if quad:
+                rows = width // 4
+                blocks = grad.reshape(4, rows, n_t, cols).transpose(0, 2, 1, 3)
+                half = n_t // 2
+                low = lax.ppermute(blocks[3, :half].astype(bf16), "plane", x_pairs)
+                high = lax.ppermute(blocks[3, half:].astype(bf16), "plane", y_pairs)
+                for_y = jnp.concatenate([blocks[2, :half] + low.astype(f32), blocks[2, half:]])
+                for_x = jnp.concatenate([blocks[1, :half], blocks[1, half:] + high.astype(f32)])
+                from_x = lax.ppermute(for_x.astype(bf16), "plane", x_pairs)
+                from_y = lax.ppermute(for_y.astype(bf16), "plane", y_pairs)
+                mine = blocks[0] + from_x.astype(f32) + from_y.astype(f32)
+            else:
+                blocks = grad.reshape(width, n_t, cols).transpose(1, 0, 2)
+                mine = lax.psum_scatter(
+                    blocks.astype(bf16), "plane", scatter_dimension=1, tiled=True
+                ).astype(f32)
+            back = [(b, a) for a, b in ring]
+            total = mine[n_t - 1]
+            for j in range(n_t - 2, -1, -1):
+                total = mine[j] + lax.ppermute(total.astype(bf16), "tensor", back).astype(f32)
+            return total
+
+        home_c = scatter(grad_w2)
+        home_b = scatter(grad_w1)
+        grad_a = jnp.concatenate(
+            [
+                grad_wqkv.reshape(width, n_t, 3 * head_cols),
+                grad_wo.reshape(width, n_t, head_cols),
+            ],
+            axis=2,
+        ).reshape(width, -1)
+        home_a = scatter(grad_a)
+        home = jnp.concatenate([home_a, home_b, home_c], axis=1)
+        home = home.reshape(2, -1, home.shape[1])
+        mine = lax.dynamic_index_in_dim(home, core, 0, keepdims=False)
+        other = lax.dynamic_index_in_dim(home, 1 - core, 0, keepdims=False)
+        got = swap_cores(other)
+
+        def row_sum(value):
+            return reorder(jnp.sum(value, axis=0), 0)
+
+        second_rows = [row_sum(grad_mixed), row_sum(grad_second * normed_two), row_sum(grad_second)]
+        norm_sums = jnp.concatenate(
+            [
+                row_sum(grad_att),
+                row_sum(grad_first * normed_one),
+                row_sum(grad_first),
+                *second_rows,
+            ]
+        )
+        qkv_sum = jnp.sum(grad_qkv.astype(f32), axis=0).reshape(n_t, 3 * head_cols)
+        pre_sum = jnp.sum(grad_pre_low.astype(f32), axis=0).reshape(n_t, ff_cols)
+        bias_sum = jnp.concatenate([qkv_sum[:, :head_cols], qkv_sum[:, 2 * head_cols :], pre_sum], axis=1)
+        at_home = lax.rem(place - jnp.arange(n_t) + n_t, n_t)
+        spread = (at_home[:, None] == jnp.arange(n_t)[None]).astype(f32)
+        by_place = jnp.sum(spread[:, :, None] * bias_sum[:, None, :], axis=0)
+        both = jnp.where(
+            (jnp.arange(2) == core)[None, :, None], by_place[:, None, :], 0.0
+        )
+        sums = lax.psum(jnp.concatenate([norm_sums, both.reshape(-1)]), ("plane", "core", "tensor"))
+        norms = sums[: 6 * width].reshape(6, width)
+        biases_out = lax.dynamic_index_in_dim(
+            sums[6 * width :].reshape(n_t, 2, -1), place, 0, keepdims=False
+        )
     def columns(start, cols):
         return by_core(mine[:, start : start + cols], got[:, start : start + cols], axis=1)
 
@@ -966,37 +1492,6 @@
     grad_w_in = columns(cuts[0], ff_cols)
     grad_w_back = columns(cuts[1], ff_cols).T
 
-    def row_sum(value):
-        return reorder(jnp.sum(value, axis=0), 0)
-
-    if quad:
-        second_rows = [reorder(second_sums[i], 0) for i in range(3)]
-    else:
-        second_rows = [
-            row_sum(grad_mixed), row_sum(grad_second * normed_two), row_sum(grad_second)
-        ]
-    norm_sums = jnp.concatenate(
-        [
-            row_sum(grad_att),
-            row_sum(grad_first * normed_one),
-            row_sum(grad_first),
-            *second_rows,
-        ]
-    )
-    qkv_sum = jnp.sum(grad_qkv.astype(f32), axis=0).reshape(n_t, 3 * head_cols)
-    pre_sum = jnp.sum(grad_pre_low.astype(f32), axis=0).reshape(n_t, ff_cols)
-    bias_sum = jnp.concatenate([qkv_sum[:, :head_cols], qkv_sum[:, 2 * head_cols :], pre_sum], axis=1)
-    at_home = lax.rem(place - jnp.arange(n_t) + n_t, n_t)
-    spread = (at_home[:, None] == jnp.arange(n_t)[None]).astype(f32)
-    by_place = jnp.sum(spread[:, :, None] * bias_sum[:, None, :], axis=0)
-    both = jnp.where(
-        (jnp.arange(2) == core)[None, :, None], by_place[:, None, :], 0.0
-    )
-    sums = lax.psum(jnp.concatenate([norm_sums, both.reshape(-1)]), ("plane", "core", "tensor"))
-    norms = sums[: 6 * width].reshape(6, width)
-    biases_out = lax.dynamic_index_in_dim(
-        sums[6 * width :].reshape(n_t, 2, -1), place, 0, keepdims=False
-    )
     grad_b_query = biases_out[:, :head_cols].reshape(-1)
     grad_b_value = biases_out[:, head_cols : 2 * head_cols].reshape(-1)
     grad_b_in = biases_out[:, 2 * head_cols :].reshape(-1)

time: 585 us -> 400 us (0.68)
  Pallas kernels: 202 us -> 356 us
  local copies, waits for them, and re-layouts: 117 us -> 22 us
  starting transfers between devices: 62.8 us -> 0.52 us
  waiting for transfers between devices: 61.8 us -> 0.01 us
  matrix products: 48.1 us -> 0 us
  blocking collectives: 38.4 us -> 0 us
  other arithmetic: 47.9 us -> 19.3 us
    pallas_call x1, Pallas kernels: 25.8 us -> 180 us  [backward(): pl.pallas_call(backward_kernel, in_specs=[any_, any_, any_, vm, any_, any...]
    ppermute x21 -> x0, waiting for transfers between devices: 61.8 us -> none  [the longest x9 23.5 us: scatter(): lax.ppermute(total.astype(bf16), 'tensor', back).astype(f32)]
    ppermute x21 -> x0, starting transfers between devices: 58.5 us -> none  [the longest x9 45.3 us: scatter(): lax.ppermute(total.astype(bf16), 'tensor', back).astype(f32)]
    dot_general x8 -> x0, matrix products: 48.1 us -> none  [the longest x4 26 us: tn(): lax.dot_general(a, b, (((0,), (0,)), ((), ())), preferred_element_type=f32)]
    reshape x10 -> x0, local copies, waits for them, and re-layouts: 42.6 us -> none  [the longest x6 42 us: scatter(): blocks = grad.reshape(4, rows, n_t, cols).transpose(0, 2, 1, 3)]
    psum x1 -> x0, blocking collectives: 38.4 us -> none  [on_device(): lax.psum(jnp.concatenate([norm_sums, both.reshape(-1)]), ('plane', 'core'...]
    squeeze x13 -> x0, local copies, waits for them, and re-layouts: 15.2 us -> none  [the longest x7 9.87 us: flat(): return jnp.concatenate([gathered[j] for j in range(n_t)], axis=1)]
    concatenate x5 -> x0, local copies, waits for them, and re-layouts: 15.1 us -> none  [the longest x4 15 us: on_device(): jnp.concatenate([grad_wqkv.reshape(width, n_t, 3 * head_cols), grad_wo.re...]
  transfers between devices with their start and end apart: 29 -> 1, of which waited for: 14 -> 0; matrix products, arithmetic and copies ran while one was open for 28% -> 6% of each run, Pallas kernels for 4% -> 0%
where the time goes in v3:
time: 400 us; the launch traced here: 399 us
  Pallas kernels  356 us (89%)
  local copies, waits for them, and re-layouts  22 us (6%)
  other arithmetic  19.3 us (5%)
    pallas_call x1, Pallas kernels, backward(): pl.pallas_call(backward_kernel, in_specs=[any_, any_, any_, vm, any_, any...  180 us
    pallas_call x1, Pallas kernels, forward(): pl.pallas_call(forward_kernel, in_specs=[sm, any_, any_, any_, any_, vm,...  176 us
  transfers between devices with their start and end apart: 1, of which 0 were waited for; matrix products, arithmetic and copies ran while one was open for 6% of the time, Pallas kernels for 0%

profile of v3, /device:TPU:0, one launch (start us, length us, event | category | flops | bytes accessed | tf_op | source)
XLA Modules:
  0.0 399.1 jit_solution(5923121791874792446)
XLA Ops:
  0.7 0.5 collective-permute-start
  1.2 0.7 dynamic_slice.210
  1.9 0.7 dynamic_slice.211
  2.6 0.9 fusion.8
  3.6 0.9 fusion.7
  4.5 0.9 fusion.6
  5.5 0.9 fusion.5
  6.5 0.9 fusion.4
  7.4 0.9 fusion.3
  8.6 0.6 stack.46.vec_ref
  9.2 1.4 constant_dynamic-slice_fusion.12
  10.6 1.5 constant_dynamic-slice_fusion.11
  12.1 1.4 constant_dynamic-slice_fusion.10
  13.5 0.8 constant_dynamic-slice_fusion.9
  14.2 0.7 copy.43
  15.0 0.7 copy.41
  15.7 0.8 dynamic_slice.212
  16.4 1.6 dynamic-slice_bitcast_fusion
  18.1 1.0 constant_dynamic-slice_fusion.8
  19.3 0.1 constant_dynamic-slice_fusion.25
  19.5 0.1 constant_dynamic-slice_fusion.21
  19.6 0.8 maximum_bitcast_fusion.2
  20.5 1.7 pad_maximum_fusion.5.give_ref
  22.2 0.8 maximum_bitcast_fusion.1
  23.0 0.8 pad_maximum_fusion.4.keep_ref
  23.8 1.1 pad_maximum_fusion
  24.9 1.1 pad_maximum_fusion.1
  26.1 0.6 dynamic_slice.189.length_ref
  26.7 0.6 broadcast_in_dim.2.bias_in_ref
  27.3 176.1 %forward_layer.1 = (bf16[3,4,1024,512]{3,2,1,0:T(8,128)(2,1)}, bf16[1024,1024]{1,0:T(8,128)(2,1)}, bf16[4,1024,384]{2,1,0:T(8,128)(2,1)}, f32[8,1,1024]{2,1,0:T(...) custom-call(s32[1]{0:T(128)} %dynamic_slice.189.length_ref, ...), custom_call_target="tpu_custom_call" | custom-call | flops 17179869184 | bytes 62914560 | tf_op jit(solution)/shard_map/forward_layer/pallas_call | solution.py:627
  203.4 180.0 %backward_layer.1 = (bf16[4,128,1024]{2,1,0:T(8,128)(2,1)}, f32[3,128,512]{2,1,0:T(8,128)}, f32[3,128,512]{2,1,0:T(8,128)}, f32[2,16,1024]{2,1,0:T(8,128)}) custom-call(bf16[3,4,1024,512]{3,2,1,0:T(8,128)(2,1)} %get-tuple-element.35.w_ref, bf16[1024,1024]{1,0:T(8,128)(2,1)} %get-tuple-element.36.xf_ref, bf16[4,1024,384]{2,1,0:T(8,128)(2,1)} %get-tuple-element.37.qkv_ref, ...), custom_call_target="tpu_custom_call" | custom-call | flops 36507222016 | bytes 62914560 | tf_op jit(solution)/shard_map/backward_layer/pallas_call | solution.py:1125
  383.5 0.8 fusion.1
  384.2 0.8 slice_add_fusion
  385.0 0.6 maximum_bitcast_fusion.4
  385.6 0.6 pad_maximum_fusion.16
  386.2 0.6 pad_maximum_fusion.9
  386.8 0.6 copy.45
  387.4 2.3 select_bitcast_fusion.1
  389.7 0.7 slice_select_fusion.1
  390.4 0.7 pad_maximum_fusion.8
  391.0 0.8 copy.39
  391.8 1.8 pad_maximum_fusion.3
  393.6 1.0 copy.40
  394.6 0.3 constant_dynamic-slice_fusion.3
  394.9 0.5 copy-done.4
  395.5 0.7 pad_maximum_fusion.6
  396.2 1.6 maximum_convert_fusion
  397.8 1.1 pad_maximum_fusion.2
  (52 shorter events, 0.6 us)
Async XLA Ops:
  0.7 18.6 %copy-start = (bf16[2,256,1024]{2,1,0:T(8,128)(2,1)S(1)}, bf16[2,256,1024]{2,1,0:T(8,128)(2,1)}, u32[]{:S(2)}) copy-start(bf16[2,256,1024]{2,1,0:T(8,128)(2,1)} %param.18) | copy-start | bytes 3145732
  0.7 25.4 %collective-permute-start = (s32[2]{0:T(128)}, s32[2]{0:T(128)S(1)}, u32[]{:S(2)}, u32[]{:S(2)}) collective-permute-start(s32[2]{0:T(128)} %param.19), channel_id=1, source_target_pairs={{0,4},{4,0},{1,5},{5,1},{2,6},{6,2},{3,7},{7,3},{8,12},{12,8},{9,1... | collective-permute-start | bytes 32 | tf_op jit(solution)/shard_map/ppermute | solution.py:1178
  10.6 8.9 %copy-start.1 = (bf16[2,256,1024]{2,1,0:T(8,128)(2,1)S(1)}, bf16[2,256,1024]{2,1,0:T(8,128)(2,1)}, u32[]{:S(2)}) copy-start(bf16[2,256,1024]{2,1,0:T(8,128)(2,1)} %param.35) | copy-start | bytes 3145732
  23.8 2.2 copy-start.6
  390.4 4.3 %copy-start.2 = (bf16[4,128,1024]{2,1,0:T(8,128)(2,1)S(1)}, bf16[4,128,1024]{2,1,0:T(8,128)(2,1)}, u32[]{:S(2)}) copy-start(bf16[4,128,1024]{2,1,0:T(8,128)(2,1)} %get-tuple-element.34) | copy-start | bytes 3145732
  390.4 4.3 %copy-start.3 = (bf16[4,128,1024]{2,1,0:T(8,128)(2,1)S(1)}, bf16[4,128,1024]{2,1,0:T(8,128)(2,1)}, u32[]{:S(2)}) copy-start(bf16[4,128,1024]{2,1,0:T(8,128)(2,1)} %get-tuple-element.47) | copy-start | bytes 3145732
  394.6 0.8 copy-start.4
  394.6 0.9 copy-start.5

commit v4 on v3

--- a/solution.py
+++ b/solution.py
@@ -161,12 +161,13 @@
 
 
 def forward_kernel(
-    length_ref, xp_ref, cp_ref, keep_ref, give_ref, bias_in_ref, vec_ref,
+    lens_ref, row_ref, x_ref, c_ref, wq_ref, wk_ref, wv_ref, wo_ref, wi_ref, wb_ref,
     w_out, xf_out, qkv_out, lse_ref, ctx_out, ff_out, hid_out, dg_out, n1_out, inv1_ref, gm_ref,
-    lo_ref, sums_ref,
-    w, xf, bias, qkv, ctx, ff, hid, dg, n1, first, other_part, own_part, att_got, mix_got, cot, lo_own,
-    z_s, z_r, x_s, x_r, y_s, y_r, f_s, f_r, pre_l, pre_s, pre_r, b_s, b_r,
-    xa_s, xa_r, ca_s, ca_r, la_s, la_r, e_s, e_r, o_s,
+    lo_ref, sums_ref, vec_ref, length_ref,
+    w, xs, xf, bias, qkv, ctx, ff, hid, dg, n1, first, other_acc, other_part, own_part, att_got, mix_got, cot,
+    wo_here, wb_here, wo_give, wb_give, lens,
+    z_s, z_r, zl_s, zl_r, x_s, x_r, y_s, y_r, f_s, f_r, pre_l, pre_s, pre_r, b_s, b_r,
+    xa_s, xa_r, ca_s, ca_r, e_s, e_r, o_s,
 ):
     plane = lax.axis_index("plane")
     core = lax.axis_index("core")
@@ -174,7 +175,11 @@
     partner = {"core": 1 - core}
     x_side = {"plane": plane + 1 - 2 * (plane % 2)}
     y_side = {"plane": (plane + 2) % 4}
-    z_next = {"tensor": (place + 1) % 4}
+    z_right = {"tensor": (place + 1) % 4}
+    z_left = {"tensor": (place + 3) % 4}
+    first_end = (3 - place) // 3
+    last_end = place // 3
+    turns = (0, 1 + 2 * first_end, 3 - first_end - last_end, 2 - first_end + last_end)
     rows = xf.shape[0]
     own = rows // 2
     part = own // 4
@@ -185,42 +190,114 @@
             source, target, send, recv, device_id=to, device_id_type=MESH
         )
 
-    def z_copy(b, s):
+    def right_copy(b, n):
         return remote(
-            w.at[b, s, 0:piece], w.at[b, s + 1, 0:piece], z_s.at[b, s], z_r.at[b, s], z_next
-        )
-
-    def x_copy(b, j):
+            w.at[b, n - 1, 0:piece], w.at[b, n, 0:piece], z_s.at[b, n - 1], z_r.at[b, n - 1], z_right
+        )
+
+    def left_copy(b, n):
         return remote(
-            w.at[b, j, 0:piece], w.at[b, j, piece : 2 * piece], x_s.at[b, j], x_r.at[b, j], x_side
-        )
-
-    def y_copy(b, j):
+            w.at[b, (5 - n) % 4, 0:piece], w.at[b, 4 - n, 0:piece],
+            zl_s.at[b, n - 1], zl_r.at[b, n - 1], z_left,
+        )
+
+    def line_do(b, n, act):
+        @pl.when(jnp.logical_and(place <= 2, place >= n - 1))
+        def _():
+            act(right_copy(b, n))
+
+        @pl.when(jnp.logical_and(place >= 1, place + n <= 4))
+        def _():
+            act(left_copy(b, n))
+
+    def line_start(b, n):
+        line_do(b, n, lambda copy: copy.start())
+
+    def line_wait(b, n):
+        @pl.when(place >= n)
+        def _():
+            right_copy(b, n).wait_recv()
+
+        @pl.when(place + n <= 3)
+        def _():
+            left_copy(b, n).wait_recv()
+
+    def x_copy(b, n):
+        j = turns[n]
         return remote(
-            w.at[b, j, 0:piece], w.at[b, j, 2 * piece : 3 * piece], y_s.at[b, j], y_r.at[b, j], y_side
-        )
-
-    def f_copy(b, j):
-        start = 2 * piece if j < 2 else piece
+            w.at[b, j, 0:piece], w.at[b, j, piece : 2 * piece], x_s.at[b, n], x_r.at[b, n], x_side
+        )
+
+    def y_copy(b, n):
+        j = turns[n]
         return remote(
-            w.at[b, j, start : start + piece],
-            w.at[b, j, 3 * piece : 4 * piece],
-            f_s.at[b, j],
-            f_r.at[b, j],
-            x_side if j < 2 else y_side,
-        )
-
-    def pre_copy(b):
-        rows_at = pl.ds(core * (piece // 2), piece // 2)
-        return remote(give_ref.at[b], w.at[b, 0, rows_at], pre_s.at[b], pre_r.at[b], partner)
-
-    def pre_got(b):
-        rows_at = pl.ds((1 - core) * (piece // 2), piece // 2)
-        return remote(give_ref.at[b], w.at[b, 0, rows_at], pre_s.at[b], pre_r.at[b], partner)
-
-    def keep_copy(b):
-        rows_at = pl.ds(core * (piece // 2), piece // 2)
-        return pltpu.make_async_copy(keep_ref.at[b], w.at[b, 0, rows_at], pre_l.at[b])
+            w.at[b, j, 0:piece], w.at[b, j, 2 * piece : 3 * piece], y_s.at[b, n], y_r.at[b, n], y_side
+        )
+
+    def fx_copy(b, n):
+        j, half = turns[n], piece // 2
+        return remote(
+            w.at[b, j, 2 * piece : 2 * piece + half], w.at[b, j, 3 * piece : 3 * piece + half],
+            f_s.at[b, n, 0], f_r.at[b, n, 0], x_side,
+        )
+
+    def fy_copy(b, n):
+        j, half = turns[n], piece // 2
+        return remote(
+            w.at[b, j, piece + half : 2 * piece], w.at[b, j, 3 * piece + half : 4 * piece],
+            f_s.at[b, n, 1], f_r.at[b, n, 1], y_side,
+        )
+
+    def cross(b, n):
+        x_copy(b, n).start()
+        y_copy(b, n).start()
+
+    def forward_on(b, n):
+        y_copy(b, n).wait_recv()
+        fx_copy(b, n).start()
+        x_copy(b, n).wait_recv()
+        fy_copy(b, n).start()
+
+    def ready(b, n):
+        fx_copy(b, n).wait_recv()
+        fy_copy(b, n).wait_recv()
+        save(w.at[b, turns[n]], w_out.at[b, turns[n]])
+
+    half_piece = piece // 2
+    head_cols = 2 * HD
+    mine_at = pl.ds(core * half_piece, half_piece)
+    theirs_at = pl.ds((1 - core) * half_piece, half_piece)
+    cols = w.shape[3]
+
+    def head_half(which):
+        return pl.ds(pl.multiple_of(which * head_cols, head_cols), head_cols)
+
+    def wide_half(which):
+        return pl.ds(pl.multiple_of(which * cols, cols), cols)
+
+    def keep_copy(n):
+        if n < 3:
+            source = (wq_ref, wk_ref, wv_ref)[n].at[:, head_half(core)]
+            target = w.at[0, 0, mine_at, n * head_cols : (n + 1) * head_cols]
+        elif n == 3:
+            source, target = wo_ref, wo_here
+        elif n == 4:
+            source, target = wi_ref.at[:, wide_half(core)], w.at[1, 0, mine_at]
+        else:
+            source, target = wb_ref, wb_here
+        return pltpu.make_async_copy(source, target, pre_l.at[n])
+
+    def pre_copy(n, at):
+        if n < 3:
+            source = (wq_ref, wk_ref, wv_ref)[n].at[:, head_half(1 - core)]
+            target = w.at[0, 0, at, n * head_cols : (n + 1) * head_cols]
+        elif n == 3:
+            source, target = wo_give, w.at[0, 0, at, 3 * head_cols : 4 * head_cols]
+        elif n == 4:
+            source, target = wi_ref.at[:, wide_half(1 - core)], w.at[1, 0, at]
+        else:
+            source, target = wb_give, w.at[2, 0, at]
+        return remote(source, target, pre_s.at[n], pre_r.at[n], partner)
 
     def bias_copy(s):
         return remote(
@@ -231,12 +308,15 @@
         at = pl.ds(place * part, part)
         to = {"core": h, "tensor": 2 * core + l}
         return remote(
-            source.at[2 * l + h], target.at[at], send.at[2 * l + h], recv.at[place], to
+            source.at[l, h * part : (h + 1) * part], target.at[at], send.at[2 * l + h],
+            recv.at[place], to,
         )
 
     def spread_local(source, target, recv, l, h):
         at = pl.ds(place * part, part)
-        return pltpu.make_async_copy(source.at[2 * l + h], target.at[at], recv.at[place])
+        return pltpu.make_async_copy(
+            source.at[l, h * part : (h + 1) * part], target.at[at], recv.at[place]
+        )
 
     def is_here(l, h):
         return jnp.logical_and(core == h, place == 2 * core + l)
@@ -255,7 +335,7 @@
     def spread_wait(source, target, recv):
         for s in range(4):
             pltpu.make_async_copy(
-                source.at[s], target.at[s * part : (s + 1) * part], recv.at[s]
+                source.at[0, 0:part], target.at[s * part : (s + 1) * part], recv.at[s]
             ).wait()
 
     def spread_sent(source, target, send, recv):
@@ -264,26 +344,6 @@
                 @pl.when(jnp.logical_not(is_here(l, h)))
                 def _():
                     spread(source, target, send, recv, l, h).wait_send()
-
-    def home(s):
-        to = {"core": place // 2, "tensor": s}
-        return remote(
-            lo_own.at[s * part : (s + 1) * part],
-            lo_ref.at[2 * (place % 2) + core],
-            la_s.at[s],
-            la_r.at[2 * (place % 2) + core],
-            to,
-        )
-
-    def home_local(s):
-        return pltpu.make_async_copy(
-            lo_own.at[s * part : (s + 1) * part],
-            lo_ref.at[2 * (place % 2) + core],
-            la_r.at[2 * (place % 2) + core],
-        )
-
-    def is_home(s):
-        return jnp.logical_and(core == place // 2, place == s)
 
     def exchange(source, target, n):
         return remote(source, target, e_s.at[n], e_r.at[n], partner)
@@ -302,72 +362,88 @@
         friends.append({"tensor": (place + s) % 4, "core": 1 - core})
     for friend in friends:
         pl.semaphore_signal(barrier, inc=1, device_id=friend, device_id_type=MESH)
-    keep_all = [keep_copy(b) for b in range(3)]
-    for copy in keep_all:
-        copy.start()
+    for n in (3, 0, 1, 2, 4, 5):
+        keep_copy(n).start()
     pl.semaphore_wait(barrier, len(friends))
 
-    for b in range(3):
-        pre_copy(b).start()
-    bias[0] = bias_in_ref[...]
-    spread_start(xp_ref, xf, xa_s, xa_r)
-    keep_all[0].wait()
-    pre_got(0).wait_recv()
-    z_copy(0, 0).start()
-    x_copy(0, 0).start()
-    y_copy(0, 0).start()
+    def block_at(k):
+        number = (plane, plane + 1 - 2 * (plane % 2), (plane + 2) % 4, 3 - plane)[k]
+        return pl.ds(pl.multiple_of(number * piece, piece), piece)
+
+    for n in range(3):
+        pre_copy(n, mine_at).start()
+    keep_copy(3).wait()
+    wo_give[...] = wo_here[head_half(1 - core), :].T
+    pre_copy(3, mine_at).start()
+    w[0, 0, mine_at, 3 * head_cols : 4 * head_cols] = wo_here[head_half(core), :].T
+    pre_copy(4, mine_at).start()
+    for n in range(3):
+        keep_copy(n).wait()
+    for n in range(4):
+        pre_copy(n, theirs_at).wait_recv()
+    line_start(0, 1)
+    cross(0, 0)
+    spread_start(x_ref, xs, xa_s, xa_r)
+    keep_copy(5).wait()
+    wb_give[...] = wb_here[wide_half(1 - core), :].T
+    pre_copy(5, mine_at).start()
+    w[2, 0, mine_at, :] = wb_here[wide_half(core), :].T
+    keep_copy(4).wait()
+    pre_copy(4, theirs_at).wait_recv()
+    cross(1, 0)
+    pre_copy(5, theirs_at).wait_recv()
+    cross(2, 0)
+
+    zero_row = jnp.zeros((1, head_cols), f32)
+    heads_q = jnp.where(core == 0, row_ref[7:8, 0:head_cols], row_ref[7:8, head_cols : 2 * head_cols])
+    heads_v = jnp.where(
+        core == 0, row_ref[7:8, 2 * head_cols : 3 * head_cols], row_ref[7:8, 3 * head_cols : 4 * head_cols]
+    )
+    wide = jnp.where(core == 0, row_ref[6:7, 0:cols], row_ref[6:7, cols : 2 * cols])
+    bias[0, 0:1, :] = jnp.concatenate([heads_q, zero_row, heads_v, zero_row, wide], axis=1)
+    for k in range(4):
+        vec_ref[:, k * piece : (k + 1) * piece] = row_ref[:, block_at(k)]
     for s in range(1, 4):
         bias_copy(s).start()
-    for b in (1, 2):
-        keep_all[b].wait()
-        pre_got(b).wait_recv()
-        x_copy(b, 0).start()
-        y_copy(b, 0).start()
-    z_copy(0, 0).wait_recv()
-    z_copy(0, 1).start()
-    x_copy(0, 1).start()
-    y_copy(0, 1).start()
-    y_copy(0, 0).wait_recv()
-    f_copy(0, 0).start()
-    z_copy(0, 1).wait_recv()
-    z_copy(0, 2).start()
-    x_copy(0, 2).start()
-    y_copy(0, 2).start()
-    z_copy(0, 2).wait_recv()
-    z_copy(1, 0).start()
-    z_copy(2, 0).start()
-    x_copy(0, 3).start()
-    y_copy(0, 3).start()
-
-    spread_wait(xp_ref, xf, xa_r)
+    lens[core] = lens_ref[...]
+    share_len = remote(lens_ref, lens.at[core], e_s.at[4], e_r.at[4], partner)
+    share_len.start()
+
+    line_wait(0, 1)
+    line_start(0, 2)
+    line_start(1, 1)
+    forward_on(0, 0)
+    cross(0, 1)
+    forward_on(1, 0)
+    forward_on(2, 0)
+    for s in range(1, 4):
+        bias_copy(s).wait_recv()
+    remote(lens_ref, lens.at[1 - core], e_s.at[4], e_r.at[4], partner).wait_recv()
+
+    spread_wait(x_ref, xs, xa_r)
+    for k in range(4):
+        xf[0:own, k * piece : (k + 1) * piece] = xs[:, block_at(k)]
     share_x = exchange(xf.at[0:own], xf.at[own : 2 * own], 0)
     share_x.start()
-    y_copy(0, 1).wait_recv()
-    f_copy(0, 1).start()
-    y_copy(1, 0).wait_recv()
-    f_copy(1, 0).start()
-    y_copy(2, 0).wait_recv()
-    f_copy(2, 0).start()
-    for s in range(1, 4):
-        bias_copy(s).wait_recv()
     share_x.wait_recv()
     save(xf, xf_out)
 
     index = lax.broadcasted_iota(jnp.int32, (rows, 1), 0)
-    length = length_ref[0]
+    length_ref[...] = lens[place // 2]
+    length = length_ref[pl.ds(place % 2, 1), 0:1]
     half = jnp.where(index < own, core, 1 - core)
     inside = index % own
     position = (inside // part) * (2 * part) + half * part + inside % part
-    key_bias = jnp.where(position < length, 0.0, NEGATIVE).astype(f32)
+    key_bias = jnp.where(position.astype(f32) < length, 0.0, NEGATIVE).astype(f32)
     lane = lax.broadcasted_iota(jnp.int32, (1, 2 * HD), 1)
-    head_cols = 2 * HD
     tile = 256
 
-    def project(j):
+    def project(n):
+        j = turns[n]
         columns = lax.broadcasted_iota(jnp.int32, (1, 3 * head_cols), 1)
         zero = jnp.zeros((1, head_cols), f32)
         add = jnp.concatenate(
-            [bias[j, 0:1, 0:head_cols], zero, bias[j, 0:1, head_cols : 2 * head_cols]], axis=1
+            [bias[j, 0:1, 0:head_cols], zero, bias[j, 0:1, 2 * head_cols : 3 * head_cols]], axis=1
         )
         times = jnp.where(columns < head_cols, HD ** (-0.5), 1.0).astype(f32)
 
@@ -380,7 +456,8 @@
         lax.fori_loop(0, rows // tile, body, 0)
         save(qkv.at[j], qkv_out.at[j])
 
-    def attend(j):
+    def attend(n):
+        j = turns[n]
         keys = qkv[j, :, head_cols : 2 * head_cols]
         values_t = qkv[j, :, 2 * head_cols : 3 * head_cols].T
 
@@ -403,52 +480,41 @@
         lax.fori_loop(0, rows // tile, body, 0)
         save(ctx.at[j], ctx_out.at[j])
 
-    def ready(b, j):
-        x_copy(b, j).wait_recv() if not (b, j, "x") in seen else None
-        seen.add((b, j, "x"))
-        y_copy(b, j).wait_recv() if not (b, j, "y") in seen else None
-        seen.add((b, j, "y"))
-        f_copy(b, j).wait_recv()
-        save(w.at[b, j], w_out.at[b, j])
-
-    seen = {(0, 0, "y"), (0, 1, "y"), (1, 0, "y"), (2, 0, "y")}
-
-    def forward_on(b, j):
-        side = "y" if j < 2 else "x"
-        (y_copy if j < 2 else x_copy)(b, j).wait_recv()
-        seen.add((b, j, side))
-        f_copy(b, j).start()
-
     ready(0, 0)
     project(0)
+    line_wait(0, 2)
+    line_start(0, 3)
+    line_start(2, 1)
+    cross(0, 2)
     attend(0)
-    forward_on(0, 2)
-    z_copy(1, 0).wait_recv()
-    z_copy(1, 1).start()
-    x_copy(1, 1).start()
-    y_copy(1, 1).start()
-    forward_on(0, 3)
-    z_copy(2, 0).wait_recv()
-    z_copy(2, 1).start()
+    forward_on(0, 1)
+    line_wait(1, 1)
+    line_start(1, 2)
     ready(0, 1)
     project(1)
+    line_wait(0, 3)
+    cross(0, 3)
+    cross(1, 1)
     attend(1)
-    z_copy(1, 1).wait_recv()
-    z_copy(1, 2).start()
-    x_copy(1, 2).start()
-    y_copy(1, 2).start()
+    forward_on(0, 2)
+    line_wait(2, 1)
+    line_start(2, 2)
     ready(0, 2)
     project(2)
+    line_wait(1, 2)
+    line_start(1, 3)
+    cross(1, 2)
     attend(2)
-    z_copy(2, 1).wait_recv()
-    z_copy(2, 2).start()
+    forward_on(0, 3)
     forward_on(1, 1)
     ready(0, 3)
     project(3)
+    line_wait(2, 2)
+    line_start(2, 3)
     attend(3)
-    z_copy(1, 2).wait_recv()
-    x_copy(1, 3).start()
-    y_copy(1, 3).start()
+    line_wait(1, 3)
+    cross(1, 3)
+    cross(2, 1)
     forward_on(1, 2)
 
     def out_rows(start, target):
@@ -458,7 +524,7 @@
             total = nt(ctx[0, at, :], w[0, 0, :, 3 * head_cols :])
             for j in range(1, 4):
                 total += nt(ctx[j, at, :], w[0, j, :, 3 * head_cols :])
-            target[to, :] = total
+            target[to, :] = total.astype(target.dtype)
             return 0
 
         lax.fori_loop(0, own // tile, body, 0)
@@ -467,9 +533,10 @@
     share_att = exchange(other_part, att_got, 1)
     share_att.start()
     out_rows(0, own_part)
-    x_copy(2, 1).start()
-    y_copy(2, 1).start()
-    spread_start(cp_ref, cot, ca_s, ca_r)
+    line_wait(2, 3)
+    spread_start(c_ref, cot, ca_s, ca_r)
+    cross(2, 2)
+    cross(2, 3)
     share_att.wait_recv()
     small = 32
 
@@ -478,7 +545,7 @@
 
     def first_body(i, _):
         at = pl.ds(pl.multiple_of(i * small, small), small)
-        total = xf[at, :].astype(f32) + (own_part[at, :] + att_got[at, :]) + vec_ref[0:1, :]
+        total = xf[at, :].astype(f32) + (own_part[at, :] + att_got[at, :].astype(f32)) + vec_ref[0:1, :]
         centered = total - mean(total)
         inverse = lax.rsqrt(mean(centered * centered) + EPSILON)
         normed = centered * inverse
@@ -494,15 +561,12 @@
     share_first.start()
     save(n1, n1_out)
     forward_on(1, 3)
-    z_copy(2, 2).wait_recv()
-    for j in (2, 3):
-        x_copy(2, j).start()
-        y_copy(2, j).start()
     share_first.wait_recv()
     save(ff, ff_out)
 
-    def expand(j):
-        add = bias[j, 0:1, 2 * head_cols :]
+    def expand(n):
+        j = turns[n]
+        add = bias[j, 0:1, 4 * head_cols : 4 * head_cols + cols]
 
         def body(i, _):
             at = pl.ds(pl.multiple_of(i * tile, tile), tile)
@@ -523,37 +587,39 @@
     forward_on(2, 1)
     ready(1, 2)
     expand(2)
-    forward_on(2, 2)
     ready(1, 3)
     expand(3)
+    forward_on(2, 2)
     share_att.wait_send()
 
-    def contract(js, start, target, fresh):
+    def contract(ns, start, target, source):
         def body(i, _):
             at = pl.ds(pl.multiple_of(start + i * tile, tile), tile)
             to = pl.ds(pl.multiple_of(i * tile, tile), tile)
-            total = nt(hid[js[0], at, :], w[2, js[0]])
-            for j in js[1:]:
-                total += nt(hid[j, at, :], w[2, j])
-            target[to, :] = total if fresh else target[to, :] + total
+            total = nt(hid[turns[ns[0]], at, :], w[2, turns[ns[0]]])
+            for n in ns[1:]:
+                total += nt(hid[turns[n], at, :], w[2, turns[n]])
+            if source is not None:
+                total += source[to, :]
+            target[to, :] = total.astype(target.dtype)
             return 0
 
         lax.fori_loop(0, own // tile, body, 0)
 
     ready(2, 0)
     ready(2, 1)
-    contract((0, 1), own, other_part, True)
-    contract((0, 1), 0, own_part, True)
+    contract((0, 1), own, other_acc, None)
+    contract((0, 1), 0, own_part, None)
     forward_on(2, 3)
     ready(2, 2)
-    contract((2,), own, other_part, False)
-    contract((2,), 0, own_part, False)
+    contract((2,), own, other_acc, other_acc)
+    contract((2,), 0, own_part, own_part)
     ready(2, 3)
-    contract((3,), own, other_part, False)
+    contract((3,), own, other_part, other_acc)
     share_mix = exchange(other_part, mix_got, 3)
     share_mix.start()
-    contract((3,), 0, own_part, False)
-    spread_wait(cp_ref, cot, ca_r)
+    contract((3,), 0, own_part, own_part)
+    spread_wait(c_ref, cot, ca_r)
     share_mix.wait_recv()
     sums_ref[...] = jnp.zeros_like(sums_ref)
 
@@ -561,14 +627,17 @@
         at = pl.ds(pl.multiple_of(i * small, small), small)
         spot = i * small + lax.broadcasted_iota(jnp.int32, (small, 1), 0)
         where = (spot // part) * (2 * part) + core * part + spot % part
-        alive = where < length
-        total = first[at, :] + (own_part[at, :] + mix_got[at, :]) + vec_ref[3:4, :]
+        alive = where.astype(f32) < length
+        total = first[at, :] + (own_part[at, :] + mix_got[at, :].astype(f32)) + vec_ref[3:4, :]
         centered = total - mean(total)
         inverse = lax.rsqrt(mean(centered * centered) + EPSILON)
         normed = centered * inverse
         value = normed * vec_ref[4:5, :] + vec_ref[5:6, :]
-        lo_own[at, :] = jnp.where(alive, value, 0.0).astype(bf16)
-        grad = jnp.where(alive, cot[at, :].astype(f32), 0.0)
+        shown = jnp.where(alive, value, 0.0).astype(bf16)
+        for k in range(4):
+            lo_ref[at, block_at(k)] = shown[:, k * piece : (k + 1) * piece]
+        given = jnp.concatenate([cot[at, block_at(k)] for k in range(4)], axis=1)
+        grad = jnp.where(alive, given.astype(f32), 0.0)
         e = grad * vec_ref[4:5, :]
         back = (e - mean(e) - normed * mean(e * normed)) * inverse
         gm_ref[at, :] = back
@@ -578,56 +647,45 @@
         return 0
 
     lax.fori_loop(0, own // small, second_body, 0)
-    for s in range(4):
-        @pl.when(is_home(s))
-        def _():
-            home_local(s).start()
-
-        @pl.when(jnp.logical_not(is_home(s)))
-        def _():
-            home(s).start()
-
+    for n in range(6):
+        pre_copy(n, mine_at).wait_send()
+    share_len.wait_send()
     for b in range(3):
-        pre_copy(b).wait_send()
-        for s in range(3):
-            z_copy(b, s).wait_send()
-        for j in range(4):
-            x_copy(b, j).wait_send()
-            y_copy(b, j).wait_send()
-            f_copy(b, j).wait_send()
+        for n in range(1, 4):
+            line_do(b, n, lambda copy: copy.wait_send())
+        for n in range(4):
+            x_copy(b, n).wait_send()
+            y_copy(b, n).wait_send()
+            fx_copy(b, n).wait_send()
+            fy_copy(b, n).wait_send()
     for s in range(1, 4):
         bias_copy(s).wait_send()
-    spread_sent(xp_ref, xf, xa_s, xa_r)
-    spread_sent(cp_ref, cot, ca_s, ca_r)
+    spread_sent(x_ref, xs, xa_s, xa_r)
+    spread_sent(c_ref, cot, ca_s, ca_r)
     share_x.wait_send()
     share_first.wait_send()
     share_mix.wait_send()
     for copy in outs:
         copy.wait()
-    for s in range(4):
-        @pl.when(jnp.logical_not(is_home(s)))
-        def _():
-            home(s).wait_send()
-    for s in range(4):
-        pltpu.make_async_copy(lo_own.at[0:part], lo_ref.at[s], la_r.at[s]).wait()
-
-
-def forward(length, xp, cp, keep, give, bias, vec):
-    part, width = xp.shape[1:]
+
+
+def forward(lens, row, inputs, cotangent, w_query, w_key, w_value, w_out, w_in, w_back):
+    part, width = inputs.shape[1] // 2, inputs.shape[2]
     own = 4 * part
     rows = 2 * own
-    cols = keep.shape[2]
+    cols = w_in.shape[1] // 2
     head_cols = 2 * HD
     any_ = pl.BlockSpec(memory_space=pltpu.HBM)
     vm = pl.BlockSpec(memory_space=pltpu.VMEM)
-    sm = pl.BlockSpec(memory_space=pltpu.SMEM)
     shape = jax.ShapeDtypeStruct
     dma = pltpu.SemaphoreType.DMA
     flops = 2 * rows * width * cols * 12 + 16 * rows * rows * HD * 4
     return pl.pallas_call(
         forward_kernel,
-        in_specs=[sm, any_, any_, any_, any_, vm, vm],
-        out_specs=[any_, any_, any_, vm, any_, any_, any_, any_, any_, vm, vm, any_, vm],
+        in_specs=[vm, vm] + [any_] * 8,
+        out_specs=[
+            any_, any_, any_, vm, any_, any_, any_, any_, any_, vm, vm, vm, vm, vm, vm
+        ],
         out_shape=[
             shape((3, 4, width, cols), bf16),
             shape((rows, width), bf16),
@@ -640,13 +698,16 @@
             shape((own, width), f32),
             shape((own, 1), f32),
             shape((own, width), f32),
-            shape((4, part, width), bf16),
+            shape((own, width), bf16),
             shape((8, width), f32),
+            shape((8, width), f32),
+            shape((8, 128), f32),
         ],
         scratch_shapes=[
             pltpu.VMEM((3, 4, width, cols), bf16),
+            pltpu.VMEM((own, width), bf16),
             pltpu.VMEM((rows, width), bf16),
-            pltpu.VMEM((4, 8, bias.shape[1]), f32),
+            pltpu.VMEM((4, 8, 4 * head_cols + cols), f32),
             pltpu.VMEM((4, rows, 3 * head_cols), bf16),
             pltpu.VMEM((4, rows, head_cols), bf16),
             pltpu.VMEM((rows, width), bf16),
@@ -655,15 +716,21 @@
             pltpu.VMEM((own, width), f32),
             pltpu.VMEM((own, width), f32),
             pltpu.VMEM((own, width), f32),
-            pltpu.VMEM((own, width), f32),
-            pltpu.VMEM((own, width), f32),
+            pltpu.VMEM((own, width), bf16),
             pltpu.VMEM((own, width), f32),
             pltpu.VMEM((own, width), bf16),
             pltpu.VMEM((own, width), bf16),
-            dma((3, 3)), dma((3, 3)), dma((3, 4)), dma((3, 4)), dma((3, 4)), dma((3, 4)),
-            dma((3, 4)), dma((3, 4)), dma((3,)), dma((3,)), dma((3,)), dma((4,)), dma((4,)),
-            dma((4,)), dma((4,)), dma((4,)), dma((4,)), dma((4,)), dma((4,)),
-            dma((4,)), dma((4,)), dma((32,)),
+            pltpu.VMEM((own, width), bf16),
+            pltpu.VMEM(w_out.shape, bf16),
+            pltpu.VMEM(w_back.shape, bf16),
+            pltpu.VMEM((w_out.shape[1], head_cols), bf16),
+            pltpu.VMEM((w_back.shape[1], cols), bf16),
+            pltpu.VMEM((2, 8, 128), f32),
+            dma((3, 3)), dma((3, 3)), dma((3, 3)), dma((3, 3)),
+            dma((3, 4)), dma((3, 4)), dma((3, 4)), dma((3, 4)),
+            dma((3, 4, 2)), dma((3, 4, 2)), dma((6,)), dma((6,)), dma((6,)), dma((4,)), dma((4,)),
+            dma((4,)), dma((4,)), dma((4,)), dma((4,)),
+            dma((5,)), dma((5,)), dma((32,)),
         ],
         compiler_params=pltpu.CompilerParams(
             collective_id=0, has_side_effects=True, vmem_limit_bytes=60 << 20
@@ -672,16 +739,17 @@
             flops=flops, bytes_accessed=60 << 20, transcendentals=8 * rows * rows
         ),
         name="forward_layer",
-    )(length, xp, cp, keep, give, bias, vec)
+    )(lens, row, inputs, cotangent, w_query, w_key, w_value, w_out, w_in, w_back)
 
 
 def backward_kernel(
     w_ref, xf_ref, qkv_ref, lse_ref, ctx_ref, ff_ref, hid_ref, dg_ref, n1_ref, inv1_ref, gm_ref,
-    vec_ref, sums_ref, length_ref,
-    gi_ref, mine_ref, got_ref, total_ref,
-    w, grad_c, pad, pre, gmf, gaf, act, turned, gm, n1, own_part, other, got, gi_own,
-    d_got, rx, ry, rz, home, dk_acc, dv_acc, vz, zg, xg, yg, cg, tot,
+    vec_ref, sums_ref, length_ref, lo_own,
+    lo_ref, gi_ref, gq_ref, gk_ref, gv_ref, go_ref, gw_ref, gb_ref, total_ref,
+    w, grad_c, pad, pre, gmf, gaf, act, turned, gm, n1, own_part, other, got,
+    d_got, rx, ry, rz, home, dk_acc, dv_acc, vz, zg, xg, yg, cg, tot, go_turned, gb_turned,
     d_s, d_r, x_s, x_r, y_s, y_r, z_s, z_r, h_s, h_r, h_l, e_s, e_r, g_s, g_r, v_s, v_r, l_s,
+    lo_s, lo_r,
 ):
     plane = lax.axis_index("plane")
     core = lax.axis_index("core")
@@ -697,6 +765,7 @@
     head_cols = 2 * HD
     tile = 256
     small = 32
+    gi_own = gmf
 
     def remote(source, target, send, recv, to):
         return pltpu.make_async_remote_copy(
@@ -724,19 +793,35 @@
             block(b, j, 0), rz.at[b, j - 1], z_s.at[b, j - 1], z_r.at[b, j - 1], z_back
         )
 
-    def home_copy(b):
-        at = pl.ds((1 - core) * (piece // 2), piece // 2)
-        return remote(home.at[b, at], got_ref.at[b], h_s.at[b], h_r.at[b], partner)
-
-    def home_keep(b):
-        at = pl.ds(core * (piece // 2), piece // 2)
-        return pltpu.make_async_copy(home.at[b, at], mine_ref.at[b], h_l.at[b])
+    half_piece = piece // 2
+    cols = w.shape[3]
+    mine_at = pl.ds(core * half_piece, half_piece)
+    theirs_at = pl.ds((1 - core) * half_piece, half_piece)
+
+    def home_parts(n, at):
+        heads = pl.ds(pl.multiple_of(core * head_cols, head_cols), head_cols)
+        wide = pl.ds(pl.multiple_of(core * cols, cols), cols)
+        if n < 3:
+            return home.at[0, at, n * head_cols : (n + 1) * head_cols], (gq_ref, gk_ref, gv_ref)[n].at[:, heads]
+        if n == 3:
+            return go_turned.at[:, at], go_ref.at[heads]
+        if n == 4:
+            return home.at[1, at], gw_ref.at[:, wide]
+        return gb_turned.at[:, at], gb_ref.at[wide]
+
+    def home_copy(n):
+        source, target = home_parts(n, theirs_at)
+        return remote(source, target, h_s.at[n], h_r.at[n], partner)
+
+    def home_keep(n):
+        source, target = home_parts(n, mine_at)
+        return pltpu.make_async_copy(source, target, h_l.at[n])
 
     def send_first(b, j):
         d_copy(b, j).start()
+
+    def send_second(b, j):
         (x_copy if j < 2 else y_copy)(b, j).start()
-
-    def send_second(b, j):
         d_copy(b, j).wait_recv()
         here = block(b, j, 2 if j < 2 else 1)
         here[...] = (here[...].astype(f32) + d_got[b, j].astype(f32)).astype(bf16)
@@ -754,27 +839,52 @@
             z_copy(b, j).start()
         else:
             home[b] = total
-            home_copy(b).start()
-            home_keep(b).start()
+            if b == 0:
+                go_turned[...] = total[:, 3 * head_cols : 4 * head_cols].T
+            if b == 2:
+                gb_turned[...] = total.T
+            for n in ((0, 1, 2, 3), (4,), (5,))[b]:
+                home_copy(n).start()
+                home_keep(n).start()
 
     def exchange(source, target, n):
         return remote(source, target, e_s.at[n], e_r.at[n], partner)
 
-    def back(s):
+    def back_parts(source, target, s):
+        at = pl.ds(core * part, part)
+        return source.at[s * part : (s + 1) * part], target.at[place % 2, at]
+
+    def back(source, target, send, recv, s):
+        here, there = back_parts(source, target, s)
         to = {"core": place // 2, "tensor": s}
-        slot = 2 * (place % 2) + core
-        return remote(
-            gi_own.at[s * part : (s + 1) * part], gi_ref.at[slot], g_s.at[s], g_r.at[slot], to
-        )
-
-    def back_local(s):
-        slot = 2 * (place % 2) + core
-        return pltpu.make_async_copy(
-            gi_own.at[s * part : (s + 1) * part], gi_ref.at[slot], g_r.at[slot]
-        )
+        return remote(here, there, send.at[s], recv.at[2 * (place % 2) + core], to)
+
+    def back_local(source, target, recv, s):
+        here, there = back_parts(source, target, s)
+        return pltpu.make_async_copy(here, there, recv.at[2 * (place % 2) + core])
 
     def is_home(s):
         return jnp.logical_and(core == place // 2, place == s)
+
+    def back_start(source, target, send, recv):
+        for s in range(4):
+            @pl.when(is_home(s))
+            def _():
+                back_local(source, target, recv, s).start()
+
+            @pl.when(jnp.logical_not(is_home(s)))
+            def _():
+                back(source, target, send, recv, s).start()
+
+    def back_end(source, target, send, recv):
+        for s in range(4):
+            @pl.when(jnp.logical_not(is_home(s)))
+            def _():
+                back(source, target, send, recv, s).wait_send()
+        for s in range(4):
+            pltpu.make_async_copy(
+                source.at[0:part], target.at[s // 2, pl.ds((s % 2) * part, part)], recv.at[s]
+            ).wait()
 
     def v_copy(j):
         to = {"tensor": (place + 4 - j) % 4}
@@ -821,6 +931,7 @@
     pl.semaphore_wait(barrier, len(friends))
     share_gm = exchange(gmf.at[0:own], gmf.at[own : 2 * own], 0)
     share_gm.start()
+    back_start(lo_own, lo_ref, lo_s, lo_r)
     vz[...] = jnp.zeros_like(vz)
 
     def turn(source, first, last):
@@ -847,7 +958,7 @@
     turn(gmf, 0, own // tile)
     share_gm.wait_recv()
     turn(gmf, own // tile, rows // tile)
-    for j in (3, 2, 1, 0):
+    for j in (3, 1, 2, 0):
         coming[("hid", j)].wait()
         weight_grad(2, j, lambda: pad[j], every)
         send_first(2, j)
@@ -871,9 +982,8 @@
     slope_rows(1)
     send_second(2, 3)
     slope_rows(2)
+    slope_rows(3)
     send_second(2, 2)
-    slope_rows(3)
-    send_second(2, 1)
     for j in range(4):
         fetch(("ctx", j), ctx_ref.at[j], pad.at[j, :, pl.ds(3 * head_cols, head_cols)])
     coming["w1"].wait()
@@ -893,6 +1003,7 @@
     first_rows(own, other)
     share_first = exchange(other, got, 1)
     share_first.start()
+    send_second(2, 1)
     first_rows(0, own_part)
     send_second(2, 0)
     coming["n1"].wait()
@@ -925,11 +1036,11 @@
     fetch("xf", xf_ref, act)
     weight_grad(1, 3, lambda: pre[3], every)
     send_first(1, 3)
+    weight_grad(1, 1, lambda: pre[1], every)
+    send_first(1, 1)
+    send_third(2, 3)
     weight_grad(1, 2, lambda: pre[2], every)
     send_first(1, 2)
-    send_third(2, 3)
-    weight_grad(1, 1, lambda: pre[1], every)
-    send_first(1, 1)
     weight_grad(1, 0, lambda: pre[0], every)
     send_first(1, 0)
     for j in range(4):
@@ -958,13 +1069,13 @@
     coming["xf"].wait()
     turn(act, 0, rows // tile)
     send_second(1, 3)
-    send_second(1, 2)
 
     index = lax.broadcasted_iota(jnp.int32, (rows, 1), 0)
     half = jnp.where(index < own, core, 1 - core)
     inside = index % own
     position = (inside // part) * (2 * part) + half * part + inside % part
-    key_bias = jnp.where(position < length_ref[0], 0.0, NEGATIVE).astype(f32)
+    length = length_ref[pl.ds(place % 2, 1), 0:1]
+    key_bias = jnp.where(position.astype(f32) < length, 0.0, NEGATIVE).astype(f32)
     lane = lax.broadcasted_iota(jnp.int32, (1, head_cols), 1)
     front = slice(0, 3 * head_cols)
 
@@ -1003,20 +1114,21 @@
         pad[j, :, 2 * head_cols : 3 * head_cols] = low
         vz[j, 8:9, head_cols : 2 * head_cols] = jnp.sum(low.astype(f32), axis=0, keepdims=True)
 
-    for j in (3, 2, 1, 0):
+    for n, j in enumerate((3, 1, 2, 0)):
         coming[("qkv", j)].wait()
         attend_back(j)
-        if j == 3:
+        if n == 0:
+            send_second(1, 2)
             send_second(1, 1)
             send_second(1, 0)
+        else:
+            send_third(1, 4 - n)
         weight_grad(0, j, lambda: pad[j, :, front], front)
         send_first(0, j)
-        if j == 1:
-            send_third(1, 3)
     for j in range(1, 4):
         v_copy(j).start()
     zg[place] = vz[0]
-    send_third(1, 2)
+    send_second(0, 3)
 
     def input_rows(start, target):
         def body(i, _):
@@ -1030,32 +1142,29 @@
 
         lax.fori_loop(0, own // tile, body, 0)
 
+    share_gm.wait_send()
     share_first.wait_send()
     input_rows(own, other)
     share_in = exchange(other, got, 3)
     share_in.start()
-    send_third(1, 1)
-    send_second(0, 3)
     send_second(0, 2)
     input_rows(0, own_part)
     send_third(1, 0)
+    send_second(0, 1)
     share_in.wait_recv()
 
     def input_body(i, _):
         at = pl.ds(pl.multiple_of(i * small, small), small)
         value = gm[at, :] + (own_part[at, :] + got[at, :].astype(f32))
-        gi_own[at, :] = value.astype(bf16)
+        low = value.astype(bf16)
+        for k in range(4):
+            number = (plane, plane + 1 - 2 * (plane % 2), (plane + 2) % 4, 3 - plane)[k]
+            to = pl.ds(pl.multiple_of(number * piece, piece), piece)
+            gi_own[at, to] = low[:, k * piece : (k + 1) * piece]
         return 0
 
     lax.fori_loop(0, own // small, input_body, 0)
-    for s in range(4):
-        @pl.when(is_home(s))
-        def _():
-            back_local(s).start()
-
-        @pl.when(jnp.logical_not(is_home(s)))
-        def _():
-            back(s).start()
+    back_start(gi_own, gi_ref, g_s, g_r)
 
     def fold(n, m, arrived, flip):
         for k in range(4):
@@ -1069,7 +1178,6 @@
     tot[0] = ((zg[0] + zg[1]) + zg[2]) + zg[3]
     v_x = remote(tot.at[0], xg, e_s.at[4], e_r.at[4], x_side)
     v_x.start()
-    send_second(0, 1)
     send_second(0, 0)
     v_x.wait_recv()
     fold(1, 0, xg, 1)
@@ -1084,8 +1192,15 @@
     send_third(0, 1)
     send_third(0, 0)
     v_c.wait_recv()
-    total_ref[0] = tot[2]
-    total_ref[1] = cg[...]
+    for k in range(4):
+        number = (plane, plane + 1 - 2 * (plane % 2), (plane + 2) % 4, 3 - plane)[k]
+        to = pl.ds(pl.multiple_of(number * piece, piece), piece)
+        here = slice(k * piece, (k + 1) * piece)
+        total_ref[0:8, to] = tot[2, 0:8, here] + cg[0:8, here]
+    own_row = tot[2, 8:9, :]
+    their_row = cg[8:9, :]
+    total_ref[8:9, :] = jnp.where(core == 0, own_row, their_row)
+    total_ref[9:10, :] = jnp.where(core == 0, their_row, own_row)
 
     for b in range(3):
         for j in range(4):
@@ -1094,22 +1209,19 @@
             y_copy(b, j).wait_send()
             if j > 0:
                 z_copy(b, j).wait_send()
-        home_keep(b).wait()
-        home_copy(b).wait_send()
-        home_copy(b).wait_recv()
+    for n in range(6):
+        home_keep(n).wait()
+        home_copy(n).wait_send()
+        home_copy(n).wait_recv()
     for j in range(1, 4):
         v_copy(j).wait_send()
-    for copy in (share_gm, share_att, share_in, v_x, v_y, v_c):
+    for copy in (share_att, share_in, v_x, v_y, v_c):
         copy.wait_send()
-    for s in range(4):
-        @pl.when(jnp.logical_not(is_home(s)))
-        def _():
-            back(s).wait_send()
-    for s in range(4):
-        pltpu.make_async_copy(gi_own.at[0:part], gi_ref.at[s], g_r.at[s]).wait()
-
-
-def backward(w_all, xf, qkv, lse, ctx, ff, hid, dg, n1, inv1, gm, vec, sums, length):
+    back_end(lo_own, lo_ref, lo_s, lo_r)
+    back_end(gi_own, gi_ref, g_s, g_r)
+
+
+def backward(w_all, xf, qkv, lse, ctx, ff, hid, dg, n1, inv1, gm, vec, sums, length, lo):
     rows, width = xf.shape
     own = rows // 2
     part = own // 4
@@ -1118,19 +1230,25 @@
     head_cols = 2 * HD
     any_ = pl.BlockSpec(memory_space=pltpu.HBM)
     vm = pl.BlockSpec(memory_space=pltpu.VMEM)
-    sm = pl.BlockSpec(memory_space=pltpu.SMEM)
     shape = jax.ShapeDtypeStruct
     dma = pltpu.SemaphoreType.DMA
     flops = 2 * rows * width * cols * 24 + 40 * rows * rows * HD * 4
     return pl.pallas_call(
         backward_kernel,
-        in_specs=[any_, any_, any_, vm, any_, any_, any_, any_, any_, vm, any_, vm, vm, sm],
-        out_specs=[any_, any_, any_, vm],
+        in_specs=[
+            any_, any_, any_, vm, any_, any_, any_, any_, any_, vm, any_, vm, vm, vm, any_
+        ],
+        out_specs=[any_] * 8 + [vm],
         out_shape=[
-            shape((4, part, width), bf16),
-            shape((3, piece // 2, cols), f32),
-            shape((3, piece // 2, cols), f32),
-            shape((2, 16, width), f32),
+            shape((2, 2 * part, width), bf16),
+            shape((2, 2 * part, width), bf16),
+            shape((piece // 2, 2 * head_cols), f32),
+            shape((piece // 2, 2 * head_cols), f32),
+            shape((piece // 2, 2 * head_cols), f32),
+            shape((2 * head_cols, piece // 2), f32),
+            shape((piece // 2, 2 * cols), f32),
+            shape((2 * cols, piece // 2), f32),
+            shape((16, width), f32),
         ],
         scratch_shapes=[
             pltpu.VMEM((3, 4, width, cols), bf16),
@@ -1146,7 +1264,6 @@
             pltpu.VMEM((own, width), f32),
             pltpu.VMEM((own, width), bf16),
             pltpu.VMEM((own, width), bf16),
-            pltpu.VMEM((own, width), bf16),
             pltpu.VMEM((3, 4, piece, cols), bf16),
             pltpu.VMEM((3, 4, piece, cols), bf16),
             pltpu.VMEM((3, 4, piece, cols), bf16),
@@ -1160,9 +1277,12 @@
             pltpu.VMEM((16, width), f32),
             pltpu.VMEM((16, width), f32),
             pltpu.VMEM((3, 16, width), f32),
+            pltpu.VMEM((head_cols, piece), f32),
+            pltpu.VMEM((cols, piece), f32),
             dma((3, 4)), dma((3, 4)), dma((3, 4)), dma((3, 4)), dma((3, 4)), dma((3, 4)),
-            dma((3, 3)), dma((3, 3)), dma((3,)), dma((3,)), dma((3,)), dma((8,)), dma((8,)),
+            dma((3, 3)), dma((3, 3)), dma((6,)), dma((6,)), dma((6,)), dma((8,)), dma((8,)),
             dma((4,)), dma((4,)), dma((3,)), dma((4,)), dma((32,)),
+            dma((4,)), dma((4,)),
         ],
         compiler_params=pltpu.CompilerParams(
             collective_id=1, has_side_effects=True, vmem_limit_bytes=60 << 20
@@ -1171,7 +1291,7 @@
             flops=flops, bytes_accessed=60 << 20, transcendentals=8 * rows * rows
         ),
         name="backward_layer",
-    )(w_all, xf, qkv, lse, ctx, ff, hid, dg, n1, inv1, gm, vec, sums, length)
+    )(w_all, xf, qkv, lse, ctx, ff, hid, dg, n1, inv1, gm, vec, sums, length, lo)
 
 
 def swap_cores(value):
@@ -1212,6 +1332,50 @@
     ff_cols = w_in.shape[1] // 2
     scale = HD ** (-0.5)
     quad = planes == 4
+    if quad:
+        row = jnp.stack(
+            [
+                value.astype(f32)
+                for value in (
+                    b_out, gain_one, shift_one, b_back, gain_two, shift_two, b_in,
+                    jnp.concatenate([b_query, b_value, jnp.zeros((width // 2,), bf16)]),
+                )
+            ]
+        )
+        lens = jnp.broadcast_to(
+            jnp.concatenate([lengths.astype(f32)] * (8 // seqs))[:, None], (8, 128)
+        )
+        (w_all, x_full, qkv4, lse8, ctx4, first_full, hid4, dg4, normed_one, inverse_one,
+         grad_mixed, lo, second_sums, vec, length_rows) = forward(
+            lens, row, inputs, cotangent, w_query, w_key, w_value, w_out, w_in, w_back
+        )
+        (layer_out, gi, grad_w_query, grad_w_key, grad_w_value, grad_w_out, grad_w_in,
+         grad_w_back, totals) = backward(
+            w_all, x_full, qkv4, lse8, ctx4, first_full, hid4, dg4, normed_one, inverse_one,
+            grad_mixed, vec, second_sums, length_rows, lo,
+        )
+        n_bias = 2 * head_cols + ff_cols
+        biases_out = totals[8:10, :n_bias]
+        return (
+            layer_out,
+            gi.astype(f32),
+            grad_w_query,
+            grad_w_key,
+            grad_w_value,
+            biases_out[:, :head_cols].reshape(-1),
+            biases_out[:, head_cols : 2 * head_cols].reshape(-1),
+            grad_w_out,
+            totals[0],
+            totals[1],
+            totals[2],
+            grad_w_in,
+            biases_out[:, 2 * head_cols :].reshape(-1),
+            grad_w_back,
+            totals[3],
+            totals[4],
+            totals[5],
+        )
+
     ring = [(i, (i + 1) % n_t) for i in range(n_t)]
     x_pairs = [(i, i ^ 1) for i in range(planes)]
     y_pairs = [(i, i ^ 2) for i in range(planes)]
@@ -1320,168 +1484,140 @@
             - normed * jnp.mean(e * normed, axis=-1, keepdims=True)
         ) * inverse
 
-    if quad:
-        def blocks_of(value):
-            return reorder(value, 2).reshape(4, half_slots, width)
-
-        pack = lambda value: jnp.stack(
-            [value[:, : cuts[0]], value[:, cuts[0] : cuts[1]], value[:, cuts[1] :]]
-        )
-        vec = jnp.stack(
-            [out_bias, gain_first, shift_first, back_bias, gain_second, shift_second,
-             out_bias, out_bias]
-        )
-        (w_all, x_full, qkv4, lse8, ctx4, first_full, hid4, dg4, normed_one, inverse_one,
-         grad_mixed, lo_blocks, second_sums) = forward(
-            length.reshape(1), blocks_of(inputs), blocks_of(cotangent), pack(keep), pack(give),
-            jnp.broadcast_to(bias_row.astype(f32), (8, bias_row.shape[1])), vec,
-        )
-        layer_out = reorder(lo_blocks.reshape(seqs, slots_here, width), 2)
-        gi_blocks, mine, got, totals = backward(
-            w_all, x_full, qkv4, lse8, ctx4, first_full, hid4, dg4, normed_one, inverse_one,
-            grad_mixed, vec, second_sums, length.reshape(1),
-        )
-        grad_inputs = reorder(gi_blocks.reshape(seqs, slots_here, width), 2).astype(f32)
-        mine = jnp.concatenate([mine[0], mine[1], mine[2]], axis=1)
-        got = jnp.concatenate([got[0], got[1], got[2]], axis=1)
-        norms = reorder(totals[0, :6] + totals[1, :6], 1)
-        n_bias = 2 * head_cols + ff_cols
-        biases_out = by_core(totals[0, 8:9, :n_bias], totals[1, 8:9, :n_bias])
-    else:
-        packed = by_core(keep, swap_cores(give))
-        bundle_a = packed[:, : cuts[0]]
-        bundle_b = packed[:, cuts[0] : cuts[1]]
-        bundle_c = packed[:, cuts[1] :]
-        def gather_z(own_piece):
-            got = [own_piece]
-            for _ in range(n_t - 1):
-                got.append(lax.ppermute(got[-1], "tensor", ring))
-            return jnp.stack(got)
-
-        def gather_planes(mine):
-            if not quad:
-                return lax.all_gather(mine, "plane", axis=1, tiled=True)
+    packed = by_core(keep, swap_cores(give))
+    bundle_a = packed[:, : cuts[0]]
+    bundle_b = packed[:, cuts[0] : cuts[1]]
+    bundle_c = packed[:, cuts[1] :]
+    def gather_z(own_piece):
+        got = [own_piece]
+        for _ in range(n_t - 1):
+            got.append(lax.ppermute(got[-1], "tensor", ring))
+        return jnp.stack(got)
+
+    def gather_planes(mine):
+        if not quad:
+            return lax.all_gather(mine, "plane", axis=1, tiled=True)
+        half = n_t // 2
+        from_x = lax.ppermute(mine, "plane", x_pairs)
+        from_y = lax.ppermute(mine, "plane", y_pairs)
+        low = lax.ppermute(from_y[:half], "plane", x_pairs)
+        high = lax.ppermute(from_x[half:], "plane", y_pairs)
+        return jnp.concatenate([mine, from_x, from_y, jnp.concatenate([low, high])], axis=1)
+
+    biases = gather_z(bias_row)[:, 0].astype(f32)
+    z_a = gather_z(bundle_a)
+    full_a = gather_planes(z_a)
+    w_qkv = flat(full_a[:, :, : 3 * head_cols])
+    w_o = flat(full_a[:, :, 3 * head_cols :])
+    w_1 = flat(gather_planes(gather_z(bundle_b)))
+    w_2 = flat(gather_planes(gather_z(bundle_c)))
+
+    zeros_k = jnp.zeros((n_t, head_cols), f32)
+    qkv_bias = jnp.concatenate(
+        [biases[:, :head_cols], zeros_k, biases[:, head_cols : 2 * head_cols]], axis=1
+    ).reshape(1, -1)
+    in_bias = biases[:, 2 * head_cols :].reshape(1, -1)
+
+    own_x = to_chip(inputs)
+    x_full = both_rows(own_x)
+    qkv = ((nn(x_full, w_qkv) + qkv_bias) * qkv_scale).astype(bf16)
+    context, lse = attend_fwd(qkv, key_bias)
+    attended = own_sum(nt(context, w_o))
+    normed_one, inverse_one = normalize(own_x.astype(f32) + attended + out_bias)
+    first_norm = normed_one * gain_first + shift_first
+    first_full = both_rows(first_norm.astype(bf16))
+    pre_act = nn(first_full, w_1) + in_bias
+    activated, slope = gelu_and_slope(pre_act)
+    hidden = activated.astype(bf16)
+    mixed = own_sum(nt(hidden, w_2))
+    normed_two, inverse_two = normalize(first_norm + mixed + back_bias)
+    second = normed_two * gain_second + shift_second
+    layer_out = from_chip(jnp.where(own_valid, second, 0.0).astype(bf16))
+
+    grad_second = jnp.where(own_valid, to_chip(cotangent).astype(f32), 0.0)
+    grad_mixed = normalize_back(grad_second, gain_second, normed_two, inverse_two)
+
+    grad_mixed_full = both_rows(grad_mixed.astype(bf16))
+    grad_w2 = tn(grad_mixed_full, hidden)
+    grad_pre_low = (nn(grad_mixed_full, w_2) * slope.astype(f32)).astype(bf16)
+    grad_w1 = tn(first_full, grad_pre_low)
+    grad_first = grad_mixed + own_sum(nt(grad_pre_low, w_1))
+    grad_att = normalize_back(grad_first, gain_first, normed_one, inverse_one)
+    grad_att_full = both_rows(grad_att.astype(bf16))
+    grad_context = nn(grad_att_full, w_o).astype(bf16)
+    grad_wo = tn(grad_att_full, context)
+    grad_qkv = attend_bwd(qkv, grad_context, lse, key_bias)
+    grad_qkv = grad_qkv * qkv_scale.astype(bf16)
+    grad_wqkv = tn(x_full, grad_qkv)
+    grad_rows = grad_att + own_sum(nt(grad_qkv, w_qkv))
+    grad_inputs = from_chip(grad_rows.astype(bf16)).astype(f32)
+
+    def scatter(grad):
+        cols = grad.shape[1] // n_t
+        if quad:
+            rows = width // 4
+            blocks = grad.reshape(4, rows, n_t, cols).transpose(0, 2, 1, 3)
             half = n_t // 2
-            from_x = lax.ppermute(mine, "plane", x_pairs)
-            from_y = lax.ppermute(mine, "plane", y_pairs)
-            low = lax.ppermute(from_y[:half], "plane", x_pairs)
-            high = lax.ppermute(from_x[half:], "plane", y_pairs)
-            return jnp.concatenate([mine, from_x, from_y, jnp.concatenate([low, high])], axis=1)
-
-        biases = gather_z(bias_row)[:, 0].astype(f32)
-        z_a = gather_z(bundle_a)
-        full_a = gather_planes(z_a)
-        w_qkv = flat(full_a[:, :, : 3 * head_cols])
-        w_o = flat(full_a[:, :, 3 * head_cols :])
-        w_1 = flat(gather_planes(gather_z(bundle_b)))
-        w_2 = flat(gather_planes(gather_z(bundle_c)))
-
-        zeros_k = jnp.zeros((n_t, head_cols), f32)
-        qkv_bias = jnp.concatenate(
-            [biases[:, :head_cols], zeros_k, biases[:, head_cols : 2 * head_cols]], axis=1
-        ).reshape(1, -1)
-        in_bias = biases[:, 2 * head_cols :].reshape(1, -1)
-
-        own_x = to_chip(inputs)
-        x_full = both_rows(own_x)
-        qkv = ((nn(x_full, w_qkv) + qkv_bias) * qkv_scale).astype(bf16)
-        context, lse = attend_fwd(qkv, key_bias)
-        attended = own_sum(nt(context, w_o))
-        normed_one, inverse_one = normalize(own_x.astype(f32) + attended + out_bias)
-        first_norm = normed_one * gain_first + shift_first
-        first_full = both_rows(first_norm.astype(bf16))
-        pre_act = nn(first_full, w_1) + in_bias
-        activated, slope = gelu_and_slope(pre_act)
-        hidden = activated.astype(bf16)
-        mixed = own_sum(nt(hidden, w_2))
-        normed_two, inverse_two = normalize(first_norm + mixed + back_bias)
-        second = normed_two * gain_second + shift_second
-        layer_out = from_chip(jnp.where(own_valid, second, 0.0).astype(bf16))
-
-        grad_second = jnp.where(own_valid, to_chip(cotangent).astype(f32), 0.0)
-        grad_mixed = normalize_back(grad_second, gain_second, normed_two, inverse_two)
-
-        grad_mixed_full = both_rows(grad_mixed.astype(bf16))
-        grad_w2 = tn(grad_mixed_full, hidden)
-        grad_pre_low = (nn(grad_mixed_full, w_2) * slope.astype(f32)).astype(bf16)
-        grad_w1 = tn(first_full, grad_pre_low)
-        grad_first = grad_mixed + own_sum(nt(grad_pre_low, w_1))
-        grad_att = normalize_back(grad_first, gain_first, normed_one, inverse_one)
-        grad_att_full = both_rows(grad_att.astype(bf16))
-        grad_context = nn(grad_att_full, w_o).astype(bf16)
-        grad_wo = tn(grad_att_full, context)
-        grad_qkv = attend_bwd(qkv, grad_context, lse, key_bias)
-        grad_qkv = grad_qkv * qkv_scale.astype(bf16)
-        grad_wqkv = tn(x_full, grad_qkv)
-        grad_rows = grad_att + own_sum(nt(grad_qkv, w_qkv))
-        grad_inputs = from_chip(grad_rows.astype(bf16)).astype(f32)
-
-        def scatter(grad):
-            cols = grad.shape[1] // n_t
-            if quad:
-                rows = width // 4
-                blocks = grad.reshape(4, rows, n_t, cols).transpose(0, 2, 1, 3)
-                half = n_t // 2
-                low = lax.ppermute(blocks[3, :half].astype(bf16), "plane", x_pairs)
-                high = lax.ppermute(blocks[3, half:].astype(bf16), "plane", y_pairs)
-                for_y = jnp.concatenate([blocks[2, :half] + low.astype(f32), blocks[2, half:]])
-                for_x = jnp.concatenate([blocks[1, :half], blocks[1, half:] + high.astype(f32)])
-                from_x = lax.ppermute(for_x.astype(bf16), "plane", x_pairs)
-                from_y = lax.ppermute(for_y.astype(bf16), "plane", y_pairs)
-                mine = blocks[0] + from_x.astype(f32) + from_y.astype(f32)
-            else:
-                blocks = grad.reshape(width, n_t, cols).transpose(1, 0, 2)
-                mine = lax.psum_scatter(
-                    blocks.astype(bf16), "plane", scatter_dimension=1, tiled=True
-                ).astype(f32)
-            back = [(b, a) for a, b in ring]
-            total = mine[n_t - 1]
-            for j in range(n_t - 2, -1, -1):
-                total = mine[j] + lax.ppermute(total.astype(bf16), "tensor", back).astype(f32)
-            return total
-
-        home_c = scatter(grad_w2)
-        home_b = scatter(grad_w1)
-        grad_a = jnp.concatenate(
-            [
-                grad_wqkv.reshape(width, n_t, 3 * head_cols),
-                grad_wo.reshape(width, n_t, head_cols),
-            ],
-            axis=2,
-        ).reshape(width, -1)
-        home_a = scatter(grad_a)
-        home = jnp.concatenate([home_a, home_b, home_c], axis=1)
-        home = home.reshape(2, -1, home.shape[1])
-        mine = lax.dynamic_index_in_dim(home, core, 0, keepdims=False)
-        other = lax.dynamic_index_in_dim(home, 1 - core, 0, keepdims=False)
-        got = swap_cores(other)
-
-        def row_sum(value):
-            return reorder(jnp.sum(value, axis=0), 0)
-
-        second_rows = [row_sum(grad_mixed), row_sum(grad_second * normed_two), row_sum(grad_second)]
-        norm_sums = jnp.concatenate(
-            [
-                row_sum(grad_att),
-                row_sum(grad_first * normed_one),
-                row_sum(grad_first),
-                *second_rows,
-            ]
-        )
-        qkv_sum = jnp.sum(grad_qkv.astype(f32), axis=0).reshape(n_t, 3 * head_cols)
-        pre_sum = jnp.sum(grad_pre_low.astype(f32), axis=0).reshape(n_t, ff_cols)
-        bias_sum = jnp.concatenate([qkv_sum[:, :head_cols], qkv_sum[:, 2 * head_cols :], pre_sum], axis=1)
-        at_home = lax.rem(place - jnp.arange(n_t) + n_t, n_t)
-        spread = (at_home[:, None] == jnp.arange(n_t)[None]).astype(f32)
-        by_place = jnp.sum(spread[:, :, None] * bias_sum[:, None, :], axis=0)
-        both = jnp.where(
-            (jnp.arange(2) == core)[None, :, None], by_place[:, None, :], 0.0
-        )
-        sums = lax.psum(jnp.concatenate([norm_sums, both.reshape(-1)]), ("plane", "core", "tensor"))
-        norms = sums[: 6 * width].reshape(6, width)
-        biases_out = lax.dynamic_index_in_dim(
-            sums[6 * width :].reshape(n_t, 2, -1), place, 0, keepdims=False
-        )
+            low = lax.ppermute(blocks[3, :half].astype(bf16), "plane", x_pairs)
+            high = lax.ppermute(blocks[3, half:].astype(bf16), "plane", y_pairs)
+            for_y = jnp.concatenate([blocks[2, :half] + low.astype(f32), blocks[2, half:]])
+            for_x = jnp.concatenate([blocks[1, :half], blocks[1, half:] + high.astype(f32)])
+            from_x = lax.ppermute(for_x.astype(bf16), "plane", x_pairs)
+            from_y = lax.ppermute(for_y.astype(bf16), "plane", y_pairs)
+            mine = blocks[0] + from_x.astype(f32) + from_y.astype(f32)
+        else:
+            blocks = grad.reshape(width, n_t, cols).transpose(1, 0, 2)
+            mine = lax.psum_scatter(
+                blocks.astype(bf16), "plane", scatter_dimension=1, tiled=True
+            ).astype(f32)
+        back = [(b, a) for a, b in ring]
+        total = mine[n_t - 1]
+        for j in range(n_t - 2, -1, -1):
+            total = mine[j] + lax.ppermute(total.astype(bf16), "tensor", back).astype(f32)
+        return total
+
+    home_c = scatter(grad_w2)
+    home_b = scatter(grad_w1)
+    grad_a = jnp.concatenate(
+        [
+            grad_wqkv.reshape(width, n_t, 3 * head_cols),
+            grad_wo.reshape(width, n_t, head_cols),
+        ],
+        axis=2,
+    ).reshape(width, -1)
+    home_a = scatter(grad_a)
+    home = jnp.concatenate([home_a, home_b, home_c], axis=1)
+    home = home.reshape(2, -1, home.shape[1])
+    mine = lax.dynamic_index_in_dim(home, core, 0, keepdims=False)
+    other = lax.dynamic_index_in_dim(home, 1 - core, 0, keepdims=False)
+    got = swap_cores(other)
+
+    def row_sum(value):
+        return reorder(jnp.sum(value, axis=0), 0)
+
+    second_rows = [row_sum(grad_mixed), row_sum(grad_second * normed_two), row_sum(grad_second)]
+    norm_sums = jnp.concatenate(
+        [
+            row_sum(grad_att),
+            row_sum(grad_first * normed_one),
+            row_sum(grad_first),
+            *second_rows,
+        ]
+    )
+    qkv_sum = jnp.sum(grad_qkv.astype(f32), axis=0).reshape(n_t, 3 * head_cols)
+    pre_sum = jnp.sum(grad_pre_low.astype(f32), axis=0).reshape(n_t, ff_cols)
+    bias_sum = jnp.concatenate([qkv_sum[:, :head_cols], qkv_sum[:, 2 * head_cols :], pre_sum], axis=1)
+    at_home = lax.rem(place - jnp.arange(n_t) + n_t, n_t)
+    spread = (at_home[:, None] == jnp.arange(n_t)[None]).astype(f32)
+    by_place = jnp.sum(spread[:, :, None] * bias_sum[:, None, :], axis=0)
+    both = jnp.where(
+        (jnp.arange(2) == core)[None, :, None], by_place[:, None, :], 0.0
+    )
+    sums = lax.psum(jnp.concatenate([norm_sums, both.reshape(-1)]), ("plane", "core", "tensor"))
+    norms = sums[: 6 * width].reshape(6, width)
+    biases_out = lax.dynamic_index_in_dim(
+        sums[6 * width :].reshape(n_t, 2, -1), place, 0, keepdims=False
+    )
     def columns(start, cols):
         return by_core(mine[:, start : start + cols], got[:, start : start + cols], axis=1)
 

time: 400 us -> 343 us (0.86); the launches traced: 399 us -> 338 us
  Pallas kernels: 356 us -> 316 us
  other arithmetic: 19.3 us -> 4.2 us
  local copies, waits for them, and re-layouts: 22 us -> 16.4 us
    pallas_call x1, Pallas kernels: 176 us -> 151 us  [forward(): pl.pallas_call(forward_kernel, in_specs=[vm, vm] + [any_] * 8, out_specs=...]
    pallas_call x1, Pallas kernels: 180 us -> 165 us  [backward(): pl.pallas_call(backward_kernel, in_specs=[any_, any_, any_, vm, any_, any...]
    dynamic_slice x17 -> x0, local copies, waits for them, and re-layouts: 13.2 us -> none  [the longest x10 6.1 us: reorder(): lax.dynamic_slice_in_dim(value, (plane ^ k) * size, size, axis)]
    concatenate x14 -> x2, other arithmetic: 7.29 us -> 0.09 us  [the longest x1 0.08 us: on_device(): jnp.concatenate([lengths.astype(f32)] * (8 // seqs))[:, None]]
    another operation x5 -> x1, other arithmetic: 4.74 us -> 0.62 us  [on_device(): jnp.stack([value.astype(f32) for value in (b_out, gain_one, shift_one, b_...]
  transfers between devices with their start and end apart: 1 -> 0, of which waited for: 0 -> 0; matrix products, arithmetic and copies ran while one was open for 6% -> 0% of each run, Pallas kernels for 0% -> 0%
where the time goes in v4:
time: 343 us; the launch traced here: 338 us
  Pallas kernels  316 us (92%)
  local copies, waits for them, and re-layouts  16.4 us (5%)
  other arithmetic  4.2 us (1%)
    pallas_call x1, Pallas kernels, backward(): pl.pallas_call(backward_kernel, in_specs=[any_, any_, any_, vm, any_, any...  165 us
    pallas_call x1, Pallas kernels, forward(): pl.pallas_call(forward_kernel, in_specs=[vm, vm] + [any_] * 8, out_specs=...  151 us

profile of v4, /device:TPU:0, one launch (start us, length us, event | category | flops | bytes accessed | tf_op | source)
XLA Modules:
  0.0 337.8 jit_solution(432834726702129731)
XLA Ops:
  0.7 0.7 convert_element_type.21
  1.3 0.1 pad_maximum_fusion
  1.4 0.7 concatenate.18
  2.1 0.7 concatenate.19
  2.7 0.7 broadcast_in_dim.4.lens_ref
  3.4 0.7 stack.34
  4.1 0.7 stack.35
  4.8 0.7 stack.36
  5.5 0.7 stack.40
  6.1 0.7 stack.37
  6.8 0.7 stack.38
  7.5 0.7 stack.39
  8.2 0.1 stack.41
  8.3 0.6 stack.42.row_ref
  8.9 151.1 %forward_layer.1 = (bf16[3,4,1024,512]{3,2,1,0:T(8,128)(2,1)}, bf16[1024,1024]{1,0:T(8,128)(2,1)}, bf16[4,1024,384]{2,1,0:T(8,128)(2,1)}, f32[8,1,1024]{2,1,0:T(...) custom-call(f32[8,128]{1,0:T(8,128)} %broadcast_in_dim.4.lens_ref, ...), custom_call_target="tpu_custom_call" | custom-call | flops 17179869184 | bytes 62914560 | tf_op jit(solution)/shard_map/forward_layer/pallas_call | solution.py:683
  160.0 165.2 %backward_layer.1 = (bf16[2,256,1024]{2,1,0:T(8,128)(2,1)}, bf16[2,256,1024]{2,1,0:T(8,128)(2,1)}, f32[128,256]{1,0:T(8,128)}, f32[128,256]{1,0:T(8,128)}, f32[1...) custom-call(bf16[3,4,1024,512]{3,2,1,0:T(8,128)(2,1)} %get-tuple-elem, ...), custom_call_target="tpu_custom_call" | custom-call | flops 36507222016 | bytes 62914560 | tf_op jit(solution)/shard_map/backward_layer/pallas_call | solution.py:1236
  325.2 0.0 copy-start
  325.2 1.3 slice_bitcast_fusion.1
  326.6 0.7 slice_bitcast_fusion
  327.3 1.7 fusion
  329.0 0.6 copy.35
  329.6 0.0 copy-start.6
  329.6 0.0 copy-start.5
  329.6 2.8 convert_element_type.22
  332.4 0.0 copy-done
  332.4 0.0 copy-start.4
  332.4 0.0 copy-start.3
  332.4 0.0 copy-start.2
  332.4 0.0 copy-start.1
  332.4 1.0 copy.43
  333.4 0.0 copy-done.6
  333.4 0.7 copy.44
  334.0 0.0 copy-done.5
  334.0 0.7 copy.45
  334.7 0.0 copy-done.4
  334.7 0.7 copy.46
  335.4 0.0 copy-done.3
  335.4 0.7 copy.47
  336.0 0.0 copy-done.2
  336.0 0.8 copy.48
  336.8 0.0 copy-done.1
  336.8 0.8 copy.49
  (3 shorter events, 0.0 us)
Async XLA Ops:
  325.2 7.2 %copy-start = (bf16[2,256,1024]{2,1,0:T(8,128)(2,1)S(1)}, bf16[2,256,1024]{2,1,0:T(8,128)(2,1)}, u32[]{:S(2)}) copy-start(bf16[2,256,1024]{2,1,0:T(8,128)(2,1)} %get-tuple-element.90) | copy-start | bytes 3145732
  329.6 3.8 %copy-start.6 = (f32[128,256]{1,0:T(8,128)S(1)}, f32[128,256]{1,0:T(8,128)}, u32[]{:S(2)}) copy-start(f32[128,256]{1,0:T(8,128)} %get-tuple-element.92) | copy-start | bytes 393220
  329.6 4.5 %copy-start.5 = (f32[128,256]{1,0:T(8,128)S(1)}, f32[128,256]{1,0:T(8,128)}, u32[]{:S(2)}) copy-start(f32[128,256]{1,0:T(8,128)} %get-tuple-element.93) | copy-start | bytes 393220
  332.4 2.3 copy-start.4
  332.4 3.0 copy-start.3
  332.4 3.6 %copy-start.2 = (f32[128,1024]{1,0:T(8,128)S(1)}, f32[128,1024]{1,0:T(8,128)}, u32[]{:S(2)}) copy-start(f32[128,1024]{1,0:T(8,128)} %get-tuple-element.101) | copy-start | bytes 1572868
  332.4 4.4 %copy-start.1 = (f32[1024,128]{1,0:T(8,128)S(1)}, f32[1024,128]{1,0:T(8,128)}, u32[]{:S(2)}) copy-start(f32[1024,128]{1,0:T(8,128)} %get-tuple-element.103) | copy-start | bytes 1572868
